TPU v7x, 128 devices: a whole 4x4x4 slice. The times are simulated.
128 devices in a mesh: row: 2 (over x_hi), col: 4 (over x_lo, core), layer: 16 (over z, y).
Axes of the slice: x: 4 (x_hi: 2, x_lo: 2; x = x_hi * 2 + x_lo), y: 4, z: 4, core: 2. Of those that a mesh axis runs over, the one named last changes fastest.
Arguments:
- front: float32 [8192, 8192], P('row', ('col', 'layer')), may hold values from -8 to 256, as said below
Outputs:
- eliminated: float32 [8192, 8192], P('row', ('col', 'layer'))
Inputs may be any that keep to these rules, and one draw needn't show every extreme that they name: `front`: every pivot block met during the elimination has a nonzero diagonal, and the Newton-Schulz iteration started from the inverse of its diagonal converges.
All inputs are finite; a program needn't handle non-finite values.
Results may differ from a plain program's by a relative error of at most 0.0001.
Values sent between devices are 32-bit elements; how exact they have to be, the bound alone decides.
No kernel may reach another device: no remote copies, remote signals or barrier semaphores. Data moves between devices by JAX's collectives and lax.ppermute only.
A program may use at most 64 MiB of HBM per device.

v0:
```python
import jax
import jax.numpy as jnp
from jax import lax
from jax.experimental import pallas as pl
from jax.experimental.pallas import tpu as pltpu
from jax.sharding import PartitionSpec as P


B = 64
ITERS = 2
P_SIZE = 256

AXES = ("row", "x", "core", "z", "y")
SHAPE = (2, 2, 2, 4, 4)
ROWS = 4096
WIDTH = 128
SHARE = 512
DPART = 128


def place(r, x, c, z, y):
    return (((r * 2 + x) * 2 + c) * 4 + z % 4) * 4 + y % 4


def everywhere(zy_pairs, xs=(0, 1)):
    return [
        (place(r, x, c, *a), place(r, x, c, *b)) for r in range(2) for x in xs for c in range(2) for a, b in zy_pairs
    ]


ALL_ZY = [(z, y) for z in range(4) for y in range(4)]


def shift(dz, dy):
    return everywhere([((z, y), (z + dz, y + dy)) for z, y in ALL_ZY])


ROW_DOWN = [(place(0, x, c, z, y), place(1, x, c, z, y)) for x in range(2) for c in range(2) for z, y in ALL_ZY]
CORE_SWAP = [
    (place(r, x, c, z, y), place(r, x, 1 - c, z, y)) for r in range(2) for x in range(2) for c in range(2) for z, y in ALL_ZY
]
X_SWAP = [
    (place(r, x, c, z, y), place(r, 1 - x, c, z, y)) for r in range(2) for x in range(2) for c in range(2) for z, y in ALL_ZY
]


def coset(z, y):
    return (z + 2 * y) % 4


SIDE = everywhere([((z, y), (z, 3 - y)) for z, y in ALL_ZY])
ROW_SWAP = ROW_DOWN + [(b, a) for a, b in ROW_DOWN]


def member(z, y):
    near = ((y == 0) & (z != 2)) | ((y == 3) & (z == 0))
    far = ((y == 1) & (z != 2)) | ((y == 2) & (z == 0))
    third = ((z == 2) & (y < 2)) | ((z == 1) & (y >= 2))
    return jnp.where(near, 0, jnp.where(far, 1, jnp.where(third, 2, 3)))


def member_pairs():
    swap, first, second = [], [], []
    for c in range(4):
        m = {}
        for z, y in ALL_ZY:
            near = (y == 0 and z != 2) or (z, y) == (0, 3)
            far = (y == 1 and z != 2) or (z, y) == (0, 2)
            third = (z == 2 and y < 2) or (z == 1 and y >= 2)
            if coset(z, y) == c:
                m[0 if near else 1 if far else 2 if third else 3] = (z, y)
        swap += [(m[0], m[1]), (m[1], m[0])]
        first += [(m[0], m[2]), (m[1], m[3])]
        second += [(m[0], m[3]), (m[1], m[2])]
    return everywhere(swap), everywhere(first), everywhere(second)


SWAP_PAIRS, FIRST_PAIRS, SECOND_PAIRS = member_pairs()


def send(value, pairs):
    return lax.ppermute(value, AXES, pairs)


def in_vmem(value):
    return pltpu.with_memory_space_constraint(value, pltpu.VMEM)


def exact_dot(left, right):
    return jnp.dot(left, right, precision=lax.Precision.HIGHEST, preferred_element_type=jnp.float32)


def factor_kernel(info, d_mine, d_other, top, update_out, top_out, f):
    core, panel, second = info[0], info[1], info[2]
    for half in range(2):
        @pl.when(core == half)
        def _():
            for part in range(2):
                f[half * DPART : (half + 1) * DPART, part * WIDTH : (part + 1) * WIDTH] = d_mine[part]
                f[(1 - half) * DPART : (2 - half) * DPART, part * WIDTH : (part + 1) * WIDTH] = d_other[part]

    f[0:P_SIZE, P_SIZE:] = top[...]
    rows = lax.broadcasted_iota(jnp.int32, (P_SIZE, P_SIZE), 0)
    cols = lax.broadcasted_iota(jnp.int32, (P_SIZE, P_SIZE), 1)
    f[P_SIZE:, 0:P_SIZE] = jnp.where(rows == cols, 1.0, 0.0)
    f[P_SIZE:, P_SIZE:] = jnp.zeros((P_SIZE, WIDTH), jnp.float32)
    total = P_SIZE + WIDTH
    for block in range(P_SIZE // B):
        lo, hi = block * B, block * B + B
        base = lo // WIDTH * WIDTH
        r = lax.broadcasted_iota(jnp.int32, (WIDTH, WIDTH), 0) + base
        c = lax.broadcasted_iota(jnp.int32, (WIDTH, WIDTH), 1) + base
        in_block = (r >= lo) & (r < hi) & (c >= lo) & (c < hi)
        on_diag = in_block & (r == c)
        window = f[base : base + WIDTH, base : base + WIDTH]
        pivot = jnp.where(in_block, window, 0.0)
        diag = jnp.where(on_diag, window, 0.0)
        diag_row = jnp.sum(diag, axis=0, keepdims=True)
        diag_col = jnp.sum(diag, axis=1, keepdims=True)
        inv_row = 1.0 / jnp.where(diag_row == 0.0, 1.0, diag_row)
        inv_col = 1.0 / jnp.where(diag_col == 0.0, 1.0, diag_col)
        inverse = jnp.where(on_diag, 2.0 * inv_row, 0.0) - inv_col * (pivot * inv_row)
        for _ in range(ITERS - 1):
            inverse = 2.0 * inverse - exact_dot(inverse, exact_dot(pivot, inverse))
        lower = exact_dot(f[hi:, base : base + WIDTH], inverse)
        col = lax.broadcasted_iota(jnp.int32, (WIDTH, total), 1)
        upper = jnp.where(col >= hi, f[base : base + WIDTH, :], 0.0)
        f[hi:, :] = f[hi:, :] - exact_dot(lower, upper)
        lane = lax.broadcasted_iota(jnp.int32, lower.shape, 1) + base
        mine = (lane >= lo) & (lane < hi)
        f[hi:, base : base + WIDTH] = jnp.where(mine, lower, f[hi:, base : base + WIDTH])

    def finish(update, done):
        high = update.astype(jnp.bfloat16)
        low = (update - high.astype(jnp.float32)).astype(jnp.bfloat16)
        update_out[...] = jnp.concatenate([high, low], axis=1)
        top_out[...] = done

    @pl.when(panel == 0)
    def _():
        finish(f[P_SIZE:, P_SIZE:], f[0:P_SIZE, P_SIZE:])

    for part in range(2):
        @pl.when((panel == 1) & (second == part))
        def _():
            side = slice(part * WIDTH, (part + 1) * WIDTH)
            finish(f[P_SIZE:, side], f[0:P_SIZE, side])


def factor(info, d_mine, d_other, top):
    vmem = pl.BlockSpec(memory_space=pltpu.VMEM)
    return pl.pallas_call(
        factor_kernel,
        out_shape=(pltpu.VMEM((P_SIZE, 2 * WIDTH), jnp.bfloat16), pltpu.VMEM((P_SIZE, WIDTH), jnp.float32)),
        in_specs=[pl.BlockSpec(memory_space=pltpu.SMEM), vmem, vmem, vmem],
        out_specs=(vmem, vmem),
        scratch_shapes=[pltpu.VMEM((2 * P_SIZE, P_SIZE + WIDTH), jnp.float32)],
        compiler_params=pltpu.CompilerParams(vmem_limit_bytes=12 << 20),
        cost_estimate=pl.CostEstimate(flops=9_000_000_000, bytes_accessed=2_000_000, transcendentals=0),
        name="factor",
    )(info, in_vmem(d_mine), in_vmem(d_other), in_vmem(top))


def update_body(places, info, front, parts, update, top, out):
    step = pl.program_id(0)

    def rows_of(part, rows):
        panel = jnp.concatenate([part[0], part[1]], axis=1)
        high = panel.astype(jnp.bfloat16)
        low = (panel - high.astype(jnp.float32)).astype(jnp.bfloat16)
        both = jnp.dot(high, update[...], preferred_element_type=jnp.float32)
        both = both + jnp.dot(low, update[...], preferred_element_type=jnp.float32)
        out[rows, :] = jnp.where(info[1] == 0, front[rows, :], 0.0) + (both[:, :WIDTH] + both[:, WIDTH:])

    for at in range(3):
        @pl.when(step == at)
        def _():
            rows_of(parts[at], slice(0, SHARE))

    @pl.when(step == 3)
    def _():
        rows_of(parts[3], slice(0, SHARE // 2))
        rows_of(parts[4], slice(SHARE // 2, SHARE))

    @pl.when((places[step] == 0) & (info[3] == 0))
    def _():
        out[0:P_SIZE, :] = top[...]


def first_update_kernel(places, info, front, p0, p1, p2, p3, p4, update, top, out):
    update_body(places, info, front, (p0, p1, p2, p3, p4), update, top, out)


def second_update_kernel(places, info, front, p0, p1, p2, p3, p4, update, top, _, out):
    update_body(places, info, front, (p0, p1, p2, p3, p4), update, top, out)


def apply_update(places, info, front, parts, update, top, done=None):
    vmem = pl.BlockSpec(memory_space=pltpu.VMEM)
    block = pl.BlockSpec((SHARE, WIDTH), lambda i, places, info: (places[i], 0))
    more = [] if done is None else [pl.BlockSpec(memory_space=pl.ANY)]
    extra = [] if done is None else [done]
    return pl.pallas_call(
        first_update_kernel if done is None else second_update_kernel,
        out_shape=jax.ShapeDtypeStruct((ROWS, WIDTH), jnp.float32),
        grid_spec=pltpu.PrefetchScalarGridSpec(
            num_scalar_prefetch=2,
            grid=(4,),
            in_specs=[block] + [vmem] * 7 + more,
            out_specs=block,
        ),
        input_output_aliases={} if done is None else {10: 0},
        compiler_params=pltpu.CompilerParams(vmem_limit_bytes=12 << 20),
        cost_estimate=pl.CostEstimate(flops=3_000_000_000, bytes_accessed=4_000_000, transcendentals=0),
        name="update_mine" if done is None else "update_other",
    )(places, info, front, *map(in_vmem, parts), in_vmem(update), in_vmem(top), *extra)


def per_device(front):
    row, x, core, z, y = (lax.axis_index(a) for a in AXES)
    mine = coset(z, y)
    panel = (x == 0) & (z == 0) & (y < 2) & (core == 0)
    info = jnp.stack([core, panel.astype(jnp.int32), y, row]).astype(jnp.int32)

    d_part = jnp.where(core == 0, front[:DPART], send(front[DPART:P_SIZE], CORE_SWAP))
    beside = send(front, CORE_SWAP)
    d_part = jnp.where(row == 0, d_part, send(d_part, ROW_SWAP))

    def share(delta):
        start = (mine + delta) % 4 * SHARE
        kept = lax.dynamic_slice(front, (start, 0), (SHARE, WIDTH))
        given = lax.dynamic_slice(beside, (start + ROWS // 2, 0), (SHARE, WIDTH))
        return jnp.concatenate([d_part, jnp.where(core == 0, kept, given)])

    up = send(share(1), shift(1, 0))
    down = send(share(3), shift(-1, 0))
    side = send(share(2), SIDE)
    top_swapped = send(front[:P_SIZE], ROW_SWAP)
    top = jnp.where(row == 0, front[:P_SIZE], top_swapped)
    near = y < 2
    held = jnp.where((z == 1) & near, up, jnp.where((z == 3) & near, down, jnp.where(near, share(0), side)))
    held = jnp.where(x == 0, held, send(held, X_SWAP))

    to_first = send(held, FIRST_PAIRS)
    swapped = send(held, SWAP_PAIRS)
    to_second = send(held, SECOND_PAIRS)
    role = member(z, y)

    def pick(a, b, c, d):
        return jnp.where(role == 0, a, jnp.where(role == 1, b, jnp.where(role == 2, c, d)))

    left = pick(held, swapped, to_first, to_second)
    right = pick(swapped, held, to_second, to_first)
    d_mine = jnp.stack([left[:DPART], right[:DPART]])
    own = jnp.stack([left[DPART:], right[DPART:]])
    d_other = send(d_mine, CORE_SWAP)
    before = send(own, shift(1, 0))
    after = send(own, shift(-1, 0))
    far_low = send(own[:, : SHARE // 2], shift(0, 1))
    far_high = send(own[:, SHARE // 2 :], shift(0, -1))
    own_other = send(own, CORE_SWAP)
    update, top_done = factor(info, d_mine, d_other, top)

    parts = (own, before, after, far_low, far_high)
    others = (own_other, *(send(v, CORE_SWAP) for v in parts[1:]))
    order = [mine, (mine + 3) % 4, (mine + 1) % 4, (mine + 2) % 4]
    places = [jnp.stack([p + 4 * c for p in order]).astype(jnp.int32) for c in (core, 1 - core)]
    out = apply_update(places[0], info, front, parts, update, top_done)
    return apply_update(places[1], info, front, others, update, top_done, out)


def solution(mesh):
    wide = jax.sharding.Mesh(mesh.devices.reshape(SHAPE), AXES)
    spec = P("row", ("x", "core", "z", "y"))

    return jax.shard_map(per_device, mesh=wide, in_specs=(spec,), out_specs=spec, check_vma=False)
```

profile of v0, /device:TPU:25, one launch (start us, length us, event | category | flops | bytes accessed | tf_op | source)
XLA Modules:
  0.0 81.7 jit_solution(9287038121995666953)
XLA Ops:
  0.0 0.7 collective-permute-start.2
  0.7 0.8 %slice.29 = f32[128,128]{1,0:T(8,128)S(1)} slice(f32[4096,128]{1,0:T(8,128)} %front.3), slice={[128:256], [0:128]} | slice | bytes 131072 | tf_op jit(solution)/shard_map/slice | solution.py:225
  1.5 3.2 %collective-permute-done = f32[128,128]{1,0:T(8,128)S(1)} collective-permute-done((f32[128,128]{1,0:T(8,128)S(1)}, f32[128,128]{1,0:T(8,128)S(1)}, u32[]{:S(2)}, u32[]{:S(2)}) %collective-permute-start) | collective-permute-done | bytes 65568 | tf_op jit(solution)/shard_map/ppermute | solution.py:82
  4.8 0.8 %slice_select_fusion = f32[128,128]{1,0:T(8,128)S(1)} fusion(f32[128,128]{1,0:T(8,128)S(1)} %collective-permute-done, f32[4096,128]{1,0:T(8,128)} %front.3, pred[]{:T(512)S(6)} %eq.66), kind=kLoop, calls=%fused_computation.26 | loop fusion | flops 16384 | bytes 196609 | tf_op jit(solution)/shard_map/jit(_where)/select_n | solution.py:225
  5.6 2.8 %collective-permute-start.1 = (f32[128,128]{1,0:T(8,128)S(1)}, f32[128,128]{1,0:T(8,128)S(1)}, u32[]{:S(2)}, u32[]{:S(2)}) collective-permute-start(f32[128,128]{1,0:T(8,128)S(1)} %slice_select_fusion), channel_id=1, source_target_pairs={{0,64},{1,65},{2,66},{3,67},{4,68},{5,69},{6,70},{7,71},{8,72},{9,... | collective-permute-start | bytes 196616 | tf_op jit(solution)/shard_map/ppermute | solution.py:82
  8.4 1.9 %collective-permute-done.1 = f32[128,128]{1,0:T(8,128)S(1)} collective-permute-done((f32[128,128]{1,0:T(8,128)S(1)}, f32[128,128]{1,0:T(8,128)S(1)}, u32[]{:S(2)}, u32[]{:S(2)}) %collective-permute-start.1) | collective-permute-done | bytes 65568 | tf_op jit(solution)/shard_map/ppermute | solution.py:82
  10.3 1.3 %dynamic-slice_select_fusion.1 = (f32[512,128]{1,0:T(8,128)S(1)}, f32[512,128]{1,0:T(8,128)S(1)}, f32[512,128]{1,0:T(8,128)S(1)}, f32[512,128]{1,0:T(8,128)S(1)}) fusion(f32[4096,128]{1,0:T(8,128)S(1)} %collective-permute-done.2, s32[]{:T(128)S(6)} %select_n.189, f32[4096,128]{1,0:T(8,128)} %front.3, s32[]{:T(128)S(6)} %select_n.188, pred[]{:T(512)S(6)} %eq.66, ...), kind=kLoop, calls=%fused_computation.19 | loop fusion | flops 262144 | bytes 3145761 | tf_op jit(solution)/shard_map/jit(_where)/select_n | solution.py:233
  11.7 1.7 %collective-permute-start.3 = (f32[640,128]{1,0:T(8,128)S(1)}, f32[640,128]{1,0:T(8,128)}, u32[]{:S(2)}, u32[]{:S(2)}) collective-permute-start(f32[640,128]{1,0:T(8,128)S(1)} %get-tuple-element.19), channel_id=1, source_target_pairs={{0,4},{1,5},{2,6},{3,7},{4,8},{5,9},{6,10},{7,11},{8,12},{9,13},{1... | collective-permute-start | bytes 983048 | tf_op jit(solution)/shard_map/ppermute | solution.py:82
  13.4 2.2 %collective-permute-start.4 = (f32[640,128]{1,0:T(8,128)S(1)}, f32[640,128]{1,0:T(8,128)}, u32[]{:S(2)}, u32[]{:S(2)}) collective-permute-start(f32[640,128]{1,0:T(8,128)S(1)} %get-tuple-element.18), channel_id=1, source_target_pairs={{0,12},{1,13},{2,14},{3,15},{4,0},{5,1},{6,2},{7,3},{8,4},{9,5},{1... | collective-permute-start | bytes 983048 | tf_op jit(solution)/shard_map/ppermute | solution.py:82
  15.7 6.6 %collective-permute-done.3 = f32[640,128]{1,0:T(8,128)} collective-permute-done((f32[640,128]{1,0:T(8,128)S(1)}, f32[640,128]{1,0:T(8,128)}, u32[]{:S(2)}, u32[]{:S(2)}) %collective-permute-start.3) | collective-permute-done | bytes 327712 | tf_op jit(solution)/shard_map/ppermute | solution.py:82
  22.2 2.2 %collective-permute-done.5 = f32[640,128]{1,0:T(8,128)} collective-permute-done((f32[640,128]{1,0:T(8,128)S(1)}, f32[640,128]{1,0:T(8,128)}, u32[]{:S(2)}, u32[]{:S(2)}) %collective-permute-start.5) | collective-permute-done | bytes 327712 | tf_op jit(solution)/shard_map/ppermute | solution.py:82
  24.4 1.0 %fusion.2 = f32[640,128]{1,0:T(8,128)S(1)} fusion(f32[640,128]{1,0:T(8,128)} %collective-permute-done.3, f32[640,128]{1,0:T(8,128)} %collective-permute-done.4, f32[640,128]{1,0:T(8,128)} %collective-permute-done.5, f32[128,128]{1,0:T(8,128)S(1)} %broadcast_select_fusion.2, f32[512,128]{1,0:T(8,128)S(1)} %get-tuple-element.9, pred[]{:T(512)S(6)} %lt.61, ...), kind=kLoop, calls=%fused_computation.11 | loop fusion | flops 327680 | bytes 1638403 | tf_op jit(solution)/shard_map/jit(_where)/select_n | solution.py:241
  25.5 1.3 %collective-permute-start.6 = (f32[640,128]{1,0:T(8,128)S(1)}, f32[640,128]{1,0:T(8,128)S(1)}, u32[]{:S(2)}, u32[]{:S(2)}) collective-permute-start(f32[640,128]{1,0:T(8,128)S(1)} %fusion.2), channel_id=1, source_target_pairs={{0,32},{1,33},{2,34},{3,35},{4,36},{5,37},{6,38},{7,39},{8,40},{9,... | collective-permute-start | bytes 983048 | tf_op jit(solution)/shard_map/ppermute | solution.py:82
  26.8 5.4 %collective-permute-done.6 = f32[640,128]{1,0:T(8,128)S(1)} collective-permute-done((f32[640,128]{1,0:T(8,128)S(1)}, f32[640,128]{1,0:T(8,128)S(1)}, u32[]{:S(2)}, u32[]{:S(2)}) %collective-permute-start.6) | collective-permute-done | bytes 327712 | tf_op jit(solution)/shard_map/ppermute | solution.py:82
  32.2 1.9 %collective-permute-start.7 = (f32[640,128]{1,0:T(8,128)S(1)}, f32[640,128]{1,0:T(8,128)S(1)}, u32[]{:S(2)}, u32[]{:S(2)}) collective-permute-start(f32[640,128]{1,0:T(8,128)S(1)} %broadcast_select_fusion), channel_id=1, source_target_pairs={{0,2},{2,0},{4,13},{13,4},{3,1},{1,3},{12,5},{5,12},{16,18},{18,16... | collective-permute-start | bytes 983048 | tf_op jit(solution)/shard_map/ppermute | solution.py:82
  34.1 1.3 %collective-permute-start.8 = (f32[640,128]{1,0:T(8,128)S(1)}, f32[640,128]{1,0:T(8,128)S(1)}, u32[]{:S(2)}, u32[]{:S(2)}) collective-permute-start(f32[640,128]{1,0:T(8,128)S(1)} %broadcast_select_fusion), channel_id=1, source_target_pairs={{0,9},{2,11},{4,6},{13,15},{3,8},{1,10},{12,7},{5,14},{16,25},{18,... | collective-permute-start | bytes 983048 | tf_op jit(solution)/shard_map/ppermute | solution.py:82
  35.4 1.3 %collective-permute-start.9 = (f32[640,128]{1,0:T(8,128)S(1)}, f32[640,128]{1,0:T(8,128)S(1)}, u32[]{:S(2)}, u32[]{:S(2)}) collective-permute-start(f32[640,128]{1,0:T(8,128)S(1)} %broadcast_select_fusion), channel_id=1, source_target_pairs={{0,11},{2,9},{4,15},{13,6},{3,10},{1,8},{12,14},{5,7},{16,27},{18,... | collective-permute-start | bytes 983048 | tf_op jit(solution)/shard_map/ppermute | solution.py:82
  36.8 0.7 slice.36
  37.4 2.7 %collective-permute-start.20 = (f32[256,128]{1,0:T(8,128)}, f32[256,128]{1,0:T(8,128)S(1)}, u32[]{:S(2)}, u32[]{:S(2)}) collective-permute-start(f32[256,128]{1,0:T(8,128)} %slice.36), channel_id=1, source_target_pairs={{0,64},{1,65},{2,66},{3,67},{4,68},{5,69},{6,70},{7,71},{8,72},{9,... | collective-permute-start | bytes 393224 | tf_op jit(solution)/shard_map/ppermute | solution.py:82
  40.3 1.3 %collective-permute-done.7 = f32[640,128]{1,0:T(8,128)S(1)} collective-permute-done((f32[640,128]{1,0:T(8,128)S(1)}, f32[640,128]{1,0:T(8,128)S(1)}, u32[]{:S(2)}, u32[]{:S(2)}) %collective-permute-start.7) | collective-permute-done | bytes 327712 | tf_op jit(solution)/shard_map/ppermute | solution.py:82
  41.6 5.2 %collective-permute-done.8 = f32[640,128]{1,0:T(8,128)S(1)} collective-permute-done((f32[640,128]{1,0:T(8,128)S(1)}, f32[640,128]{1,0:T(8,128)S(1)}, u32[]{:S(2)}, u32[]{:S(2)}) %collective-permute-start.8) | collective-permute-done | bytes 327712 | tf_op jit(solution)/shard_map/ppermute | solution.py:82
  47.0 1.6 %collective-permute-start.11 = (f32[2,512,128]{2,1,0:T(8,128)S(1)}, f32[2,512,128]{2,1,0:T(8,128)S(1)}, u32[]{:S(2)}, u32[]{:S(2)}) collective-permute-start(f32[2,512,128]{2,1,0:T(8,128)S(1)} %pad_maximum_fusion.p0), channel_id=1, source_target_pairs={{0,4},{1,5},{2,6},{3,7},{4,8},{5,9},{6,10},{7,11},{8,12},{9,13},{1... | collective-permute-start | bytes 1572872 | tf_op jit(solution)/shard_map/ppermute | solution.py:82
  48.6 7.1 %collective-permute-start.13 = (f32[2,512,128]{2,1,0:T(8,128)S(1)}, f32[2,512,128]{2,1,0:T(8,128)S(1)}, u32[]{:S(2)}, u32[]{:S(2)}) collective-permute-start(f32[2,512,128]{2,1,0:T(8,128)S(1)} %pad_maximum_fusion.p0), channel_id=1, source_target_pairs={{0,12},{1,13},{2,14},{3,15},{4,0},{5,1},{6,2},{7,3},{8,4},{9,5},{1... | collective-permute-start | bytes 1572872 | tf_op jit(solution)/shard_map/ppermute | solution.py:82
  55.8 2.6 %collective-permute-start.19 = (f32[2,128,128]{2,1,0:T(8,128)S(1)}, f32[2,128,128]{2,1,0:T(8,128)S(1)}, u32[]{:S(2)}, u32[]{:S(2)}) collective-permute-start(f32[2,128,128]{2,1,0:T(8,128)S(1)} %pad_maximum_fusion.5.d_mine), channel_id=1, source_target_pairs={{0,16},{1,17},{2,18},{3,19},{4,20},{5,21},{6,22},{7,23},{8,24},{9,... | collective-permute-start | bytes 393224 | tf_op jit(solution)/shard_map/ppermute | solution.py:82
  58.6 0.7 collective-permute-done.19.d_other
  59.4 0.7 collective-permute-start.17
  60.1 5.6 %collective-permute-done.11.p1 = f32[2,512,128]{2,1,0:T(8,128)S(1)} collective-permute-done((f32[2,512,128]{2,1,0:T(8,128)S(1)}, f32[2,512,128]{2,1,0:T(8,128)S(1)}, u32[]{:S(2)}, u32[]{:S(2)}) %collective-permute-start.11) | collective-permute-done | bytes 524320 | tf_op jit(solution)/shard_map/ppermute | solution.py:82
  65.7 2.8 %collective-permute-start.12 = (f32[2,512,128]{2,1,0:T(8,128)S(1)}, f32[2,512,128]{2,1,0:T(8,128)S(1)}, u32[]{:S(2)}, u32[]{:S(2)}) collective-permute-start(f32[2,512,128]{2,1,0:T(8,128)S(1)} %collective-permute-done.11.p1), channel_id=1, source_target_pairs={{0,16},{1,17},{2,18},{3,19},{4,20},{5,21},{6,22},{7,23},{8,24},{9,... | collective-permute-start | bytes 1572872 | tf_op jit(solution)/shard_map/ppermute | solution.py:82
  68.5 6.4 %factor.1 = (bf16[256,256]{1,0:T(8,128)(2,1)S(1)}, f32[256,128]{1,0:T(8,128)S(1)}) custom-call(s32[4]{0:T(128)S(1)} %pad_add_fusion.1.info, f32[2,128,128]{2,1,0:T(8,128)S(1)} %pad_maximum_fusion.5.d_mine, f32[2,128,128]{2,1,0:T(8,128)S(1)} %collective-permute-done.19.d_other, f32[256,128]{1,0:T(8,128)S(1)} %broadcast_select_fusion.1.top), custom_call_target="tpu_custom_call" | custom-call | flops 8999999488 | bytes 2000000 | tf_op jit(solution)/shard_map/factor/pallas_call | solution.py:152
  75.0 0.6 collective-permute-start.16
  75.6 3.0 %update_mine.1._ = f32[4096,128]{1,0:T(8,128)} custom-call(s32[4]{0:T(128)S(1)} %get-tuple-element.21.places, s32[4]{0:T(128)S(1)} %pad_add_fusion.1.info, f32[4096,128]{1,0:T(8,128)S(1)} %copy-done, f32[2,512,128]{2,1,0:T(8,128)S(1)} %pad_maximum_fusion.p0, f32[2,512,128]{2,1,0:T(8,128)S(1)} %collective-permute-done.11.p1, ...), custom_call_target="tpu_custom_call" | custom-call | flops 3000000000 | bytes 4000000 | tf_op jit(solution)/shard_map/update_mine/pallas_call | solution.py:203
  78.7 3.0 %update_other.1 = f32[4096,128]{1,0:T(8,128)} custom-call(s32[4]{0:T(128)S(1)} %get-tuple-element.20.places, s32[4]{0:T(128)S(1)} %pad_add_fusion.1.info, f32[4096,128]{1,0:T(8,128)S(1)} %copy-done, f32[2,512,128]{2,1,0:T(8,128)S(1)} %collective-permute-done.10.p0, f32[2,512,128]{2,1,0:T(8,128)S(1)} %collective-permute-done.12.p1, ...), custom_call_target="tpu_custom_call", output_to_operand_aliasing={{}: (10, {})} | custom-call | flops 3000000000 | bytes 4000000 | tf_op jit(solution)/shard_map/update_other/pallas_call | solution.py:203
  (32 shorter events, 0.8 us)
Async XLA Ops:
  0.0 10.3 %collective-permute-start.2 = (f32[4096,128]{1,0:T(8,128)}, f32[4096,128]{1,0:T(8,128)S(1)}, u32[]{:S(2)}, u32[]{:S(2)}) collective-permute-start(f32[4096,128]{1,0:T(8,128)} %front.3), channel_id=1, source_target_pairs={{0,16},{1,17},{2,18},{3,19},{4,20},{5,21},{6,22},{7,23},{8,24},{9,... | collective-permute-start | bytes 6291464 | tf_op jit(solution)/shard_map/ppermute | solution.py:82
  1.5 3.2 %collective-permute-start = (f32[128,128]{1,0:T(8,128)S(1)}, f32[128,128]{1,0:T(8,128)S(1)}, u32[]{:S(2)}, u32[]{:S(2)}) collective-permute-start(f32[128,128]{1,0:T(8,128)S(1)} %slice.29), channel_id=1, source_target_pairs={{0,16},{1,17},{2,18},{3,19},{4,20},{5,21},{6,22},{7,23},{8,24},{9,... | collective-permute-start | bytes 196616 | tf_op jit(solution)/shard_map/ppermute | solution.py:82
  5.6 4.7 %collective-permute-start.1 = (f32[128,128]{1,0:T(8,128)S(1)}, f32[128,128]{1,0:T(8,128)S(1)}, u32[]{:S(2)}, u32[]{:S(2)}) collective-permute-start(f32[128,128]{1,0:T(8,128)S(1)} %slice_select_fusion), channel_id=1, source_target_pairs={{0,64},{1,65},{2,66},{3,67},{4,68},{5,69},{6,70},{7,71},{8,72},{9,... | collective-permute-start | bytes 196616 | tf_op jit(solution)/shard_map/ppermute | solution.py:82
  11.7 25.1 %copy-start = (f32[4096,128]{1,0:T(8,128)S(1)}, f32[4096,128]{1,0:T(8,128)}, u32[]{:S(2)}) copy-start(f32[4096,128]{1,0:T(8,128)} %front.3) | copy-start | bytes 6291460
  11.7 10.5 %collective-permute-start.3 = (f32[640,128]{1,0:T(8,128)S(1)}, f32[640,128]{1,0:T(8,128)}, u32[]{:S(2)}, u32[]{:S(2)}) collective-permute-start(f32[640,128]{1,0:T(8,128)S(1)} %get-tuple-element.19), channel_id=1, source_target_pairs={{0,4},{1,5},{2,6},{3,7},{4,8},{5,9},{6,10},{7,11},{8,12},{9,13},{1... | collective-permute-start | bytes 983048 | tf_op jit(solution)/shard_map/ppermute | solution.py:82
  13.4 8.8 %collective-permute-start.4 = (f32[640,128]{1,0:T(8,128)S(1)}, f32[640,128]{1,0:T(8,128)}, u32[]{:S(2)}, u32[]{:S(2)}) collective-permute-start(f32[640,128]{1,0:T(8,128)S(1)} %get-tuple-element.18), channel_id=1, source_target_pairs={{0,12},{1,13},{2,14},{3,15},{4,0},{5,1},{6,2},{7,3},{8,4},{9,5},{1... | collective-permute-start | bytes 983048 | tf_op jit(solution)/shard_map/ppermute | solution.py:82
  15.7 8.8 %collective-permute-start.5 = (f32[640,128]{1,0:T(8,128)S(1)}, f32[640,128]{1,0:T(8,128)}, u32[]{:S(2)}, u32[]{:S(2)}) collective-permute-start(f32[640,128]{1,0:T(8,128)S(1)} %get-tuple-element.17), channel_id=1, source_target_pairs={{0,3},{1,2},{2,1},{3,0},{4,7},{5,6},{6,5},{7,4},{8,11},{9,10},{10,... | collective-permute-start | bytes 983048 | tf_op jit(solution)/shard_map/ppermute | solution.py:82
  25.5 6.7 %collective-permute-start.6 = (f32[640,128]{1,0:T(8,128)S(1)}, f32[640,128]{1,0:T(8,128)S(1)}, u32[]{:S(2)}, u32[]{:S(2)}) collective-permute-start(f32[640,128]{1,0:T(8,128)S(1)} %fusion.2), channel_id=1, source_target_pairs={{0,32},{1,33},{2,34},{3,35},{4,36},{5,37},{6,38},{7,39},{8,40},{9,... | collective-permute-start | bytes 983048 | tf_op jit(solution)/shard_map/ppermute | solution.py:82
  32.2 9.4 %collective-permute-start.7 = (f32[640,128]{1,0:T(8,128)S(1)}, f32[640,128]{1,0:T(8,128)S(1)}, u32[]{:S(2)}, u32[]{:S(2)}) collective-permute-start(f32[640,128]{1,0:T(8,128)S(1)} %broadcast_select_fusion), channel_id=1, source_target_pairs={{0,2},{2,0},{4,13},{13,4},{3,1},{1,3},{12,5},{5,12},{16,18},{18,16... | collective-permute-start | bytes 983048 | tf_op jit(solution)/shard_map/ppermute | solution.py:82
  34.1 12.7 %collective-permute-start.8 = (f32[640,128]{1,0:T(8,128)S(1)}, f32[640,128]{1,0:T(8,128)S(1)}, u32[]{:S(2)}, u32[]{:S(2)}) collective-permute-start(f32[640,128]{1,0:T(8,128)S(1)} %broadcast_select_fusion), channel_id=1, source_target_pairs={{0,9},{2,11},{4,6},{13,15},{3,8},{1,10},{12,7},{5,14},{16,25},{18,... | collective-permute-start | bytes 983048 | tf_op jit(solution)/shard_map/ppermute | solution.py:82
  35.4 11.4 %collective-permute-start.9 = (f32[640,128]{1,0:T(8,128)S(1)}, f32[640,128]{1,0:T(8,128)S(1)}, u32[]{:S(2)}, u32[]{:S(2)}) collective-permute-start(f32[640,128]{1,0:T(8,128)S(1)} %broadcast_select_fusion), channel_id=1, source_target_pairs={{0,11},{2,9},{4,15},{13,6},{3,10},{1,8},{12,14},{5,7},{16,27},{18,... | collective-permute-start | bytes 983048 | tf_op jit(solution)/shard_map/ppermute | solution.py:82
  37.4 20.9 %collective-permute-start.20 = (f32[256,128]{1,0:T(8,128)}, f32[256,128]{1,0:T(8,128)S(1)}, u32[]{:S(2)}, u32[]{:S(2)}) collective-permute-start(f32[256,128]{1,0:T(8,128)} %slice.36), channel_id=1, source_target_pairs={{0,64},{1,65},{2,66},{3,67},{4,68},{5,69},{6,70},{7,71},{8,72},{9,... | collective-permute-start | bytes 393224 | tf_op jit(solution)/shard_map/ppermute | solution.py:82
  47.0 18.6 %collective-permute-start.11 = (f32[2,512,128]{2,1,0:T(8,128)S(1)}, f32[2,512,128]{2,1,0:T(8,128)S(1)}, u32[]{:S(2)}, u32[]{:S(2)}) collective-permute-start(f32[2,512,128]{2,1,0:T(8,128)S(1)} %pad_maximum_fusion.p0), channel_id=1, source_target_pairs={{0,4},{1,5},{2,6},{3,7},{4,8},{5,9},{6,10},{7,11},{8,12},{9,13},{1... | collective-permute-start | bytes 1572872 | tf_op jit(solution)/shard_map/ppermute | solution.py:82
  48.6 19.9 %collective-permute-start.13 = (f32[2,512,128]{2,1,0:T(8,128)S(1)}, f32[2,512,128]{2,1,0:T(8,128)S(1)}, u32[]{:S(2)}, u32[]{:S(2)}) collective-permute-start(f32[2,512,128]{2,1,0:T(8,128)S(1)} %pad_maximum_fusion.p0), channel_id=1, source_target_pairs={{0,12},{1,13},{2,14},{3,15},{4,0},{5,1},{6,2},{7,3},{8,4},{9,5},{1... | collective-permute-start | bytes 1572872 | tf_op jit(solution)/shard_map/ppermute | solution.py:82
  55.8 3.6 %collective-permute-start.19 = (f32[2,128,128]{2,1,0:T(8,128)S(1)}, f32[2,128,128]{2,1,0:T(8,128)S(1)}, u32[]{:S(2)}, u32[]{:S(2)}) collective-permute-start(f32[2,128,128]{2,1,0:T(8,128)S(1)} %pad_maximum_fusion.5.d_mine), channel_id=1, source_target_pairs={{0,16},{1,17},{2,18},{3,19},{4,20},{5,21},{6,22},{7,23},{8,24},{9,... | collective-permute-start | bytes 393224 | tf_op jit(solution)/shard_map/ppermute | solution.py:82
  58.4 20.2 %collective-permute-start.10 = (f32[2,512,128]{2,1,0:T(8,128)S(1)}, f32[2,512,128]{2,1,0:T(8,128)S(1)}, u32[]{:S(2)}, u32[]{:S(2)}) collective-permute-start(f32[2,512,128]{2,1,0:T(8,128)S(1)} %pad_maximum_fusion.p0), channel_id=1, source_target_pairs={{0,16},{1,17},{2,18},{3,19},{4,20},{5,21},{6,22},{7,23},{8,24},{9,... | collective-permute-start | bytes 1572872 | tf_op jit(solution)/shard_map/ppermute | solution.py:82
  58.5 16.4 %collective-permute-start.15 = (f32[2,256,128]{2,1,0:T(8,128)S(1)}, f32[2,256,128]{2,1,0:T(8,128)S(1)}, u32[]{:S(2)}, u32[]{:S(2)}) collective-permute-start(f32[2,256,128]{2,1,0:T(8,128)S(1)} %get-tuple-element.16), channel_id=1, source_target_pairs={{0,1},{1,2},{2,3},{3,0},{4,5},{5,6},{6,7},{7,4},{8,9},{9,10},{10,1... | collective-permute-start | bytes 786440 | tf_op jit(solution)/shard_map/ppermute | solution.py:82
  59.4 16.2 %collective-permute-start.17 = (f32[2,256,128]{2,1,0:T(8,128)S(1)}, f32[2,256,128]{2,1,0:T(8,128)S(1)}, u32[]{:S(2)}, u32[]{:S(2)}) collective-permute-start(f32[2,256,128]{2,1,0:T(8,128)S(1)} %get-tuple-element.15), channel_id=1, source_target_pairs={{0,3},{1,0},{2,1},{3,2},{4,7},{5,4},{6,5},{7,6},{8,11},{9,8},{10,9... | collective-permute-start | bytes 786440 | tf_op jit(solution)/shard_map/ppermute | solution.py:82
  65.7 13.0 %collective-permute-start.12 = (f32[2,512,128]{2,1,0:T(8,128)S(1)}, f32[2,512,128]{2,1,0:T(8,128)S(1)}, u32[]{:S(2)}, u32[]{:S(2)}) collective-permute-start(f32[2,512,128]{2,1,0:T(8,128)S(1)} %collective-permute-done.11.p1), channel_id=1, source_target_pairs={{0,16},{1,17},{2,18},{3,19},{4,20},{5,21},{6,22},{7,23},{8,24},{9,... | collective-permute-start | bytes 1572872 | tf_op jit(solution)/shard_map/ppermute | solution.py:82
  68.5 10.1 %collective-permute-start.14 = (f32[2,512,128]{2,1,0:T(8,128)S(1)}, f32[2,512,128]{2,1,0:T(8,128)S(1)}, u32[]{:S(2)}, u32[]{:S(2)}) collective-permute-start(f32[2,512,128]{2,1,0:T(8,128)S(1)} %collective-permute-done.13.p2), channel_id=1, source_target_pairs={{0,16},{1,17},{2,18},{3,19},{4,20},{5,21},{6,22},{7,23},{8,24},{9,... | collective-permute-start | bytes 1572872 | tf_op jit(solution)/shard_map/ppermute | solution.py:82
  75.0 3.7 %collective-permute-start.16 = (f32[2,256,128]{2,1,0:T(8,128)S(1)}, f32[2,256,128]{2,1,0:T(8,128)S(1)}, u32[]{:S(2)}, u32[]{:S(2)}) collective-permute-start(f32[2,256,128]{2,1,0:T(8,128)S(1)} %collective-permute-done.15.p3), channel_id=1, source_target_pairs={{0,16},{1,17},{2,18},{3,19},{4,20},{5,21},{6,22},{7,23},{8,24},{9,... | collective-permute-start | bytes 786440 | tf_op jit(solution)/shard_map/ppermute | solution.py:82
  75.5 3.1 %collective-permute-start.18 = (f32[2,256,128]{2,1,0:T(8,128)S(1)}, f32[2,256,128]{2,1,0:T(8,128)S(1)}, u32[]{:S(2)}, u32[]{:S(2)}) collective-permute-start(f32[2,256,128]{2,1,0:T(8,128)S(1)} %collective-permute-done.17.p4), channel_id=1, source_target_pairs={{0,16},{1,17},{2,18},{3,19},{4,20},{5,21},{6,22},{7,23},{8,24},{9,... | collective-permute-start | bytes 786440 | tf_op jit(solution)/shard_map/ppermute | solution.py:82
where the time goes:
time: 82 us; the launch traced here: 81.7 us
  waiting for transfers between devices  32.2 us (39%)
  starting transfers between devices  31.7 us (39%)
  Pallas kernels  12.4 us (15%)
  other arithmetic  3.64 us (4%)
  local copies, waits for them, and re-layouts  1.56 us (2%)
    ppermute x21, waiting for transfers between devices, send(): return lax.ppermute(value, AXES, pairs)  32.2 us
    ppermute x21, starting transfers between devices, send(): return lax.ppermute(value, AXES, pairs)  31.7 us
    pallas_call x1, Pallas kernels, factor(): pl.pallas_call(factor_kernel, out_shape=(pltpu.VMEM((P_SIZE, 2 * WIDTH),...  6.4 us
    pallas_call x2, Pallas kernels, apply_update(): pl.pallas_call(first_update_kernel if done is None else second_update_ker...  6 us
  transfers between devices with their start and end apart: 21, of which 9 were waited for; matrix products, arithmetic and copies ran while one was open for 3% of the time, Pallas kernels for 12%

commit v1 on v0

--- a/solution.py
+++ b/solution.py
@@ -86,8 +86,20 @@
     return pltpu.with_memory_space_constraint(value, pltpu.VMEM)
 
 
-def exact_dot(left, right):
-    return jnp.dot(left, right, precision=lax.Precision.HIGHEST, preferred_element_type=jnp.float32)
+def split3(value):
+    high = value.astype(jnp.bfloat16)
+    rest = value - high.astype(jnp.float32)
+    middle = rest.astype(jnp.bfloat16)
+    low = (rest - middle.astype(jnp.float32)).astype(jnp.bfloat16)
+    return high, middle, low
+
+
+def stacked_dot(left, right):
+    lh, lm, ll = split3(left)
+    rh, rm, rl = split3(right)
+    lefts = jnp.concatenate([ll, lh, lm, lm, lh, lh], axis=1)
+    rights = jnp.concatenate([rh, rl, rm, rh, rm, rh], axis=0)
+    return jnp.dot(lefts, rights, preferred_element_type=jnp.float32)
 
 
 def factor_kernel(info, d_mine, d_other, top, update_out, top_out, f):
@@ -121,11 +133,12 @@
         inv_col = 1.0 / jnp.where(diag_col == 0.0, 1.0, diag_col)
         inverse = jnp.where(on_diag, 2.0 * inv_row, 0.0) - inv_col * (pivot * inv_row)
         for _ in range(ITERS - 1):
-            inverse = 2.0 * inverse - exact_dot(inverse, exact_dot(pivot, inverse))
-        lower = exact_dot(f[hi:, base : base + WIDTH], inverse)
-        col = lax.broadcasted_iota(jnp.int32, (WIDTH, total), 1)
-        upper = jnp.where(col >= hi, f[base : base + WIDTH, :], 0.0)
-        f[hi:, :] = f[hi:, :] - exact_dot(lower, upper)
+            inverse = 2.0 * inverse - stacked_dot(inverse, stacked_dot(pivot, inverse))
+        lower = stacked_dot(f[hi:, base : base + WIDTH], inverse)
+        left_col = hi // WIDTH * WIDTH
+        col = lax.broadcasted_iota(jnp.int32, (WIDTH, total - left_col), 1) + left_col
+        upper = jnp.where(col >= hi, f[base : base + WIDTH, left_col:], 0.0)
+        f[hi:, left_col:] = f[hi:, left_col:] - stacked_dot(lower, upper)
         lane = lax.broadcasted_iota(jnp.int32, lower.shape, 1) + base
         mine = (lane >= lo) & (lane < hi)
         f[hi:, base : base + WIDTH] = jnp.where(mine, lower, f[hi:, base : base + WIDTH])
@@ -155,7 +168,7 @@
         in_specs=[pl.BlockSpec(memory_space=pltpu.SMEM), vmem, vmem, vmem],
         out_specs=(vmem, vmem),
         scratch_shapes=[pltpu.VMEM((2 * P_SIZE, P_SIZE + WIDTH), jnp.float32)],
-        compiler_params=pltpu.CompilerParams(vmem_limit_bytes=12 << 20),
+        compiler_params=pltpu.CompilerParams(vmem_limit_bytes=4 << 20),
         cost_estimate=pl.CostEstimate(flops=9_000_000_000, bytes_accessed=2_000_000, transcendentals=0),
         name="factor",
     )(info, in_vmem(d_mine), in_vmem(d_other), in_vmem(top))
@@ -164,35 +177,27 @@
 def update_body(places, info, front, parts, update, top, out):
     step = pl.program_id(0)
 
-    def rows_of(part, rows):
-        panel = jnp.concatenate([part[0], part[1]], axis=1)
-        high = panel.astype(jnp.bfloat16)
-        low = (panel - high.astype(jnp.float32)).astype(jnp.bfloat16)
-        both = jnp.dot(high, update[...], preferred_element_type=jnp.float32)
-        both = both + jnp.dot(low, update[...], preferred_element_type=jnp.float32)
-        out[rows, :] = jnp.where(info[1] == 0, front[rows, :], 0.0) + (both[:, :WIDTH] + both[:, WIDTH:])
-
-    for at in range(3):
+    for at in range(4):
         @pl.when(step == at)
         def _():
-            rows_of(parts[at], slice(0, SHARE))
-
-    @pl.when(step == 3)
-    def _():
-        rows_of(parts[3], slice(0, SHARE // 2))
-        rows_of(parts[4], slice(SHARE // 2, SHARE))
+            panel = jnp.concatenate([parts[at][0], parts[at][1]], axis=1)
+            high = panel.astype(jnp.bfloat16)
+            low = (panel - high.astype(jnp.float32)).astype(jnp.bfloat16)
+            both = jnp.dot(high, update[...], preferred_element_type=jnp.float32)
+            both = both + jnp.dot(low, update[...], preferred_element_type=jnp.float32)
+            out[...] = jnp.where(info[1] == 0, front[...], 0.0) + (both[:, :WIDTH] + both[:, WIDTH:])
 
     @pl.when((places[step] == 0) & (info[3] == 0))
     def _():
         out[0:P_SIZE, :] = top[...]
 
 
-def first_update_kernel(places, info, front, p0, p1, p2, p3, p4, update, top, out):
-    update_body(places, info, front, (p0, p1, p2, p3, p4), update, top, out)
-
-
-def second_update_kernel(places, info, front, p0, p1, p2, p3, p4, update, top, _, out):
-    update_body(places, info, front, (p0, p1, p2, p3, p4), update, top, out)
+def first_update_kernel(places, info, front, p0, p1, p2, p3, update, top, out):
+    update_body(places, info, front, (p0, p1, p2, p3), update, top, out)
+
+
+def second_update_kernel(places, info, front, p0, p1, p2, p3, update, top, _, out):
+    update_body(places, info, front, (p0, p1, p2, p3), update, top, out)
 
 
 def apply_update(places, info, front, parts, update, top, done=None):
@@ -206,14 +211,14 @@
         grid_spec=pltpu.PrefetchScalarGridSpec(
             num_scalar_prefetch=2,
             grid=(4,),
-            in_specs=[block] + [vmem] * 7 + more,
+            in_specs=[block] + [vmem] * 6 + more,
             out_specs=block,
         ),
-        input_output_aliases={} if done is None else {10: 0},
-        compiler_params=pltpu.CompilerParams(vmem_limit_bytes=12 << 20),
+        input_output_aliases={} if done is None else {9: 0},
+        compiler_params=pltpu.CompilerParams(vmem_limit_bytes=4 << 20),
         cost_estimate=pl.CostEstimate(flops=3_000_000_000, bytes_accessed=4_000_000, transcendentals=0),
         name="update_mine" if done is None else "update_other",
-    )(places, info, front, *map(in_vmem, parts), in_vmem(update), in_vmem(top), *extra)
+    )(places, info, pltpu.with_memory_space_constraint(front, pltpu.HBM), *map(in_vmem, parts), in_vmem(update), in_vmem(top), *extra)
 
 
 def per_device(front):
@@ -224,7 +229,6 @@
 
     d_part = jnp.where(core == 0, front[:DPART], send(front[DPART:P_SIZE], CORE_SWAP))
     beside = send(front, CORE_SWAP)
-    d_part = jnp.where(row == 0, d_part, send(d_part, ROW_SWAP))
 
     def share(delta):
         start = (mine + delta) % 4 * SHARE
@@ -253,15 +257,15 @@
     right = pick(swapped, held, to_second, to_first)
     d_mine = jnp.stack([left[:DPART], right[:DPART]])
     own = jnp.stack([left[DPART:], right[DPART:]])
-    d_other = send(d_mine, CORE_SWAP)
     before = send(own, shift(1, 0))
     after = send(own, shift(-1, 0))
-    far_low = send(own[:, : SHARE // 2], shift(0, 1))
-    far_high = send(own[:, SHARE // 2 :], shift(0, -1))
+    far = send(own, shift(0, 1))
+    d_mine = jnp.where(row == 0, d_mine, send(d_mine, ROW_SWAP))
+    d_other = send(d_mine, CORE_SWAP)
     own_other = send(own, CORE_SWAP)
     update, top_done = factor(info, d_mine, d_other, top)
 
-    parts = (own, before, after, far_low, far_high)
+    parts = (own, before, after, far)
     others = (own_other, *(send(v, CORE_SWAP) for v in parts[1:]))
     order = [mine, (mine + 3) % 4, (mine + 1) % 4, (mine + 2) % 4]
     places = [jnp.stack([p + 4 * c for p in order]).astype(jnp.int32) for c in (core, 1 - core)]

time: 82 us -> 86.3 us (1.052)
  the two profiles are of different devices: /device:TPU:25 before, /device:TPU:1 now
where the time goes in v1:
time: 86.3 us; the launch traced here: 85.9 us
  starting transfers between devices  35.2 us (41%)
  waiting for transfers between devices  30.9 us (36%)
  Pallas kernels  14.3 us (17%)
  other arithmetic  3.54 us (4%)
  local copies, waits for them, and re-layouts  1.81 us (2%)
    ppermute x19, starting transfers between devices, send(): return lax.ppermute(value, AXES, pairs)  35.2 us
    ppermute x19, waiting for transfers between devices, send(): return lax.ppermute(value, AXES, pairs)  30.9 us
    pallas_call x2, Pallas kernels, apply_update(): pl.pallas_call(first_update_kernel if done is None else second_update_ker...  9.11 us
    pallas_call x1, Pallas kernels, factor(): pl.pallas_call(factor_kernel, out_shape=(pltpu.VMEM((P_SIZE, 2 * WIDTH),...  5.22 us
  transfers between devices with their start and end apart: 19, of which 7 were waited for; matrix products, arithmetic and copies ran while one was open for 5% of the time, Pallas kernels for 11%

profile of v1, /device:TPU:1, one launch (start us, length us, event | category | flops | bytes accessed | tf_op | source)
XLA Modules:
  0.0 85.9 jit_solution(2215473255245807921)
XLA Ops:
  0.0 1.4 %collective-permute-start.1 = (f32[4096,128]{1,0:T(8,128)}, f32[4096,128]{1,0:T(8,128)S(1)}, u32[]{:S(2)}, u32[]{:S(2)}) collective-permute-start(f32[4096,128]{1,0:T(8,128)} %front.3), channel_id=1, source_target_pairs={{0,16},{1,17},{2,18},{3,19},{4,20},{5,21},{6,22},{7,23},{8,24},{9,... | collective-permute-start | bytes 6291464 | tf_op jit(solution)/shard_map/ppermute | solution.py:82
  1.4 0.8 slice.23
  2.2 3.2 %collective-permute-done = f32[128,128]{1,0:T(8,128)S(1)} collective-permute-done((f32[128,128]{1,0:T(8,128)S(1)}, f32[128,128]{1,0:T(8,128)S(1)}, u32[]{:S(2)}, u32[]{:S(2)}) %collective-permute-start) | collective-permute-done | bytes 65568 | tf_op jit(solution)/shard_map/ppermute | solution.py:82
  5.5 0.8 slice_select_fusion
  6.3 1.3 %dynamic-slice_select_fusion.1 = (f32[512,128]{1,0:T(8,128)S(1)}, f32[512,128]{1,0:T(8,128)S(1)}, f32[512,128]{1,0:T(8,128)S(1)}, f32[512,128]{1,0:T(8,128)S(1)}) fusion(f32[4096,128]{1,0:T(8,128)S(1)} %collective-permute-done.1, s32[]{:T(128)S(6)} %select_n.189, f32[4096,128]{1,0:T(8,128)} %front.3, s32[]{:T(128)S(6)} %select_n.188, pred[]{:T(512)S(6)} %eq.66, ...), kind=kLoop, calls=%fused_computation.13 | loop fusion | flops 262144 | bytes 3145761 | tf_op jit(solution)/shard_map/jit(_where)/select_n | solution.py:237
  7.7 1.8 %collective-permute-start.2 = (f32[640,128]{1,0:T(8,128)S(1)}, f32[640,128]{1,0:T(8,128)S(1)}, u32[]{:S(2)}, u32[]{:S(2)}) collective-permute-start(f32[640,128]{1,0:T(8,128)S(1)} %get-tuple-element.17), channel_id=1, source_target_pairs={{0,4},{1,5},{2,6},{3,7},{4,8},{5,9},{6,10},{7,11},{8,12},{9,13},{1... | collective-permute-start | bytes 983048 | tf_op jit(solution)/shard_map/ppermute | solution.py:82
  9.5 2.2 %collective-permute-start.3 = (f32[640,128]{1,0:T(8,128)S(1)}, f32[640,128]{1,0:T(8,128)S(1)}, u32[]{:S(2)}, u32[]{:S(2)}) collective-permute-start(f32[640,128]{1,0:T(8,128)S(1)} %get-tuple-element.16), channel_id=1, source_target_pairs={{0,12},{1,13},{2,14},{3,15},{4,0},{5,1},{6,2},{7,3},{8,4},{9,5},{1... | collective-permute-start | bytes 983048 | tf_op jit(solution)/shard_map/ppermute | solution.py:82
  11.7 2.7 %collective-permute-start.4 = (f32[640,128]{1,0:T(8,128)S(1)}, f32[640,128]{1,0:T(8,128)S(1)}, u32[]{:S(2)}, u32[]{:S(2)}) collective-permute-start(f32[640,128]{1,0:T(8,128)S(1)} %get-tuple-element.15), channel_id=1, source_target_pairs={{0,3},{1,2},{2,1},{3,0},{4,7},{5,6},{6,5},{7,4},{8,11},{9,10},{10,... | collective-permute-start | bytes 983048 | tf_op jit(solution)/shard_map/ppermute | solution.py:82
  14.5 4.9 %collective-permute-done.2 = f32[640,128]{1,0:T(8,128)S(1)} collective-permute-done((f32[640,128]{1,0:T(8,128)S(1)}, f32[640,128]{1,0:T(8,128)S(1)}, u32[]{:S(2)}, u32[]{:S(2)}) %collective-permute-start.2) | collective-permute-done | bytes 327712 | tf_op jit(solution)/shard_map/ppermute | solution.py:82
  19.4 2.3 %collective-permute-done.4 = f32[640,128]{1,0:T(8,128)S(1)} collective-permute-done((f32[640,128]{1,0:T(8,128)S(1)}, f32[640,128]{1,0:T(8,128)S(1)}, u32[]{:S(2)}, u32[]{:S(2)}) %collective-permute-start.4) | collective-permute-done | bytes 327712 | tf_op jit(solution)/shard_map/ppermute | solution.py:82
  21.8 1.3 %collective-permute-start.5 = (f32[640,128]{1,0:T(8,128)S(1)}, f32[640,128]{1,0:T(8,128)S(1)}, u32[]{:S(2)}, u32[]{:S(2)}) collective-permute-start(f32[640,128]{1,0:T(8,128)S(1)} %fusion.2), channel_id=1, source_target_pairs={{0,32},{1,33},{2,34},{3,35},{4,36},{5,37},{6,38},{7,39},{8,40},{9,... | collective-permute-start | bytes 983048 | tf_op jit(solution)/shard_map/ppermute | solution.py:82
  23.0 6.6 %collective-permute-done.5 = f32[640,128]{1,0:T(8,128)S(1)} collective-permute-done((f32[640,128]{1,0:T(8,128)S(1)}, f32[640,128]{1,0:T(8,128)S(1)}, u32[]{:S(2)}, u32[]{:S(2)}) %collective-permute-start.5) | collective-permute-done | bytes 327712 | tf_op jit(solution)/shard_map/ppermute | solution.py:82
  29.7 3.4 %collective-permute-start.6 = (f32[640,128]{1,0:T(8,128)S(1)}, f32[640,128]{1,0:T(8,128)S(1)}, u32[]{:S(2)}, u32[]{:S(2)}) collective-permute-start(f32[640,128]{1,0:T(8,128)S(1)} %broadcast_select_fusion), channel_id=1, source_target_pairs={{0,2},{2,0},{4,13},{13,4},{3,1},{1,3},{12,5},{5,12},{16,18},{18,16... | collective-permute-start | bytes 983048 | tf_op jit(solution)/shard_map/ppermute | solution.py:82
  33.1 1.3 %collective-permute-start.7 = (f32[640,128]{1,0:T(8,128)S(1)}, f32[640,128]{1,0:T(8,128)S(1)}, u32[]{:S(2)}, u32[]{:S(2)}) collective-permute-start(f32[640,128]{1,0:T(8,128)S(1)} %broadcast_select_fusion), channel_id=1, source_target_pairs={{0,9},{2,11},{4,6},{13,15},{3,8},{1,10},{12,7},{5,14},{16,25},{18,... | collective-permute-start | bytes 983048 | tf_op jit(solution)/shard_map/ppermute | solution.py:82
  34.4 2.1 %collective-permute-start.8 = (f32[640,128]{1,0:T(8,128)S(1)}, f32[640,128]{1,0:T(8,128)S(1)}, u32[]{:S(2)}, u32[]{:S(2)}) collective-permute-start(f32[640,128]{1,0:T(8,128)S(1)} %broadcast_select_fusion), channel_id=1, source_target_pairs={{0,11},{2,9},{4,15},{13,6},{3,10},{1,8},{12,14},{5,7},{16,27},{18,... | collective-permute-start | bytes 983048 | tf_op jit(solution)/shard_map/ppermute | solution.py:82
  36.5 0.9 %slice.28 = f32[256,128]{1,0:T(8,128)S(1)} slice(f32[4096,128]{1,0:T(8,128)} %front.3), slice={[0:256], [0:128]} | slice | bytes 262144 | tf_op jit(solution)/shard_map/slice | solution.py:243
  37.5 2.8 %collective-permute-start.18 = (f32[256,128]{1,0:T(8,128)S(1)}, f32[256,128]{1,0:T(8,128)S(1)}, u32[]{:S(2)}, u32[]{:S(2)}) collective-permute-start(f32[256,128]{1,0:T(8,128)S(1)} %slice.28), channel_id=1, source_target_pairs={{0,64},{1,65},{2,66},{3,67},{4,68},{5,69},{6,70},{7,71},{8,72},{9,... | collective-permute-start | bytes 393224 | tf_op jit(solution)/shard_map/ppermute | solution.py:82
  40.4 4.9 %collective-permute-done.7 = f32[640,128]{1,0:T(8,128)S(1)} collective-permute-done((f32[640,128]{1,0:T(8,128)S(1)}, f32[640,128]{1,0:T(8,128)S(1)}, u32[]{:S(2)}, u32[]{:S(2)}) %collective-permute-start.7) | collective-permute-done | bytes 327712 | tf_op jit(solution)/shard_map/ppermute | solution.py:82
  45.3 4.7 %collective-permute-done.8 = f32[640,128]{1,0:T(8,128)S(1)} collective-permute-done((f32[640,128]{1,0:T(8,128)S(1)}, f32[640,128]{1,0:T(8,128)S(1)}, u32[]{:S(2)}, u32[]{:S(2)}) %collective-permute-start.8) | collective-permute-done | bytes 327712 | tf_op jit(solution)/shard_map/ppermute | solution.py:82
  50.1 2.8 %collective-permute-start.16 = (f32[2,128,128]{2,1,0:T(8,128)S(1)}, f32[2,128,128]{2,1,0:T(8,128)S(1)}, u32[]{:S(2)}, u32[]{:S(2)}) collective-permute-start(f32[2,128,128]{2,1,0:T(8,128)S(1)} %pad_maximum_fusion.5), channel_id=1, source_target_pairs={{0,64},{1,65},{2,66},{3,67},{4,68},{5,69},{6,70},{7,71},{8,72},{9,... | collective-permute-start | bytes 393224 | tf_op jit(solution)/shard_map/ppermute | solution.py:82
  53.1 2.7 %collective-permute-start.12 = (f32[2,512,128]{2,1,0:T(8,128)S(1)}, f32[2,512,128]{2,1,0:T(8,128)S(1)}, u32[]{:S(2)}, u32[]{:S(2)}) collective-permute-start(f32[2,512,128]{2,1,0:T(8,128)S(1)} %pad_maximum_fusion.4.p0), channel_id=1, source_target_pairs={{0,12},{1,13},{2,14},{3,15},{4,0},{5,1},{6,2},{7,3},{8,4},{9,5},{1... | collective-permute-start | bytes 1572872 | tf_op jit(solution)/shard_map/ppermute | solution.py:82
  55.8 2.1 %collective-permute-start.14 = (f32[2,512,128]{2,1,0:T(8,128)S(1)}, f32[2,512,128]{2,1,0:T(8,128)S(1)}, u32[]{:S(2)}, u32[]{:S(2)}) collective-permute-start(f32[2,512,128]{2,1,0:T(8,128)S(1)} %pad_maximum_fusion.4.p0), channel_id=1, source_target_pairs={{0,1},{1,2},{2,3},{3,0},{4,5},{5,6},{6,7},{7,4},{8,9},{9,10},{10,1... | collective-permute-start | bytes 1572872 | tf_op jit(solution)/shard_map/ppermute | solution.py:82
  58.0 3.0 %collective-permute-start.17 = (f32[2,128,128]{2,1,0:T(8,128)S(1)}, f32[2,128,128]{2,1,0:T(8,128)S(1)}, u32[]{:S(2)}, u32[]{:S(2)}) collective-permute-start(f32[2,128,128]{2,1,0:T(8,128)S(1)} %broadcast_select_fusion.2.d_mine), channel_id=1, source_target_pairs={{0,16},{1,17},{2,18},{3,19},{4,20},{5,21},{6,22},{7,23},{8,24},{9,... | collective-permute-start | bytes 393224 | tf_op jit(solution)/shard_map/ppermute | solution.py:82
  60.9 0.9 %broadcast_select_fusion.1.top = f32[256,128]{1,0:T(8,128)S(1)} fusion(f32[256,128]{1,0:T(8,128)S(1)} %collective-permute-done.18, pred[]{:T(512)S(6)} %eq.77, f32[4096,128]{1,0:T(8,128)} %front.3), kind=kLoop, calls=%fused_computation.21 | loop fusion | flops 32768 | bytes 393217 | tf_op jit(solution)/shard_map/jit(_where)/select_n | solution.py:243
  61.9 0.1 collective-permute-start.9
  62.0 4.2 %collective-permute-done.10.p1 = f32[2,512,128]{2,1,0:T(8,128)S(1)} collective-permute-done((f32[2,512,128]{2,1,0:T(8,128)S(1)}, f32[2,512,128]{2,1,0:T(8,128)S(1)}, u32[]{:S(2)}, u32[]{:S(2)}) %collective-permute-start.10) | collective-permute-done | bytes 524320 | tf_op jit(solution)/shard_map/ppermute | solution.py:82
  66.1 2.5 %collective-permute-start.11 = (f32[2,512,128]{2,1,0:T(8,128)S(1)}, f32[2,512,128]{2,1,0:T(8,128)S(1)}, u32[]{:S(2)}, u32[]{:S(2)}) collective-permute-start(f32[2,512,128]{2,1,0:T(8,128)S(1)} %collective-permute-done.10.p1), channel_id=1, source_target_pairs={{0,16},{1,17},{2,18},{3,19},{4,20},{5,21},{6,22},{7,23},{8,24},{9,... | collective-permute-start | bytes 1572872 | tf_op jit(solution)/shard_map/ppermute | solution.py:82
  68.6 2.1 %collective-permute-start.13 = (f32[2,512,128]{2,1,0:T(8,128)S(1)}, f32[2,512,128]{2,1,0:T(8,128)S(1)}, u32[]{:S(2)}, u32[]{:S(2)}) collective-permute-start(f32[2,512,128]{2,1,0:T(8,128)S(1)} %collective-permute-done.12.p2), channel_id=1, source_target_pairs={{0,16},{1,17},{2,18},{3,19},{4,20},{5,21},{6,22},{7,23},{8,24},{9,... | collective-permute-start | bytes 1572872 | tf_op jit(solution)/shard_map/ppermute | solution.py:82
  70.7 0.8 collective-permute-start.15
  71.5 5.2 %factor.1 = (bf16[256,256]{1,0:T(8,128)(2,1)S(1)}, f32[256,128]{1,0:T(8,128)S(1)}) custom-call(s32[4]{0:T(128)S(1)} %pad_add_fusion.1.info, f32[2,128,128]{2,1,0:T(8,128)S(1)} %broadcast_select_fusion.2.d_mine, f32[2,128,128]{2,1,0:T(8,128)S(1)} %collective-permute-done.17.d_other, f32[256,128]{1,0:T(8,128)S(1)} %broadcast_select_fusion.1.top), custom_call_target="tpu_custom_call" | custom-call | flops 8999999488 | bytes 2000000 | tf_op jit(solution)/shard_map/factor/pallas_call | solution.py:165
  76.7 4.6 %update_mine.1._ = f32[4096,128]{1,0:T(8,128)} custom-call(s32[4]{0:T(128)S(1)} %get-tuple-element.19.places, s32[4]{0:T(128)S(1)} %pad_add_fusion.1.info, f32[4096,128]{1,0:T(8,128)} %front.3, f32[2,512,128]{2,1,0:T(8,128)S(1)} %pad_maximum_fusion.4.p0, f32[2,512,128]{2,1,0:T(8,128)S(1)} %collective-permute-done.10.p1, ...), custom_call_target="tpu_custom_call" | custom-call | flops 3000000000 | bytes 4000000 | tf_op jit(solution)/shard_map/update_mine/pallas_call | solution.py:208
  81.3 4.6 %update_other.1 = f32[4096,128]{1,0:T(8,128)} custom-call(s32[4]{0:T(128)S(1)} %get-tuple-element.18.places, s32[4]{0:T(128)S(1)} %pad_add_fusion.1.info, f32[4096,128]{1,0:T(8,128)} %front.3, f32[2,512,128]{2,1,0:T(8,128)S(1)} %collective-permute-done.9.p0, f32[2,512,128]{2,1,0:T(8,128)S(1)} %collective-permute-done.11.p1, ...), custom_call_target="tpu_custom_call", output_to_operand_aliasing={{}: (9, {})} | custom-call | flops 3000000000 | bytes 4000000 | tf_op jit(solution)/shard_map/update_other/pallas_call | solution.py:208
  (25 shorter events, 0.6 us)
Async XLA Ops:
  0.0 6.3 %collective-permute-start.1 = (f32[4096,128]{1,0:T(8,128)}, f32[4096,128]{1,0:T(8,128)S(1)}, u32[]{:S(2)}, u32[]{:S(2)}) collective-permute-start(f32[4096,128]{1,0:T(8,128)} %front.3), channel_id=1, source_target_pairs={{0,16},{1,17},{2,18},{3,19},{4,20},{5,21},{6,22},{7,23},{8,24},{9,... | collective-permute-start | bytes 6291464 | tf_op jit(solution)/shard_map/ppermute | solution.py:82
  2.2 3.2 %collective-permute-start = (f32[128,128]{1,0:T(8,128)S(1)}, f32[128,128]{1,0:T(8,128)S(1)}, u32[]{:S(2)}, u32[]{:S(2)}) collective-permute-start(f32[128,128]{1,0:T(8,128)S(1)} %slice.23), channel_id=1, source_target_pairs={{0,16},{1,17},{2,18},{3,19},{4,20},{5,21},{6,22},{7,23},{8,24},{9,... | collective-permute-start | bytes 196616 | tf_op jit(solution)/shard_map/ppermute | solution.py:82
  7.7 11.7 %collective-permute-start.2 = (f32[640,128]{1,0:T(8,128)S(1)}, f32[640,128]{1,0:T(8,128)S(1)}, u32[]{:S(2)}, u32[]{:S(2)}) collective-permute-start(f32[640,128]{1,0:T(8,128)S(1)} %get-tuple-element.17), channel_id=1, source_target_pairs={{0,4},{1,5},{2,6},{3,7},{4,8},{5,9},{6,10},{7,11},{8,12},{9,13},{1... | collective-permute-start | bytes 983048 | tf_op jit(solution)/shard_map/ppermute | solution.py:82
  9.5 9.8 %collective-permute-start.3 = (f32[640,128]{1,0:T(8,128)S(1)}, f32[640,128]{1,0:T(8,128)S(1)}, u32[]{:S(2)}, u32[]{:S(2)}) collective-permute-start(f32[640,128]{1,0:T(8,128)S(1)} %get-tuple-element.16), channel_id=1, source_target_pairs={{0,12},{1,13},{2,14},{3,15},{4,0},{5,1},{6,2},{7,3},{8,4},{9,5},{1... | collective-permute-start | bytes 983048 | tf_op jit(solution)/shard_map/ppermute | solution.py:82
  11.7 9.9 %collective-permute-start.4 = (f32[640,128]{1,0:T(8,128)S(1)}, f32[640,128]{1,0:T(8,128)S(1)}, u32[]{:S(2)}, u32[]{:S(2)}) collective-permute-start(f32[640,128]{1,0:T(8,128)S(1)} %get-tuple-element.15), channel_id=1, source_target_pairs={{0,3},{1,2},{2,1},{3,0},{4,7},{5,6},{6,5},{7,4},{8,11},{9,10},{10,... | collective-permute-start | bytes 983048 | tf_op jit(solution)/shard_map/ppermute | solution.py:82
  21.8 7.9 %collective-permute-start.5 = (f32[640,128]{1,0:T(8,128)S(1)}, f32[640,128]{1,0:T(8,128)S(1)}, u32[]{:S(2)}, u32[]{:S(2)}) collective-permute-start(f32[640,128]{1,0:T(8,128)S(1)} %fusion.2), channel_id=1, source_target_pairs={{0,32},{1,33},{2,34},{3,35},{4,36},{5,37},{6,38},{7,39},{8,40},{9,... | collective-permute-start | bytes 983048 | tf_op jit(solution)/shard_map/ppermute | solution.py:82
  29.7 10.7 %collective-permute-start.6 = (f32[640,128]{1,0:T(8,128)S(1)}, f32[640,128]{1,0:T(8,128)S(1)}, u32[]{:S(2)}, u32[]{:S(2)}) collective-permute-start(f32[640,128]{1,0:T(8,128)S(1)} %broadcast_select_fusion), channel_id=1, source_target_pairs={{0,2},{2,0},{4,13},{13,4},{3,1},{1,3},{12,5},{5,12},{16,18},{18,16... | collective-permute-start | bytes 983048 | tf_op jit(solution)/shard_map/ppermute | solution.py:82
  33.1 12.2 %collective-permute-start.7 = (f32[640,128]{1,0:T(8,128)S(1)}, f32[640,128]{1,0:T(8,128)S(1)}, u32[]{:S(2)}, u32[]{:S(2)}) collective-permute-start(f32[640,128]{1,0:T(8,128)S(1)} %broadcast_select_fusion), channel_id=1, source_target_pairs={{0,9},{2,11},{4,6},{13,15},{3,8},{1,10},{12,7},{5,14},{16,25},{18,... | collective-permute-start | bytes 983048 | tf_op jit(solution)/shard_map/ppermute | solution.py:82
  34.4 15.5 %collective-permute-start.8 = (f32[640,128]{1,0:T(8,128)S(1)}, f32[640,128]{1,0:T(8,128)S(1)}, u32[]{:S(2)}, u32[]{:S(2)}) collective-permute-start(f32[640,128]{1,0:T(8,128)S(1)} %broadcast_select_fusion), channel_id=1, source_target_pairs={{0,11},{2,9},{4,15},{13,6},{3,10},{1,8},{12,14},{5,7},{16,27},{18,... | collective-permute-start | bytes 983048 | tf_op jit(solution)/shard_map/ppermute | solution.py:82
  37.5 23.5 %collective-permute-start.18 = (f32[256,128]{1,0:T(8,128)S(1)}, f32[256,128]{1,0:T(8,128)S(1)}, u32[]{:S(2)}, u32[]{:S(2)}) collective-permute-start(f32[256,128]{1,0:T(8,128)S(1)} %slice.28), channel_id=1, source_target_pairs={{0,64},{1,65},{2,66},{3,67},{4,68},{5,69},{6,70},{7,71},{8,72},{9,... | collective-permute-start | bytes 393224 | tf_op jit(solution)/shard_map/ppermute | solution.py:82
  50.1 7.8 %collective-permute-start.16 = (f32[2,128,128]{2,1,0:T(8,128)S(1)}, f32[2,128,128]{2,1,0:T(8,128)S(1)}, u32[]{:S(2)}, u32[]{:S(2)}) collective-permute-start(f32[2,128,128]{2,1,0:T(8,128)S(1)} %pad_maximum_fusion.5), channel_id=1, source_target_pairs={{0,64},{1,65},{2,66},{3,67},{4,68},{5,69},{6,70},{7,71},{8,72},{9,... | collective-permute-start | bytes 393224 | tf_op jit(solution)/shard_map/ppermute | solution.py:82
  53.0 13.1 %collective-permute-start.10 = (f32[2,512,128]{2,1,0:T(8,128)S(1)}, f32[2,512,128]{2,1,0:T(8,128)S(1)}, u32[]{:S(2)}, u32[]{:S(2)}) collective-permute-start(f32[2,512,128]{2,1,0:T(8,128)S(1)} %pad_maximum_fusion.4.p0), channel_id=1, source_target_pairs={{0,4},{1,5},{2,6},{3,7},{4,8},{5,9},{6,10},{7,11},{8,12},{9,13},{1... | collective-permute-start | bytes 1572872 | tf_op jit(solution)/shard_map/ppermute | solution.py:82
  53.1 15.5 %collective-permute-start.12 = (f32[2,512,128]{2,1,0:T(8,128)S(1)}, f32[2,512,128]{2,1,0:T(8,128)S(1)}, u32[]{:S(2)}, u32[]{:S(2)}) collective-permute-start(f32[2,512,128]{2,1,0:T(8,128)S(1)} %pad_maximum_fusion.4.p0), channel_id=1, source_target_pairs={{0,12},{1,13},{2,14},{3,15},{4,0},{5,1},{6,2},{7,3},{8,4},{9,5},{1... | collective-permute-start | bytes 1572872 | tf_op jit(solution)/shard_map/ppermute | solution.py:82
  55.8 15.0 %collective-permute-start.14 = (f32[2,512,128]{2,1,0:T(8,128)S(1)}, f32[2,512,128]{2,1,0:T(8,128)S(1)}, u32[]{:S(2)}, u32[]{:S(2)}) collective-permute-start(f32[2,512,128]{2,1,0:T(8,128)S(1)} %pad_maximum_fusion.4.p0), channel_id=1, source_target_pairs={{0,1},{1,2},{2,3},{3,0},{4,5},{5,6},{6,7},{7,4},{8,9},{9,10},{10,1... | collective-permute-start | bytes 1572872 | tf_op jit(solution)/shard_map/ppermute | solution.py:82
  58.0 13.5 %collective-permute-start.17 = (f32[2,128,128]{2,1,0:T(8,128)S(1)}, f32[2,128,128]{2,1,0:T(8,128)S(1)}, u32[]{:S(2)}, u32[]{:S(2)}) collective-permute-start(f32[2,128,128]{2,1,0:T(8,128)S(1)} %broadcast_select_fusion.2.d_mine), channel_id=1, source_target_pairs={{0,16},{1,17},{2,18},{3,19},{4,20},{5,21},{6,22},{7,23},{8,24},{9,... | collective-permute-start | bytes 393224 | tf_op jit(solution)/shard_map/ppermute | solution.py:82
  61.9 19.4 %collective-permute-start.9 = (f32[2,512,128]{2,1,0:T(8,128)S(1)}, f32[2,512,128]{2,1,0:T(8,128)S(1)}, u32[]{:S(2)}, u32[]{:S(2)}) collective-permute-start(f32[2,512,128]{2,1,0:T(8,128)S(1)} %pad_maximum_fusion.4.p0), channel_id=1, source_target_pairs={{0,16},{1,17},{2,18},{3,19},{4,20},{5,21},{6,22},{7,23},{8,24},{9,... | collective-permute-start | bytes 1572872 | tf_op jit(solution)/shard_map/ppermute | solution.py:82
  66.1 15.2 %collective-permute-start.11 = (f32[2,512,128]{2,1,0:T(8,128)S(1)}, f32[2,512,128]{2,1,0:T(8,128)S(1)}, u32[]{:S(2)}, u32[]{:S(2)}) collective-permute-start(f32[2,512,128]{2,1,0:T(8,128)S(1)} %collective-permute-done.10.p1), channel_id=1, source_target_pairs={{0,16},{1,17},{2,18},{3,19},{4,20},{5,21},{6,22},{7,23},{8,24},{9,... | collective-permute-start | bytes 1572872 | tf_op jit(solution)/shard_map/ppermute | solution.py:82
  68.6 12.7 %collective-permute-start.13 = (f32[2,512,128]{2,1,0:T(8,128)S(1)}, f32[2,512,128]{2,1,0:T(8,128)S(1)}, u32[]{:S(2)}, u32[]{:S(2)}) collective-permute-start(f32[2,512,128]{2,1,0:T(8,128)S(1)} %collective-permute-done.12.p2), channel_id=1, source_target_pairs={{0,16},{1,17},{2,18},{3,19},{4,20},{5,21},{6,22},{7,23},{8,24},{9,... | collective-permute-start | bytes 1572872 | tf_op jit(solution)/shard_map/ppermute | solution.py:82
  70.7 10.6 %collective-permute-start.15 = (f32[2,512,128]{2,1,0:T(8,128)S(1)}, f32[2,512,128]{2,1,0:T(8,128)S(1)}, u32[]{:S(2)}, u32[]{:S(2)}) collective-permute-start(f32[2,512,128]{2,1,0:T(8,128)S(1)} %collective-permute-done.14.p3), channel_id=1, source_target_pairs={{0,16},{1,17},{2,18},{3,19},{4,20},{5,21},{6,22},{7,23},{8,24},{9,... | collective-permute-start | bytes 1572872 | tf_op jit(solution)/shard_map/ppermute | solution.py:82

commit v2 on v1

--- a/solution.py
+++ b/solution.py
@@ -55,27 +55,20 @@
 def member(z, y):
     near = ((y == 0) & (z != 2)) | ((y == 3) & (z == 0))
     far = ((y == 1) & (z != 2)) | ((y == 2) & (z == 0))
-    third = ((z == 2) & (y < 2)) | ((z == 1) & (y >= 2))
-    return jnp.where(near, 0, jnp.where(far, 1, jnp.where(third, 2, 3)))
+    third = ((y == 2) & (z != 0)) | ((y == 1) & (z == 2))
+    return 3 - 3 * near - 2 * far - third
 
 
 def member_pairs():
-    swap, first, second = [], [], []
+    spread, trade = [], []
     for c in range(4):
-        m = {}
-        for z, y in ALL_ZY:
-            near = (y == 0 and z != 2) or (z, y) == (0, 3)
-            far = (y == 1 and z != 2) or (z, y) == (0, 2)
-            third = (z == 2 and y < 2) or (z == 1 and y >= 2)
-            if coset(z, y) == c:
-                m[0 if near else 1 if far else 2 if third else 3] = (z, y)
-        swap += [(m[0], m[1]), (m[1], m[0])]
-        first += [(m[0], m[2]), (m[1], m[3])]
-        second += [(m[0], m[3]), (m[1], m[2])]
-    return everywhere(swap), everywhere(first), everywhere(second)
-
-
-SWAP_PAIRS, FIRST_PAIRS, SECOND_PAIRS = member_pairs()
+        m = {int(member(z, y)): (z, y) for z, y in ALL_ZY if coset(z, y) == c}
+        spread += [(m[0], m[2]), (m[1], m[3])]
+        trade += [(m[0], m[1]), (m[1], m[0]), (m[2], m[3]), (m[3], m[2])]
+    return everywhere(spread), everywhere(trade)
+
+
+SPREAD, TRADE = member_pairs()
 
 
 def send(value, pairs):
@@ -174,10 +167,9 @@
     )(info, in_vmem(d_mine), in_vmem(d_other), in_vmem(top))
 
 
-def update_body(places, info, front, parts, update, top, out):
+def update_body(steps, places, info, front, parts, update, top, out):
     step = pl.program_id(0)
-
-    for at in range(4):
+    for at in range(steps):
         @pl.when(step == at)
         def _():
             panel = jnp.concatenate([parts[at][0], parts[at][1]], axis=1)
@@ -192,12 +184,12 @@
         out[0:P_SIZE, :] = top[...]
 
 
-def first_update_kernel(places, info, front, p0, p1, p2, p3, update, top, out):
-    update_body(places, info, front, (p0, p1, p2, p3), update, top, out)
-
-
-def second_update_kernel(places, info, front, p0, p1, p2, p3, update, top, _, out):
-    update_body(places, info, front, (p0, p1, p2, p3), update, top, out)
+def first_update_kernel(places, info, front, p0, p1, update, top, out):
+    update_body(2, places, info, front, (p0, p1), update, top, out)
+
+
+def later_update_kernel(places, info, front, p0, p1, p2, update, top, _, out):
+    update_body(3, places, info, front, (p0, p1, p2), update, top, out)
 
 
 def apply_update(places, info, front, parts, update, top, done=None):
@@ -205,20 +197,20 @@
     block = pl.BlockSpec((SHARE, WIDTH), lambda i, places, info: (places[i], 0))
     more = [] if done is None else [pl.BlockSpec(memory_space=pl.ANY)]
     extra = [] if done is None else [done]
+    front = pltpu.with_memory_space_constraint(front, pltpu.HBM)
     return pl.pallas_call(
-        first_update_kernel if done is None else second_update_kernel,
+        first_update_kernel if done is None else later_update_kernel,
         out_shape=jax.ShapeDtypeStruct((ROWS, WIDTH), jnp.float32),
         grid_spec=pltpu.PrefetchScalarGridSpec(
             num_scalar_prefetch=2,
-            grid=(4,),
-            in_specs=[block] + [vmem] * 6 + more,
+            grid=(len(parts),),
+            in_specs=[block] + [vmem] * (len(parts) + 2) + more,
             out_specs=block,
         ),
-        input_output_aliases={} if done is None else {9: 0},
+        input_output_aliases={} if done is None else {8: 0},
         compiler_params=pltpu.CompilerParams(vmem_limit_bytes=4 << 20),
         cost_estimate=pl.CostEstimate(flops=3_000_000_000, bytes_accessed=4_000_000, transcendentals=0),
-        name="update_mine" if done is None else "update_other",
-    )(places, info, pltpu.with_memory_space_constraint(front, pltpu.HBM), *map(in_vmem, parts), in_vmem(update), in_vmem(top), *extra)
+    )(places, info, front, *map(in_vmem, parts), in_vmem(update), in_vmem(top), *extra)
 
 
 def per_device(front):
@@ -227,50 +219,63 @@
     panel = (x == 0) & (z == 0) & (y < 2) & (core == 0)
     info = jnp.stack([core, panel.astype(jnp.int32), y, row]).astype(jnp.int32)
 
-    d_part = jnp.where(core == 0, front[:DPART], send(front[DPART:P_SIZE], CORE_SWAP))
+    def start(delta):
+        return (mine + delta) % 4 * SHARE
+
+    def rows(array, at, size=SHARE):
+        return lax.dynamic_slice(array, (at, 0), (size, WIDTH))
+
+    early = lax.optimization_barrier(front)
+    kept = jnp.concatenate([early[:DPART], rows(early, start(1))])
+    given = jnp.concatenate([early[DPART:P_SIZE], rows(early, start(1) + ROWS // 2)])
+    to_up = jnp.where(core == 0, kept, send(given, CORE_SWAP))
     beside = send(front, CORE_SWAP)
+    up = send(to_up, shift(1, 0))
 
     def share(delta):
-        start = (mine + delta) % 4 * SHARE
-        kept = lax.dynamic_slice(front, (start, 0), (SHARE, WIDTH))
-        given = lax.dynamic_slice(beside, (start + ROWS // 2, 0), (SHARE, WIDTH))
-        return jnp.concatenate([d_part, jnp.where(core == 0, kept, given)])
-
-    up = send(share(1), shift(1, 0))
+        half = jnp.where(core == 0, rows(front, start(delta)), rows(beside, start(delta) + ROWS // 2))
+        return jnp.concatenate([to_up[:DPART], half])
+
     down = send(share(3), shift(-1, 0))
     side = send(share(2), SIDE)
-    top_swapped = send(front[:P_SIZE], ROW_SWAP)
-    top = jnp.where(row == 0, front[:P_SIZE], top_swapped)
     near = y < 2
     held = jnp.where((z == 1) & near, up, jnp.where((z == 3) & near, down, jnp.where(near, share(0), side)))
     held = jnp.where(x == 0, held, send(held, X_SWAP))
 
-    to_first = send(held, FIRST_PAIRS)
-    swapped = send(held, SWAP_PAIRS)
-    to_second = send(held, SECOND_PAIRS)
     role = member(z, y)
-
-    def pick(a, b, c, d):
-        return jnp.where(role == 0, a, jnp.where(role == 1, b, jnp.where(role == 2, c, d)))
-
-    left = pick(held, swapped, to_first, to_second)
-    right = pick(swapped, held, to_second, to_first)
-    d_mine = jnp.stack([left[:DPART], right[:DPART]])
-    own = jnp.stack([left[DPART:], right[DPART:]])
+    part = jnp.where(role < 2, held, send(held, SPREAD))
+    top_swapped = send(front[:P_SIZE], ROW_SWAP)
+    top = jnp.where(row == 0, front[:P_SIZE], top_swapped)
+    part, d_part = part[DPART:], part[:DPART]
+    other = send(part, TRADE)
+    d_part = jnp.where(row == 0, d_part, send(d_part, ROW_SWAP))
+    d_traded = send(d_part, TRADE)
+
+    def in_order(a, b):
+        first = role % 2 == 0
+        return jnp.stack([jnp.where(first, a, b), jnp.where(first, b, a)])
+
+    own = in_order(part, other)
+    d_mine = in_order(d_part, d_traded)
     before = send(own, shift(1, 0))
     after = send(own, shift(-1, 0))
     far = send(own, shift(0, 1))
-    d_mine = jnp.where(row == 0, d_mine, send(d_mine, ROW_SWAP))
     d_other = send(d_mine, CORE_SWAP)
     own_other = send(own, CORE_SWAP)
     update, top_done = factor(info, d_mine, d_other, top)
 
-    parts = (own, before, after, far)
-    others = (own_other, *(send(v, CORE_SWAP) for v in parts[1:]))
-    order = [mine, (mine + 3) % 4, (mine + 1) % 4, (mine + 2) % 4]
-    places = [jnp.stack([p + 4 * c for p in order]).astype(jnp.int32) for c in (core, 1 - core)]
-    out = apply_update(places[0], info, front, parts, update, top_done)
-    return apply_update(places[1], info, front, others, update, top_done, out)
+    order = [(mine + 3) % 4, (mine + 1) % 4, (mine + 2) % 4]
+
+    def at(*blocks):
+        return jnp.stack(blocks).astype(jnp.int32)
+
+    out = apply_update(at(mine + 4 * core, mine + 4 * (1 - core)), info, front, (own, own_other), update, top_done)
+    received = (before, after, far)
+    others = tuple(send(v, CORE_SWAP) for v in received)
+    places = at(*(p + 4 * core for p in order))
+    out = apply_update(places, info, front, received, update, top_done, out)
+    places = at(*(p + 4 * (1 - core) for p in order))
+    return apply_update(places, info, front, others, update, top_done, out)
 
 
 def solution(mesh):

time: 86.3 us -> 89.4 us (1.036)
  the two profiles are of different devices: /device:TPU:1 before, /device:TPU:9 now
where the time goes in v2:
time: 89.4 us; the launch traced here: 89.1 us
  starting transfers between devices  39.9 us (45%)
  waiting for transfers between devices  28.4 us (32%)
  Pallas kernels  16 us (18%)
  other arithmetic  2.61 us (3%)
  local copies, waits for them, and re-layouts  1.99 us (2%)
    ppermute x19, starting transfers between devices, send(): return lax.ppermute(value, AXES, pairs)  39.9 us
    ppermute x19, waiting for transfers between devices, send(): return lax.ppermute(value, AXES, pairs)  28.4 us
    pallas_call x3, Pallas kernels, apply_update(): pl.pallas_call(first_update_kernel if done is None else later_update_kern...  10.8 us
    pallas_call x1, Pallas kernels, factor(): pl.pallas_call(factor_kernel, out_shape=(pltpu.VMEM((P_SIZE, 2 * WIDTH),...  5.22 us
  transfers between devices with their start and end apart: 19, of which 11 were waited for; matrix products, arithmetic and copies ran while one was open for 5% of the time, Pallas kernels for 14%

profile of v2, /device:TPU:9, one launch (start us, length us, event | category | flops | bytes accessed | tf_op | source)
XLA Modules:
  0.0 89.1 jit_solution(2982730093086732527)
XLA Ops:
  0.7 1.1 %constant_dynamic-slice_fusion.1 = (f32[512,128]{1,0:T(8,128)S(1)}, f32[512,128]{1,0:T(8,128)S(1)}) fusion(f32[4096,128]{1,0:T(8,128)} %front.5, s32[]{:T(128)S(6)} %select_n.176, s32[]{:T(128)S(6)} %select_n.177), kind=kLoop, calls=%fused_computation.22 | loop fusion | bytes 1048584 | tf_op jit(solution)/shard_map/dynamic_slice | solution.py:226
  2.9 2.2 %collective-permute-done = f32[640,128]{1,0:T(8,128)S(1)} collective-permute-done((f32[640,128]{1,0:T(8,128)S(1)}, f32[640,128]{1,0:T(8,128)S(1)}, u32[]{:S(2)}, u32[]{:S(2)}) %collective-permute-start) | collective-permute-done | bytes 327712 | tf_op jit(solution)/shard_map/ppermute | solution.py:75
  5.2 1.7 %collective-permute-start.1 = (f32[640,128]{1,0:T(8,128)S(1)}, f32[640,128]{1,0:T(8,128)S(1)}, u32[]{:S(2)}, u32[]{:S(2)}) collective-permute-start(f32[640,128]{1,0:T(8,128)S(1)} %maximum_select_fusion), channel_id=1, source_target_pairs={{0,4},{1,5},{2,6},{3,7},{4,8},{5,9},{6,10},{7,11},{8,12},{9,13},{1... | collective-permute-start | bytes 983048 | tf_op jit(solution)/shard_map/ppermute | solution.py:75
  6.9 1.2 %dynamic-slice_select_fusion.1 = (f32[512,128]{1,0:T(8,128)S(1)}, f32[512,128]{1,0:T(8,128)S(1)}, f32[512,128]{1,0:T(8,128)S(1)}) fusion(f32[4096,128]{1,0:T(8,128)} %collective-permute-done.2, s32[]{:T(128)S(6)} %select_n.187, f32[4096,128]{1,0:T(8,128)S(1)} %copy-done, s32[]{:T(128)S(6)} %select_n.186, pred[]{:T(512)S(6)} %eq.65, s32[]{:T(128)S(6)} %select_n.190, ...), kind=kLoop, calls=%fused_computation.12 | loop fusion | flops 196608 | bytes 2359321 | tf_op jit(solution)/shard_map/jit(_where)/select_n | solution.py:236
  9.0 2.2 %collective-permute-start.3 = (f32[640,128]{1,0:T(8,128)}, f32[640,128]{1,0:T(8,128)S(1)}, u32[]{:S(2)}, u32[]{:S(2)}) collective-permute-start(f32[640,128]{1,0:T(8,128)} %get-tuple-element.21), channel_id=1, source_target_pairs={{0,12},{1,13},{2,14},{3,15},{4,0},{5,1},{6,2},{7,3},{8,4},{9,5},{1... | collective-permute-start | bytes 983048 | tf_op jit(solution)/shard_map/ppermute | solution.py:75
  11.1 1.3 %collective-permute-start.4 = (f32[640,128]{1,0:T(8,128)}, f32[640,128]{1,0:T(8,128)}, u32[]{:S(2)}, u32[]{:S(2)}) collective-permute-start(f32[640,128]{1,0:T(8,128)} %get-tuple-element.20), channel_id=1, source_target_pairs={{0,3},{1,2},{2,1},{3,0},{4,7},{5,6},{6,5},{7,4},{8,11},{9,10},{10,... | collective-permute-start | bytes 983048 | tf_op jit(solution)/shard_map/ppermute | solution.py:75
  12.4 4.3 %collective-permute-done.1 = f32[640,128]{1,0:T(8,128)S(1)} collective-permute-done((f32[640,128]{1,0:T(8,128)S(1)}, f32[640,128]{1,0:T(8,128)S(1)}, u32[]{:S(2)}, u32[]{:S(2)}) %collective-permute-start.1) | collective-permute-done | bytes 327712 | tf_op jit(solution)/shard_map/ppermute | solution.py:75
  16.7 1.5 %collective-permute-done.3 = f32[640,128]{1,0:T(8,128)S(1)} collective-permute-done((f32[640,128]{1,0:T(8,128)}, f32[640,128]{1,0:T(8,128)S(1)}, u32[]{:S(2)}, u32[]{:S(2)}) %collective-permute-start.3) | collective-permute-done | bytes 327712 | tf_op jit(solution)/shard_map/ppermute | solution.py:75
  18.3 1.8 %collective-permute-done.4 = f32[640,128]{1,0:T(8,128)} collective-permute-done((f32[640,128]{1,0:T(8,128)}, f32[640,128]{1,0:T(8,128)}, u32[]{:S(2)}, u32[]{:S(2)}) %collective-permute-start.4) | collective-permute-done | bytes 327712 | tf_op jit(solution)/shard_map/ppermute | solution.py:75
  20.1 1.3 %collective-permute-start.5 = (f32[640,128]{1,0:T(8,128)S(1)}, f32[640,128]{1,0:T(8,128)S(1)}, u32[]{:S(2)}, u32[]{:S(2)}) collective-permute-start(f32[640,128]{1,0:T(8,128)S(1)} %fusion.2), channel_id=1, source_target_pairs={{0,32},{1,33},{2,34},{3,35},{4,36},{5,37},{6,38},{7,39},{8,40},{9,... | collective-permute-start | bytes 983048 | tf_op jit(solution)/shard_map/ppermute | solution.py:75
  21.4 6.5 %collective-permute-done.5 = f32[640,128]{1,0:T(8,128)S(1)} collective-permute-done((f32[640,128]{1,0:T(8,128)S(1)}, f32[640,128]{1,0:T(8,128)S(1)}, u32[]{:S(2)}, u32[]{:S(2)}) %collective-permute-start.5) | collective-permute-done | bytes 327712 | tf_op jit(solution)/shard_map/ppermute | solution.py:75
  28.0 3.9 %collective-permute-start.6 = (f32[640,128]{1,0:T(8,128)S(1)}, f32[640,128]{1,0:T(8,128)S(1)}, u32[]{:S(2)}, u32[]{:S(2)}) collective-permute-start(f32[640,128]{1,0:T(8,128)S(1)} %broadcast_select_fusion), channel_id=1, source_target_pairs={{0,9},{2,11},{4,6},{13,15},{3,10},{1,8},{12,14},{5,7},{16,25},{18,... | collective-permute-start | bytes 983048 | tf_op jit(solution)/shard_map/ppermute | solution.py:75
  31.9 2.8 %collective-permute-start.17 = (f32[256,128]{1,0:T(8,128)S(1)}, f32[256,128]{1,0:T(8,128)S(1)}, u32[]{:S(2)}, u32[]{:S(2)}) collective-permute-start(f32[256,128]{1,0:T(8,128)S(1)} %slice.26), channel_id=1, source_target_pairs={{0,64},{1,65},{2,66},{3,67},{4,68},{5,69},{6,70},{7,71},{8,72},{9,... | collective-permute-start | bytes 393224 | tf_op jit(solution)/shard_map/ppermute | solution.py:75
  34.9 1.4 %collective-permute-done.6 = f32[640,128]{1,0:T(8,128)S(1)} collective-permute-done((f32[640,128]{1,0:T(8,128)S(1)}, f32[640,128]{1,0:T(8,128)S(1)}, u32[]{:S(2)}, u32[]{:S(2)}) %collective-permute-start.6) | collective-permute-done | bytes 327712 | tf_op jit(solution)/shard_map/ppermute | solution.py:75
  36.4 2.8 %collective-permute-start.14 = (f32[128,128]{1,0:T(8,128)S(1)}, f32[128,128]{1,0:T(8,128)S(1)}, u32[]{:S(2)}, u32[]{:S(2)}) collective-permute-start(f32[128,128]{1,0:T(8,128)S(1)} %slice.31), channel_id=1, source_target_pairs={{0,64},{1,65},{2,66},{3,67},{4,68},{5,69},{6,70},{7,71},{8,72},{9,... | collective-permute-start | bytes 196616 | tf_op jit(solution)/shard_map/ppermute | solution.py:75
  39.3 2.1 %collective-permute-done.14 = f32[128,128]{1,0:T(8,128)S(1)} collective-permute-done((f32[128,128]{1,0:T(8,128)S(1)}, f32[128,128]{1,0:T(8,128)S(1)}, u32[]{:S(2)}, u32[]{:S(2)}) %collective-permute-start.14) | collective-permute-done | bytes 65568 | tf_op jit(solution)/shard_map/ppermute | solution.py:75
  41.4 2.2 %collective-permute-start.15 = (f32[128,128]{1,0:T(8,128)S(1)}, f32[128,128]{1,0:T(8,128)S(1)}, u32[]{:S(2)}, u32[]{:S(2)}) collective-permute-start(f32[128,128]{1,0:T(8,128)S(1)} %broadcast_select_fusion.3), channel_id=1, source_target_pairs={{0,2},{2,0},{9,11},{11,9},{4,13},{13,4},{6,15},{15,6},{3,1},{1,3},... | collective-permute-start | bytes 196616 | tf_op jit(solution)/shard_map/ppermute | solution.py:75
  43.6 0.9 %collective-permute-start.7 = (f32[512,128]{1,0:T(8,128)S(1)}, f32[512,128]{1,0:T(8,128)S(1)}, u32[]{:S(2)}, u32[]{:S(2)}) collective-permute-start(f32[512,128]{1,0:T(8,128)S(1)} %slice.30), channel_id=1, source_target_pairs={{0,2},{2,0},{9,11},{11,9},{4,13},{13,4},{6,15},{15,6},{3,1},{1,3},... | collective-permute-start | bytes 786440 | tf_op jit(solution)/shard_map/ppermute | solution.py:75
  44.6 1.5 %collective-permute-done.15 = f32[128,128]{1,0:T(8,128)S(1)} collective-permute-done((f32[128,128]{1,0:T(8,128)S(1)}, f32[128,128]{1,0:T(8,128)S(1)}, u32[]{:S(2)}, u32[]{:S(2)}) %collective-permute-start.15) | collective-permute-done | bytes 65568 | tf_op jit(solution)/shard_map/ppermute | solution.py:75
  46.1 5.8 %collective-permute-start.16 = (f32[2,128,128]{2,1,0:T(8,128)S(1)}, f32[2,128,128]{2,1,0:T(8,128)S(1)}, u32[]{:S(2)}, u32[]{:S(2)}) collective-permute-start(f32[2,128,128]{2,1,0:T(8,128)S(1)} %pad_maximum_fusion.5.d_mine), channel_id=1, source_target_pairs={{0,16},{1,17},{2,18},{3,19},{4,20},{5,21},{6,22},{7,23},{8,24},{9,... | collective-permute-start | bytes 393224 | tf_op jit(solution)/shard_map/ppermute | solution.py:75
  52.0 4.4 %collective-permute-start.18 = (f32[2,512,128]{2,1,0:T(8,128)S(1)}, f32[2,512,128]{2,1,0:T(8,128)S(1)}, u32[]{:S(2)}, u32[]{:S(2)}) collective-permute-start(f32[2,512,128]{2,1,0:T(8,128)S(1)} %pad_maximum_fusion.3.p0), channel_id=1, source_target_pairs={{0,16},{1,17},{2,18},{3,19},{4,20},{5,21},{6,22},{7,23},{8,24},{9,... | collective-permute-start | bytes 1572872 | tf_op jit(solution)/shard_map/ppermute | solution.py:75
  56.5 2.4 %collective-permute-start.10 = (f32[2,512,128]{2,1,0:T(8,128)S(1)}, f32[2,512,128]{2,1,0:T(8,128)S(1)}, u32[]{:S(2)}, u32[]{:S(2)}) collective-permute-start(f32[2,512,128]{2,1,0:T(8,128)S(1)} %pad_maximum_fusion.3.p0), channel_id=1, source_target_pairs={{0,12},{1,13},{2,14},{3,15},{4,0},{5,1},{6,2},{7,3},{8,4},{9,5},{1... | collective-permute-start | bytes 1572872 | tf_op jit(solution)/shard_map/ppermute | solution.py:75
  58.8 3.9 %collective-permute-start.12 = (f32[2,512,128]{2,1,0:T(8,128)S(1)}, f32[2,512,128]{2,1,0:T(8,128)S(1)}, u32[]{:S(2)}, u32[]{:S(2)}) collective-permute-start(f32[2,512,128]{2,1,0:T(8,128)S(1)} %pad_maximum_fusion.3.p0), channel_id=1, source_target_pairs={{0,1},{1,2},{2,3},{3,0},{4,5},{5,6},{6,7},{7,4},{8,9},{9,10},{10,1... | collective-permute-start | bytes 1572872 | tf_op jit(solution)/shard_map/ppermute | solution.py:75
  62.8 5.2 %factor.1 = (bf16[256,256]{1,0:T(8,128)(2,1)S(1)}, f32[256,128]{1,0:T(8,128)S(1)}) custom-call(s32[4]{0:T(128)S(1)} %pad_add_fusion.1.info, f32[2,128,128]{2,1,0:T(8,128)S(1)} %pad_maximum_fusion.5.d_mine, f32[2,128,128]{2,1,0:T(8,128)S(1)} %collective-permute-done.16.d_other, f32[256,128]{1,0:T(8,128)S(1)} %broadcast_select_fusion.2.top), custom_call_target="tpu_custom_call" | custom-call | flops 8999999488 | bytes 2000000 | tf_op jit(solution)/shard_map/factor/pallas_call | solution.py:158
  68.0 3.1 %collective-permute-done.10.p1 = f32[2,512,128]{2,1,0:T(8,128)S(1)} collective-permute-done((f32[2,512,128]{2,1,0:T(8,128)S(1)}, f32[2,512,128]{2,1,0:T(8,128)S(1)}, u32[]{:S(2)}, u32[]{:S(2)}) %collective-permute-start.10) | collective-permute-done | bytes 524320 | tf_op jit(solution)/shard_map/ppermute | solution.py:75
  71.8 1.9 %collective-permute-done.12.p2 = f32[2,512,128]{2,1,0:T(8,128)S(1)} collective-permute-done((f32[2,512,128]{2,1,0:T(8,128)S(1)}, f32[2,512,128]{2,1,0:T(8,128)S(1)}, u32[]{:S(2)}, u32[]{:S(2)}) %collective-permute-start.12) | collective-permute-done | bytes 524320 | tf_op jit(solution)/shard_map/ppermute | solution.py:75
  73.7 1.2 %collective-permute-start.13 = (f32[2,512,128]{2,1,0:T(8,128)S(1)}, f32[2,512,128]{2,1,0:T(8,128)S(1)}, u32[]{:S(2)}, u32[]{:S(2)}) collective-permute-start(f32[2,512,128]{2,1,0:T(8,128)S(1)} %collective-permute-done.12.p2), channel_id=1, source_target_pairs={{0,16},{1,17},{2,18},{3,19},{4,20},{5,21},{6,22},{7,23},{8,24},{9,... | collective-permute-start | bytes 1572872 | tf_op jit(solution)/shard_map/ppermute | solution.py:75
  74.9 1.9 %collective-permute-done.8.p0 = f32[2,512,128]{2,1,0:T(8,128)S(1)} collective-permute-done((f32[2,512,128]{2,1,0:T(8,128)S(1)}, f32[2,512,128]{2,1,0:T(8,128)S(1)}, u32[]{:S(2)}, u32[]{:S(2)}) %collective-permute-start.8) | collective-permute-done | bytes 524320 | tf_op jit(solution)/shard_map/ppermute | solution.py:75
  76.8 1.5 %collective-permute-start.9 = (f32[2,512,128]{2,1,0:T(8,128)S(1)}, f32[2,512,128]{2,1,0:T(8,128)S(1)}, u32[]{:S(2)}, u32[]{:S(2)}) collective-permute-start(f32[2,512,128]{2,1,0:T(8,128)S(1)} %collective-permute-done.8.p0), channel_id=1, source_target_pairs={{0,16},{1,17},{2,18},{3,19},{4,20},{5,21},{6,22},{7,23},{8,24},{9,... | collective-permute-start | bytes 1572872 | tf_op jit(solution)/shard_map/ppermute | solution.py:75
  78.3 2.9 %shard_map.17._ = f32[4096,128]{1,0:T(8,128)} custom-call(s32[2]{0:T(128)S(1)} %pad_add_fusion.3.places, s32[4]{0:T(128)S(1)} %pad_add_fusion.1.info, f32[4096,128]{1,0:T(8,128)} %front.5, f32[2,512,128]{2,1,0:T(8,128)S(1)} %pad_maximum_fusion.3.p0, f32[2,512,128]{2,1,0:T(8,128)S(1)} %collective-permute-done.18.p1, ...), custom_call_target="tpu_custom_call" | custom-call | flops 3000000000 | bytes 4000000 | tf_op jit(solution)/shard_map/pallas_call | solution.py:201
  81.2 3.9 %shard_map.18._ = f32[4096,128]{1,0:T(8,128)} custom-call(s32[3]{0:T(128)S(1)} %get-tuple-element.23.places, s32[4]{0:T(128)S(1)} %pad_add_fusion.1.info, f32[4096,128]{1,0:T(8,128)} %front.5, f32[2,512,128]{2,1,0:T(8,128)S(1)} %collective-permute-done.8.p0, f32[2,512,128]{2,1,0:T(8,128)S(1)} %collective-permute-done.10.p1, ...), custom_call_target="tpu_custom_call", output_to_operand_aliasing={{}: (8, {})} | custom-call | flops 3000000000 | bytes 4000000 | tf_op jit(solution)/shard_map/pallas_call | solution.py:201
  85.2 3.9 %shard_map.19 = f32[4096,128]{1,0:T(8,128)} custom-call(s32[3]{0:T(128)S(1)} %get-tuple-element.22.places, s32[4]{0:T(128)S(1)} %pad_add_fusion.1.info, f32[4096,128]{1,0:T(8,128)} %front.5, f32[2,512,128]{2,1,0:T(8,128)S(1)} %collective-permute-done.9.p0, f32[2,512,128]{2,1,0:T(8,128)S(1)} %collective-permute-done.11.p1, ...), custom_call_target="tpu_custom_call", output_to_operand_aliasing={{}: (8, {})} | custom-call | flops 3000000000 | bytes 4000000 | tf_op jit(solution)/shard_map/pallas_call | solution.py:201
  (34 shorter events, 3.9 us)
Async XLA Ops:
  0.0 6.9 %copy-start = (f32[4096,128]{1,0:T(8,128)S(1)}, f32[4096,128]{1,0:T(8,128)}, u32[]{:S(2)}) copy-start(f32[4096,128]{1,0:T(8,128)} %front.5) | copy-start | bytes 6291460
  0.0 6.9 %collective-permute-start.2 = (f32[4096,128]{1,0:T(8,128)}, f32[4096,128]{1,0:T(8,128)}, u32[]{:S(2)}, u32[]{:S(2)}) collective-permute-start(f32[4096,128]{1,0:T(8,128)} %front.5), channel_id=1, source_target_pairs={{0,16},{1,17},{2,18},{3,19},{4,20},{5,21},{6,22},{7,23},{8,24},{9,... | collective-permute-start | bytes 6291464 | tf_op jit(solution)/shard_map/ppermute | solution.py:75
  2.7 2.5 %collective-permute-start = (f32[640,128]{1,0:T(8,128)S(1)}, f32[640,128]{1,0:T(8,128)S(1)}, u32[]{:S(2)}, u32[]{:S(2)}) collective-permute-start(f32[640,128]{1,0:T(8,128)S(1)} %pad_maximum_fusion.4), channel_id=1, source_target_pairs={{0,16},{1,17},{2,18},{3,19},{4,20},{5,21},{6,22},{7,23},{8,24},{9,... | collective-permute-start | bytes 983048 | tf_op jit(solution)/shard_map/ppermute | solution.py:75
  5.2 11.5 %collective-permute-start.1 = (f32[640,128]{1,0:T(8,128)S(1)}, f32[640,128]{1,0:T(8,128)S(1)}, u32[]{:S(2)}, u32[]{:S(2)}) collective-permute-start(f32[640,128]{1,0:T(8,128)S(1)} %maximum_select_fusion), channel_id=1, source_target_pairs={{0,4},{1,5},{2,6},{3,7},{4,8},{5,9},{6,10},{7,11},{8,12},{9,13},{1... | collective-permute-start | bytes 983048 | tf_op jit(solution)/shard_map/ppermute | solution.py:75
  9.0 9.3 %collective-permute-start.3 = (f32[640,128]{1,0:T(8,128)}, f32[640,128]{1,0:T(8,128)S(1)}, u32[]{:S(2)}, u32[]{:S(2)}) collective-permute-start(f32[640,128]{1,0:T(8,128)} %get-tuple-element.21), channel_id=1, source_target_pairs={{0,12},{1,13},{2,14},{3,15},{4,0},{5,1},{6,2},{7,3},{8,4},{9,5},{1... | collective-permute-start | bytes 983048 | tf_op jit(solution)/shard_map/ppermute | solution.py:75
  11.1 8.9 %collective-permute-start.4 = (f32[640,128]{1,0:T(8,128)}, f32[640,128]{1,0:T(8,128)}, u32[]{:S(2)}, u32[]{:S(2)}) collective-permute-start(f32[640,128]{1,0:T(8,128)} %get-tuple-element.20), channel_id=1, source_target_pairs={{0,3},{1,2},{2,1},{3,0},{4,7},{5,6},{6,5},{7,4},{8,11},{9,10},{10,... | collective-permute-start | bytes 983048 | tf_op jit(solution)/shard_map/ppermute | solution.py:75
  20.1 7.8 %collective-permute-start.5 = (f32[640,128]{1,0:T(8,128)S(1)}, f32[640,128]{1,0:T(8,128)S(1)}, u32[]{:S(2)}, u32[]{:S(2)}) collective-permute-start(f32[640,128]{1,0:T(8,128)S(1)} %fusion.2), channel_id=1, source_target_pairs={{0,32},{1,33},{2,34},{3,35},{4,36},{5,37},{6,38},{7,39},{8,40},{9,... | collective-permute-start | bytes 983048 | tf_op jit(solution)/shard_map/ppermute | solution.py:75
  28.0 8.4 %collective-permute-start.6 = (f32[640,128]{1,0:T(8,128)S(1)}, f32[640,128]{1,0:T(8,128)S(1)}, u32[]{:S(2)}, u32[]{:S(2)}) collective-permute-start(f32[640,128]{1,0:T(8,128)S(1)} %broadcast_select_fusion), channel_id=1, source_target_pairs={{0,9},{2,11},{4,6},{13,15},{3,10},{1,8},{12,14},{5,7},{16,25},{18,... | collective-permute-start | bytes 983048 | tf_op jit(solution)/shard_map/ppermute | solution.py:75
  31.9 11.6 %collective-permute-start.17 = (f32[256,128]{1,0:T(8,128)S(1)}, f32[256,128]{1,0:T(8,128)S(1)}, u32[]{:S(2)}, u32[]{:S(2)}) collective-permute-start(f32[256,128]{1,0:T(8,128)S(1)} %slice.26), channel_id=1, source_target_pairs={{0,64},{1,65},{2,66},{3,67},{4,68},{5,69},{6,70},{7,71},{8,72},{9,... | collective-permute-start | bytes 393224 | tf_op jit(solution)/shard_map/ppermute | solution.py:75
  36.4 5.0 %collective-permute-start.14 = (f32[128,128]{1,0:T(8,128)S(1)}, f32[128,128]{1,0:T(8,128)S(1)}, u32[]{:S(2)}, u32[]{:S(2)}) collective-permute-start(f32[128,128]{1,0:T(8,128)S(1)} %slice.31), channel_id=1, source_target_pairs={{0,64},{1,65},{2,66},{3,67},{4,68},{5,69},{6,70},{7,71},{8,72},{9,... | collective-permute-start | bytes 196616 | tf_op jit(solution)/shard_map/ppermute | solution.py:75
  41.4 4.7 %collective-permute-start.15 = (f32[128,128]{1,0:T(8,128)S(1)}, f32[128,128]{1,0:T(8,128)S(1)}, u32[]{:S(2)}, u32[]{:S(2)}) collective-permute-start(f32[128,128]{1,0:T(8,128)S(1)} %broadcast_select_fusion.3), channel_id=1, source_target_pairs={{0,2},{2,0},{9,11},{11,9},{4,13},{13,4},{6,15},{15,6},{3,1},{1,3},... | collective-permute-start | bytes 196616 | tf_op jit(solution)/shard_map/ppermute | solution.py:75
  43.6 8.3 %collective-permute-start.7 = (f32[512,128]{1,0:T(8,128)S(1)}, f32[512,128]{1,0:T(8,128)S(1)}, u32[]{:S(2)}, u32[]{:S(2)}) collective-permute-start(f32[512,128]{1,0:T(8,128)S(1)} %slice.30), channel_id=1, source_target_pairs={{0,2},{2,0},{9,11},{11,9},{4,13},{13,4},{6,15},{15,6},{3,1},{1,3},... | collective-permute-start | bytes 786440 | tf_op jit(solution)/shard_map/ppermute | solution.py:75
  46.1 16.6 %collective-permute-start.16 = (f32[2,128,128]{2,1,0:T(8,128)S(1)}, f32[2,128,128]{2,1,0:T(8,128)S(1)}, u32[]{:S(2)}, u32[]{:S(2)}) collective-permute-start(f32[2,128,128]{2,1,0:T(8,128)S(1)} %pad_maximum_fusion.5.d_mine), channel_id=1, source_target_pairs={{0,16},{1,17},{2,18},{3,19},{4,20},{5,21},{6,22},{7,23},{8,24},{9,... | collective-permute-start | bytes 393224 | tf_op jit(solution)/shard_map/ppermute | solution.py:75
  52.0 26.3 %collective-permute-start.18 = (f32[2,512,128]{2,1,0:T(8,128)S(1)}, f32[2,512,128]{2,1,0:T(8,128)S(1)}, u32[]{:S(2)}, u32[]{:S(2)}) collective-permute-start(f32[2,512,128]{2,1,0:T(8,128)S(1)} %pad_maximum_fusion.3.p0), channel_id=1, source_target_pairs={{0,16},{1,17},{2,18},{3,19},{4,20},{5,21},{6,22},{7,23},{8,24},{9,... | collective-permute-start | bytes 1572872 | tf_op jit(solution)/shard_map/ppermute | solution.py:75
  56.5 14.6 %collective-permute-start.10 = (f32[2,512,128]{2,1,0:T(8,128)S(1)}, f32[2,512,128]{2,1,0:T(8,128)S(1)}, u32[]{:S(2)}, u32[]{:S(2)}) collective-permute-start(f32[2,512,128]{2,1,0:T(8,128)S(1)} %pad_maximum_fusion.3.p0), channel_id=1, source_target_pairs={{0,12},{1,13},{2,14},{3,15},{4,0},{5,1},{6,2},{7,3},{8,4},{9,5},{1... | collective-permute-start | bytes 1572872 | tf_op jit(solution)/shard_map/ppermute | solution.py:75
  58.8 14.8 %collective-permute-start.12 = (f32[2,512,128]{2,1,0:T(8,128)S(1)}, f32[2,512,128]{2,1,0:T(8,128)S(1)}, u32[]{:S(2)}, u32[]{:S(2)}) collective-permute-start(f32[2,512,128]{2,1,0:T(8,128)S(1)} %pad_maximum_fusion.3.p0), channel_id=1, source_target_pairs={{0,1},{1,2},{2,3},{3,0},{4,5},{5,6},{6,7},{7,4},{8,9},{9,10},{10,1... | collective-permute-start | bytes 1572872 | tf_op jit(solution)/shard_map/ppermute | solution.py:75
  62.7 14.1 %collective-permute-start.8 = (f32[2,512,128]{2,1,0:T(8,128)S(1)}, f32[2,512,128]{2,1,0:T(8,128)S(1)}, u32[]{:S(2)}, u32[]{:S(2)}) collective-permute-start(f32[2,512,128]{2,1,0:T(8,128)S(1)} %pad_maximum_fusion.3.p0), channel_id=1, source_target_pairs={{0,4},{1,5},{2,6},{3,7},{4,8},{5,9},{6,10},{7,11},{8,12},{9,13},{1... | collective-permute-start | bytes 1572872 | tf_op jit(solution)/shard_map/ppermute | solution.py:75
  71.1 14.0 %collective-permute-start.11 = (f32[2,512,128]{2,1,0:T(8,128)S(1)}, f32[2,512,128]{2,1,0:T(8,128)S(1)}, u32[]{:S(2)}, u32[]{:S(2)}) collective-permute-start(f32[2,512,128]{2,1,0:T(8,128)S(1)} %collective-permute-done.10.p1), channel_id=1, source_target_pairs={{0,16},{1,17},{2,18},{3,19},{4,20},{5,21},{6,22},{7,23},{8,24},{9,... | collective-permute-start | bytes 1572872 | tf_op jit(solution)/shard_map/ppermute | solution.py:75
  73.7 11.5 %collective-permute-start.13 = (f32[2,512,128]{2,1,0:T(8,128)S(1)}, f32[2,512,128]{2,1,0:T(8,128)S(1)}, u32[]{:S(2)}, u32[]{:S(2)}) collective-permute-start(f32[2,512,128]{2,1,0:T(8,128)S(1)} %collective-permute-done.12.p2), channel_id=1, source_target_pairs={{0,16},{1,17},{2,18},{3,19},{4,20},{5,21},{6,22},{7,23},{8,24},{9,... | collective-permute-start | bytes 1572872 | tf_op jit(solution)/shard_map/ppermute | solution.py:75
  76.8 8.4 %collective-permute-start.9 = (f32[2,512,128]{2,1,0:T(8,128)S(1)}, f32[2,512,128]{2,1,0:T(8,128)S(1)}, u32[]{:S(2)}, u32[]{:S(2)}) collective-permute-start(f32[2,512,128]{2,1,0:T(8,128)S(1)} %collective-permute-done.8.p0), channel_id=1, source_target_pairs={{0,16},{1,17},{2,18},{3,19},{4,20},{5,21},{6,22},{7,23},{8,24},{9,... | collective-permute-start | bytes 1572872 | tf_op jit(solution)/shard_map/ppermute | solution.py:75

commit v3 on v2

--- a/solution.py
+++ b/solution.py
@@ -48,7 +48,9 @@
     return (z + 2 * y) % 4
 
 
-SIDE = everywhere([((z, y), (z, 3 - y)) for z, y in ALL_ZY])
+UP = everywhere([((0, 0), (1, 0)), ((0, 1), (1, 1))], xs=(0,))
+DOWN = everywhere([((0, 0), (3, 0)), ((0, 1), (3, 1))], xs=(0,))
+SIDE = everywhere([((0, 0), (0, 3)), ((0, 1), (0, 2))], xs=(0,))
 ROW_SWAP = ROW_DOWN + [(b, a) for a, b in ROW_DOWN]
 
 
@@ -95,8 +97,10 @@
     return jnp.dot(lefts, rights, preferred_element_type=jnp.float32)
 
 
-def factor_kernel(info, d_mine, d_other, top, update_out, top_out, f):
-    core, panel, second = info[0], info[1], info[2]
+def factor_kernel(info, d_mine, d_other, top, update_out, top_out, f, sem):
+    core = info[0]
+    kind = jnp.where(info[1] == 0, 0, info[2] + 1)
+    sides = (slice(P_SIZE, P_SIZE + WIDTH), slice(0, WIDTH), slice(WIDTH, P_SIZE))
     for half in range(2):
         @pl.when(core == half)
         def _():
@@ -135,82 +139,97 @@
         lane = lax.broadcasted_iota(jnp.int32, lower.shape, 1) + base
         mine = (lane >= lo) & (lane < hi)
         f[hi:, base : base + WIDTH] = jnp.where(mine, lower, f[hi:, base : base + WIDTH])
-
-    def finish(update, done):
+        if block == P_SIZE // B - 2:
+            for case, side in enumerate(sides):
+                @pl.when(kind == case)
+                def _():
+                    pltpu.make_async_copy(f.at[0:P_SIZE, side], top_out, sem).start()
+
+    def finish(update):
         high = update.astype(jnp.bfloat16)
         low = (update - high.astype(jnp.float32)).astype(jnp.bfloat16)
         update_out[...] = jnp.concatenate([high, low], axis=1)
-        top_out[...] = done
-
-    @pl.when(panel == 0)
-    def _():
-        finish(f[P_SIZE:, P_SIZE:], f[0:P_SIZE, P_SIZE:])
-
-    for part in range(2):
-        @pl.when((panel == 1) & (second == part))
+
+    for case, side in enumerate(sides):
+        @pl.when(kind == case)
         def _():
-            side = slice(part * WIDTH, (part + 1) * WIDTH)
-            finish(f[P_SIZE:, side], f[0:P_SIZE, side])
+            finish(f[P_SIZE:, side])
+
+    pltpu.make_async_copy(f.at[0:P_SIZE, sides[0]], top_out, sem).wait()
 
 
 def factor(info, d_mine, d_other, top):
     vmem = pl.BlockSpec(memory_space=pltpu.VMEM)
     return pl.pallas_call(
         factor_kernel,
-        out_shape=(pltpu.VMEM((P_SIZE, 2 * WIDTH), jnp.bfloat16), pltpu.VMEM((P_SIZE, WIDTH), jnp.float32)),
+        out_shape=(pltpu.VMEM((P_SIZE, 2 * WIDTH), jnp.bfloat16), pltpu.HBM((P_SIZE, WIDTH), jnp.float32)),
         in_specs=[pl.BlockSpec(memory_space=pltpu.SMEM), vmem, vmem, vmem],
-        out_specs=(vmem, vmem),
-        scratch_shapes=[pltpu.VMEM((2 * P_SIZE, P_SIZE + WIDTH), jnp.float32)],
+        out_specs=(vmem, pl.BlockSpec(memory_space=pltpu.HBM)),
+        scratch_shapes=[pltpu.VMEM((2 * P_SIZE, P_SIZE + WIDTH), jnp.float32), pltpu.SemaphoreType.DMA],
         compiler_params=pltpu.CompilerParams(vmem_limit_bytes=4 << 20),
         cost_estimate=pl.CostEstimate(flops=9_000_000_000, bytes_accessed=2_000_000, transcendentals=0),
         name="factor",
     )(info, in_vmem(d_mine), in_vmem(d_other), in_vmem(top))
 
 
-def update_body(steps, places, info, front, parts, update, top, out):
-    step = pl.program_id(0)
-    for at in range(steps):
-        @pl.when(step == at)
+def update_kernel(info, front, *refs):
+    out, blocks, top_rows, loads, stores, top_sem = refs[-6:]
+    count = blocks.shape[0]
+    parts, update, top = refs[:count], refs[count], refs[count + 1]
+    top_load = pltpu.make_async_copy(top, top_rows, top_sem)
+    has_top = [(info[2 + at] == 0) & (info[1] == 0) for at in range(count)]
+
+    def load(at):
+        rows = pl.ds(pl.multiple_of(info[2 + at] * SHARE, SHARE), SHARE)
+        return pltpu.make_async_copy(front.at[rows, :], blocks.at[at], loads.at[at])
+
+    def store(at):
+        rows = pl.ds(pl.multiple_of(info[2 + at] * SHARE, SHARE), SHARE)
+        return pltpu.make_async_copy(blocks.at[at], out.at[rows, :], stores.at[at])
+
+    for at in range(count):
+        load(at).start()
+        pl.when(has_top[at])(top_load.start)
+    for at in range(count):
+        panel = jnp.concatenate([parts[at][0], parts[at][1]], axis=1)
+        high = panel.astype(jnp.bfloat16)
+        low = (panel - high.astype(jnp.float32)).astype(jnp.bfloat16)
+        both = jnp.dot(high, update[...], preferred_element_type=jnp.float32)
+        both = both + jnp.dot(low, update[...], preferred_element_type=jnp.float32)
+        added = both[:, :WIDTH] + both[:, WIDTH:]
+        load(at).wait()
+        blocks[at] = jnp.where(info[0] == 0, blocks[at], 0.0) + added
+
+        @pl.when(has_top[at])
         def _():
-            panel = jnp.concatenate([parts[at][0], parts[at][1]], axis=1)
-            high = panel.astype(jnp.bfloat16)
-            low = (panel - high.astype(jnp.float32)).astype(jnp.bfloat16)
-            both = jnp.dot(high, update[...], preferred_element_type=jnp.float32)
-            both = both + jnp.dot(low, update[...], preferred_element_type=jnp.float32)
-            out[...] = jnp.where(info[1] == 0, front[...], 0.0) + (both[:, :WIDTH] + both[:, WIDTH:])
-
-    @pl.when((places[step] == 0) & (info[3] == 0))
-    def _():
-        out[0:P_SIZE, :] = top[...]
-
-
-def first_update_kernel(places, info, front, p0, p1, update, top, out):
-    update_body(2, places, info, front, (p0, p1), update, top, out)
-
-
-def later_update_kernel(places, info, front, p0, p1, p2, update, top, _, out):
-    update_body(3, places, info, front, (p0, p1, p2), update, top, out)
-
-
-def apply_update(places, info, front, parts, update, top, done=None):
-    vmem = pl.BlockSpec(memory_space=pltpu.VMEM)
-    block = pl.BlockSpec((SHARE, WIDTH), lambda i, places, info: (places[i], 0))
-    more = [] if done is None else [pl.BlockSpec(memory_space=pl.ANY)]
-    extra = [] if done is None else [done]
+            top_load.wait()
+            blocks[at, 0:P_SIZE, :] = top_rows[...]
+
+        store(at).start()
+    for at in range(count):
+        store(at).wait()
+
+
+def apply_update(info, front, parts, update, top, done=None):
+    vmem, hbm = pl.BlockSpec(memory_space=pltpu.VMEM), pl.BlockSpec(memory_space=pltpu.HBM)
+    count = len(parts)
     front = pltpu.with_memory_space_constraint(front, pltpu.HBM)
     return pl.pallas_call(
-        first_update_kernel if done is None else later_update_kernel,
+        update_kernel,
         out_shape=jax.ShapeDtypeStruct((ROWS, WIDTH), jnp.float32),
-        grid_spec=pltpu.PrefetchScalarGridSpec(
-            num_scalar_prefetch=2,
-            grid=(len(parts),),
-            in_specs=[block] + [vmem] * (len(parts) + 2) + more,
-            out_specs=block,
-        ),
-        input_output_aliases={} if done is None else {8: 0},
+        in_specs=[pl.BlockSpec(memory_space=pltpu.SMEM), hbm] + [vmem] * (count + 1) + [hbm] * (1 + (done is not None)),
+        out_specs=hbm,
+        scratch_shapes=[
+            pltpu.VMEM((count, SHARE, WIDTH), jnp.float32),
+            pltpu.VMEM((P_SIZE, WIDTH), jnp.float32),
+            pltpu.SemaphoreType.DMA((count,)),
+            pltpu.SemaphoreType.DMA((count,)),
+            pltpu.SemaphoreType.DMA,
+        ],
+        input_output_aliases={} if done is None else {count + 4: 0},
         compiler_params=pltpu.CompilerParams(vmem_limit_bytes=4 << 20),
         cost_estimate=pl.CostEstimate(flops=3_000_000_000, bytes_accessed=4_000_000, transcendentals=0),
-    )(places, info, front, *map(in_vmem, parts), in_vmem(update), in_vmem(top), *extra)
+    )(info, front, *map(in_vmem, parts), in_vmem(update), pltpu.with_memory_space_constraint(top, pltpu.HBM), *([] if done is None else [done]))
 
 
 def per_device(front):
@@ -230,13 +249,13 @@
     given = jnp.concatenate([early[DPART:P_SIZE], rows(early, start(1) + ROWS // 2)])
     to_up = jnp.where(core == 0, kept, send(given, CORE_SWAP))
     beside = send(front, CORE_SWAP)
-    up = send(to_up, shift(1, 0))
+    up = send(to_up, UP)
 
     def share(delta):
         half = jnp.where(core == 0, rows(front, start(delta)), rows(beside, start(delta) + ROWS // 2))
         return jnp.concatenate([to_up[:DPART], half])
 
-    down = send(share(3), shift(-1, 0))
+    down = send(share(3), DOWN)
     side = send(share(2), SIDE)
     near = y < 2
     held = jnp.where((z == 1) & near, up, jnp.where((z == 3) & near, down, jnp.where(near, share(0), side)))
@@ -267,15 +286,16 @@
     order = [(mine + 3) % 4, (mine + 1) % 4, (mine + 2) % 4]
 
     def at(*blocks):
-        return jnp.stack(blocks).astype(jnp.int32)
-
-    out = apply_update(at(mine + 4 * core, mine + 4 * (1 - core)), info, front, (own, own_other), update, top_done)
+        return jnp.stack([panel.astype(jnp.int32), row, *blocks]).astype(jnp.int32)
+
+    places = at(mine + 4 * core, mine + 4 * (1 - core))
+    out = apply_update(places, front, (own, own_other), update, top_done)
     received = (before, after, far)
     others = tuple(send(v, CORE_SWAP) for v in received)
     places = at(*(p + 4 * core for p in order))
-    out = apply_update(places, info, front, received, update, top_done, out)
+    out = apply_update(places, front, received, update, top_done, out)
     places = at(*(p + 4 * (1 - core) for p in order))
-    return apply_update(places, info, front, others, update, top_done, out)
+    return apply_update(places, front, others, update, top_done, out)
 
 
 def solution(mesh):

time: 89.4 us -> 86.9 us (0.972)
  the two profiles are of different devices: /device:TPU:9 before, /device:TPU:0 now
where the time goes in v3:
time: 86.9 us; the launch traced here: 85.3 us
  waiting for transfers between devices  40.5 us (47%)
  starting transfers between devices  24.8 us (29%)
  Pallas kernels  14.9 us (17%)
  other arithmetic  2.59 us (3%)
  local copies, waits for them, and re-layouts  2.31 us (3%)
    ppermute x19, waiting for transfers between devices, send(): return lax.ppermute(value, AXES, pairs)  40.5 us
    ppermute x19, starting transfers between devices, send(): return lax.ppermute(value, AXES, pairs)  24.8 us
    pallas_call x3, Pallas kernels, apply_update(): pl.pallas_call(update_kernel, out_shape=jax.ShapeDtypeStruct((ROWS, WIDTH...  9.68 us
    pallas_call x1, Pallas kernels, factor(): pl.pallas_call(factor_kernel, out_shape=(pltpu.VMEM((P_SIZE, 2 * WIDTH),...  5.23 us
  transfers between devices with their start and end apart: 19, of which 12 were waited for; matrix products, arithmetic and copies ran while one was open for 6% of the time, Pallas kernels for 14%

profile of v3, /device:TPU:0, one launch (start us, length us, event | category | flops | bytes accessed | tf_op | source)
XLA Modules:
  0.0 85.3 jit_solution(5921232061173862649)
XLA Ops:
  0.0 1.2 %constant_dynamic-slice_fusion.1 = (f32[512,128]{1,0:T(8,128)S(1)}, f32[512,128]{1,0:T(8,128)S(1)}) fusion(f32[4096,128]{1,0:T(8,128)} %front.5, s32[]{:T(128)S(6)} %select_n.176, s32[]{:T(128)S(6)} %select_n.177), kind=kLoop, calls=%fused_computation.22 | loop fusion | bytes 1048584 | tf_op jit(solution)/shard_map/dynamic_slice | solution.py:245
  1.2 0.9 %fusion.3 = (f32[128,128]{1,0:T(8,128)S(1)}, f32[128,128]{1,0:T(8,128)S(1)}) fusion(f32[4096,128]{1,0:T(8,128)} %front.5), kind=kLoop, calls=%fused_computation.25 | loop fusion | bytes 262144 | tf_op jit(solution)/shard_map/slice | solution.py:248
  2.1 0.4 collective-permute-start
  2.6 2.3 %collective-permute-done = f32[640,128]{1,0:T(8,128)S(1)} collective-permute-done((f32[640,128]{1,0:T(8,128)S(1)}, f32[640,128]{1,0:T(8,128)S(1)}, u32[]{:S(2)}, u32[]{:S(2)}) %collective-permute-start) | collective-permute-done | bytes 327712 | tf_op jit(solution)/shard_map/ppermute | solution.py:77
  4.9 4.0 %collective-permute-start.1 = (f32[640,128]{1,0:T(8,128)S(1)}, f32[640,128]{1,0:T(8,128)S(1)}, u32[]{:S(2)}, u32[]{:S(2)}) collective-permute-start(f32[640,128]{1,0:T(8,128)S(1)} %maximum_select_fusion), channel_id=1, source_target_pairs={{0,4},{1,5},{16,20},{17,21},{64,68},{65,69},{80,84},{81,85}} | collective-permute-start | bytes 983048 | tf_op jit(solution)/shard_map/ppermute | solution.py:77
  8.9 1.2 %dynamic-slice_select_fusion.1 = (f32[512,128]{1,0:T(8,128)S(1)}, f32[512,128]{1,0:T(8,128)S(1)}, f32[512,128]{1,0:T(8,128)S(1)}) fusion(f32[4096,128]{1,0:T(8,128)} %collective-permute-done.2, s32[]{:T(128)S(6)} %select_n.187, f32[4096,128]{1,0:T(8,128)S(1)} %copy-done, s32[]{:T(128)S(6)} %select_n.186, pred[]{:T(512)S(6)} %eq.65, s32[]{:T(128)S(6)} %select_n.190, ...), kind=kLoop, calls=%fused_computation.12 | loop fusion | flops 196608 | bytes 2359321 | tf_op jit(solution)/shard_map/jit(_where)/select_n | solution.py:255
  10.1 0.9 %pad_maximum_fusion = (f32[640,128]{1,0:T(8,128)}, f32[640,128]{1,0:T(8,128)}) fusion(f32[128,128]{1,0:T(8,128)S(1)} %slice.29, f32[512,128]{1,0:T(8,128)S(1)} %get-tuple-element.10, f32[512,128]{1,0:T(8,128)S(1)} %get-tuple-element.11), kind=kLoop, calls=%fused_computation | loop fusion | flops 163840 | bytes 1245184 | tf_op jit(solution)/shard_map/concatenate | solution.py:256
  11.0 2.8 %collective-permute-start.3 = (f32[640,128]{1,0:T(8,128)}, f32[640,128]{1,0:T(8,128)S(1)}, u32[]{:S(2)}, u32[]{:S(2)}) collective-permute-start(f32[640,128]{1,0:T(8,128)} %get-tuple-element.21), channel_id=1, source_target_pairs={{0,12},{1,13},{16,28},{17,29},{64,76},{65,77},{80,92},{81,93}} | collective-permute-start | bytes 983048 | tf_op jit(solution)/shard_map/ppermute | solution.py:77
  13.8 2.0 %collective-permute-start.4 = (f32[640,128]{1,0:T(8,128)}, f32[640,128]{1,0:T(8,128)}, u32[]{:S(2)}, u32[]{:S(2)}) collective-permute-start(f32[640,128]{1,0:T(8,128)} %get-tuple-element.20), channel_id=1, source_target_pairs={{0,3},{1,2},{16,19},{17,18},{64,67},{65,66},{80,83},{81,82}} | collective-permute-start | bytes 983048 | tf_op jit(solution)/shard_map/ppermute | solution.py:77
  15.8 0.3 collective-permute-done.1
  16.1 5.2 %collective-permute-done.3 = f32[640,128]{1,0:T(8,128)S(1)} collective-permute-done((f32[640,128]{1,0:T(8,128)}, f32[640,128]{1,0:T(8,128)S(1)}, u32[]{:S(2)}, u32[]{:S(2)}) %collective-permute-start.3) | collective-permute-done | bytes 327712 | tf_op jit(solution)/shard_map/ppermute | solution.py:77
  21.3 1.3 %collective-permute-done.4 = f32[640,128]{1,0:T(8,128)} collective-permute-done((f32[640,128]{1,0:T(8,128)}, f32[640,128]{1,0:T(8,128)}, u32[]{:S(2)}, u32[]{:S(2)}) %collective-permute-start.4) | collective-permute-done | bytes 327712 | tf_op jit(solution)/shard_map/ppermute | solution.py:77
  22.7 0.1 collective-permute-start.5
  22.8 8.9 %collective-permute-done.5 = f32[640,128]{1,0:T(8,128)S(1)} collective-permute-done((f32[640,128]{1,0:T(8,128)S(1)}, f32[640,128]{1,0:T(8,128)S(1)}, u32[]{:S(2)}, u32[]{:S(2)}) %collective-permute-start.5) | collective-permute-done | bytes 327712 | tf_op jit(solution)/shard_map/ppermute | solution.py:77
  31.8 1.3 %collective-permute-start.6 = (f32[640,128]{1,0:T(8,128)S(1)}, f32[640,128]{1,0:T(8,128)S(1)}, u32[]{:S(2)}, u32[]{:S(2)}) collective-permute-start(f32[640,128]{1,0:T(8,128)S(1)} %broadcast_select_fusion), channel_id=1, source_target_pairs={{0,9},{2,11},{4,6},{13,15},{3,10},{1,8},{12,14},{5,7},{16,25},{18,... | collective-permute-start | bytes 983048 | tf_op jit(solution)/shard_map/ppermute | solution.py:77
  33.1 3.1 %collective-permute-start.17 = (f32[256,128]{1,0:T(8,128)S(1)}, f32[256,128]{1,0:T(8,128)S(1)}, u32[]{:S(2)}, u32[]{:S(2)}) collective-permute-start(f32[256,128]{1,0:T(8,128)S(1)} %slice.26), channel_id=1, source_target_pairs={{0,64},{1,65},{2,66},{3,67},{4,68},{5,69},{6,70},{7,71},{8,72},{9,... | collective-permute-start | bytes 393224 | tf_op jit(solution)/shard_map/ppermute | solution.py:77
  36.4 2.4 %collective-permute-done.6 = f32[640,128]{1,0:T(8,128)S(1)} collective-permute-done((f32[640,128]{1,0:T(8,128)S(1)}, f32[640,128]{1,0:T(8,128)S(1)}, u32[]{:S(2)}, u32[]{:S(2)}) %collective-permute-start.6) | collective-permute-done | bytes 327712 | tf_op jit(solution)/shard_map/ppermute | solution.py:77
  38.9 3.1 %collective-permute-start.14 = (f32[128,128]{1,0:T(8,128)S(1)}, f32[128,128]{1,0:T(8,128)S(1)}, u32[]{:S(2)}, u32[]{:S(2)}) collective-permute-start(f32[128,128]{1,0:T(8,128)S(1)} %slice.31), channel_id=1, source_target_pairs={{0,64},{1,65},{2,66},{3,67},{4,68},{5,69},{6,70},{7,71},{8,72},{9,... | collective-permute-start | bytes 196616 | tf_op jit(solution)/shard_map/ppermute | solution.py:77
  42.1 2.7 %collective-permute-done.14 = f32[128,128]{1,0:T(8,128)S(1)} collective-permute-done((f32[128,128]{1,0:T(8,128)S(1)}, f32[128,128]{1,0:T(8,128)S(1)}, u32[]{:S(2)}, u32[]{:S(2)}) %collective-permute-start.14) | collective-permute-done | bytes 65568 | tf_op jit(solution)/shard_map/ppermute | solution.py:77
  44.8 5.1 %collective-permute-start.15 = (f32[128,128]{1,0:T(8,128)S(1)}, f32[128,128]{1,0:T(8,128)S(1)}, u32[]{:S(2)}, u32[]{:S(2)}) collective-permute-start(f32[128,128]{1,0:T(8,128)S(1)} %broadcast_select_fusion.3), channel_id=1, source_target_pairs={{0,2},{2,0},{9,11},{11,9},{4,13},{13,4},{6,15},{15,6},{3,1},{1,3},... | collective-permute-start | bytes 196616 | tf_op jit(solution)/shard_map/ppermute | solution.py:77
  50.0 0.1 collective-permute-start.7
  50.1 2.8 %collective-permute-done.15 = f32[128,128]{1,0:T(8,128)S(1)} collective-permute-done((f32[128,128]{1,0:T(8,128)S(1)}, f32[128,128]{1,0:T(8,128)S(1)}, u32[]{:S(2)}, u32[]{:S(2)}) %collective-permute-start.15) | collective-permute-done | bytes 65568 | tf_op jit(solution)/shard_map/ppermute | solution.py:77
  53.0 4.9 %collective-permute-done.7 = f32[512,128]{1,0:T(8,128)S(1)} collective-permute-done((f32[512,128]{1,0:T(8,128)S(1)}, f32[512,128]{1,0:T(8,128)S(1)}, u32[]{:S(2)}, u32[]{:S(2)}) %collective-permute-start.7) | collective-permute-done | bytes 262176 | tf_op jit(solution)/shard_map/ppermute | solution.py:77
  58.2 0.5 collective-permute-start.12
  58.7 1.9 %collective-permute-start.8 = (f32[2,512,128]{2,1,0:T(8,128)S(1)}, f32[2,512,128]{2,1,0:T(8,128)S(1)}, u32[]{:S(2)}, u32[]{:S(2)}) collective-permute-start(f32[2,512,128]{2,1,0:T(8,128)S(1)} %pad_maximum_fusion.3.refs_0_), channel_id=1, source_target_pairs={{0,4},{1,5},{2,6},{3,7},{4,8},{5,9},{6,10},{7,11},{8,12},{9,13},{1... | collective-permute-start | bytes 1572872 | tf_op jit(solution)/shard_map/ppermute | solution.py:77
  60.7 5.2 %factor.1 = (bf16[256,256]{1,0:T(8,128)(2,1)S(1)}, f32[256,128]{1,0:T(8,128)}) custom-call(s32[4]{0:T(128)S(1)} %pad_add_fusion.info, f32[2,128,128]{2,1,0:T(8,128)S(1)} %pad_maximum_fusion.5.d_mine, f32[2,128,128]{2,1,0:T(8,128)S(1)} %collective-permute-done.16.d_other, f32[256,128]{1,0:T(8,128)S(1)} %broadcast_select_fusion.2.top), custom_call_target="tpu_custom_call" | custom-call | flops 8999999488 | bytes 2000000 | tf_op jit(solution)/shard_map/factor/pallas_call | solution.py:163
  65.9 6.5 %collective-permute-done.10.refs_1_ = f32[2,512,128]{2,1,0:T(8,128)S(1)} collective-permute-done((f32[2,512,128]{2,1,0:T(8,128)S(1)}, f32[2,512,128]{2,1,0:T(8,128)S(1)}, u32[]{:S(2)}, u32[]{:S(2)}) %collective-permute-start.10) | collective-permute-done | bytes 524320 | tf_op jit(solution)/shard_map/ppermute | solution.py:77
  72.4 1.4 %collective-permute-done.12.refs_2_ = f32[2,512,128]{2,1,0:T(8,128)S(1)} collective-permute-done((f32[2,512,128]{2,1,0:T(8,128)S(1)}, f32[2,512,128]{2,1,0:T(8,128)S(1)}, u32[]{:S(2)}, u32[]{:S(2)}) %collective-permute-start.12) | collective-permute-done | bytes 524320 | tf_op jit(solution)/shard_map/ppermute | solution.py:77
  73.8 1.7 %collective-permute-done.8.refs_0_ = f32[2,512,128]{2,1,0:T(8,128)S(1)} collective-permute-done((f32[2,512,128]{2,1,0:T(8,128)S(1)}, f32[2,512,128]{2,1,0:T(8,128)S(1)}, u32[]{:S(2)}, u32[]{:S(2)}) %collective-permute-start.8) | collective-permute-done | bytes 524320 | tf_op jit(solution)/shard_map/ppermute | solution.py:77
  75.6 3.0 %shard_map.17.refs_5_ = f32[4096,128]{1,0:T(8,128)} custom-call(s32[4]{0:T(128)S(1)} %pad_add_fusion.1.info, f32[4096,128]{1,0:T(8,128)} %front.5, f32[2,512,128]{2,1,0:T(8,128)S(1)} %pad_maximum_fusion.3.refs_0_, f32[2,512,128]{2,1,0:T(8,128)S(1)} %collective-permute-done.18.refs_1_, bf16[256,256]{1,0:T(8,128)(2,1)S(1)} %get-tuple-element.7.refs_2_.refs_3_, ...), custom_call_target="tpu_custom_call" | custom-call | flops 3000000000 | bytes 4000000 | tf_op jit(solution)/shard_map/pallas_call | solution.py:217
  78.5 3.4 %shard_map.18.refs_5_ = f32[4096,128]{1,0:T(8,128)} custom-call(s32[5]{0:T(128)S(1)} %stack.94.info, f32[4096,128]{1,0:T(8,128)} %front.5, f32[2,512,128]{2,1,0:T(8,128)S(1)} %collective-permute-done.8.refs_0_, f32[2,512,128]{2,1,0:T(8,128)S(1)} %collective-permute-done.10.refs_1_, ...), custom_call_target="tpu_custom_call", output_to_operand_aliasing={{}: (7, {})} | custom-call | flops 3000000000 | bytes 4000000 | tf_op jit(solution)/shard_map/pallas_call | solution.py:217
  81.9 3.4 %shard_map.19 = f32[4096,128]{1,0:T(8,128)} custom-call(s32[5]{0:T(128)S(1)} %stack.81.info, f32[4096,128]{1,0:T(8,128)} %front.5, f32[2,512,128]{2,1,0:T(8,128)S(1)} %collective-permute-done.9.refs_0_, f32[2,512,128]{2,1,0:T(8,128)S(1)} %collective-permute-done.11.refs_1_, ...), custom_call_target="tpu_custom_call", output_to_operand_aliasing={{}: (7, {})} | custom-call | flops 3000000000 | bytes 4000000 | tf_op jit(solution)/shard_map/pallas_call | solution.py:217
  (35 shorter events, 1.0 us)
Async XLA Ops:
  0.0 8.9 %copy-start = (f32[4096,128]{1,0:T(8,128)S(1)}, f32[4096,128]{1,0:T(8,128)}, u32[]{:S(2)}) copy-start(f32[4096,128]{1,0:T(8,128)} %front.5) | copy-start | bytes 6291460
  0.0 8.9 %collective-permute-start.2 = (f32[4096,128]{1,0:T(8,128)}, f32[4096,128]{1,0:T(8,128)}, u32[]{:S(2)}, u32[]{:S(2)}) collective-permute-start(f32[4096,128]{1,0:T(8,128)} %front.5), channel_id=1, source_target_pairs={{0,16},{1,17},{2,18},{3,19},{4,20},{5,21},{6,22},{7,23},{8,24},{9,... | collective-permute-start | bytes 6291464 | tf_op jit(solution)/shard_map/ppermute | solution.py:77
  2.1 2.7 %collective-permute-start = (f32[640,128]{1,0:T(8,128)S(1)}, f32[640,128]{1,0:T(8,128)S(1)}, u32[]{:S(2)}, u32[]{:S(2)}) collective-permute-start(f32[640,128]{1,0:T(8,128)S(1)} %pad_maximum_fusion.4), channel_id=1, source_target_pairs={{0,16},{1,17},{2,18},{3,19},{4,20},{5,21},{6,22},{7,23},{8,24},{9,... | collective-permute-start | bytes 983048 | tf_op jit(solution)/shard_map/ppermute | solution.py:77
  4.9 11.2 %collective-permute-start.1 = (f32[640,128]{1,0:T(8,128)S(1)}, f32[640,128]{1,0:T(8,128)S(1)}, u32[]{:S(2)}, u32[]{:S(2)}) collective-permute-start(f32[640,128]{1,0:T(8,128)S(1)} %maximum_select_fusion), channel_id=1, source_target_pairs={{0,4},{1,5},{16,20},{17,21},{64,68},{65,69},{80,84},{81,85}} | collective-permute-start | bytes 983048 | tf_op jit(solution)/shard_map/ppermute | solution.py:77
  11.0 10.3 %collective-permute-start.3 = (f32[640,128]{1,0:T(8,128)}, f32[640,128]{1,0:T(8,128)S(1)}, u32[]{:S(2)}, u32[]{:S(2)}) collective-permute-start(f32[640,128]{1,0:T(8,128)} %get-tuple-element.21), channel_id=1, source_target_pairs={{0,12},{1,13},{16,28},{17,29},{64,76},{65,77},{80,92},{81,93}} | collective-permute-start | bytes 983048 | tf_op jit(solution)/shard_map/ppermute | solution.py:77
  13.8 8.9 %collective-permute-start.4 = (f32[640,128]{1,0:T(8,128)}, f32[640,128]{1,0:T(8,128)}, u32[]{:S(2)}, u32[]{:S(2)}) collective-permute-start(f32[640,128]{1,0:T(8,128)} %get-tuple-element.20), channel_id=1, source_target_pairs={{0,3},{1,2},{16,19},{17,18},{64,67},{65,66},{80,83},{81,82}} | collective-permute-start | bytes 983048 | tf_op jit(solution)/shard_map/ppermute | solution.py:77
  22.7 9.0 %collective-permute-start.5 = (f32[640,128]{1,0:T(8,128)S(1)}, f32[640,128]{1,0:T(8,128)S(1)}, u32[]{:S(2)}, u32[]{:S(2)}) collective-permute-start(f32[640,128]{1,0:T(8,128)S(1)} %fusion.2), channel_id=1, source_target_pairs={{0,32},{1,33},{2,34},{3,35},{4,36},{5,37},{6,38},{7,39},{8,40},{9,... | collective-permute-start | bytes 983048 | tf_op jit(solution)/shard_map/ppermute | solution.py:77
  31.8 7.1 %collective-permute-start.6 = (f32[640,128]{1,0:T(8,128)S(1)}, f32[640,128]{1,0:T(8,128)S(1)}, u32[]{:S(2)}, u32[]{:S(2)}) collective-permute-start(f32[640,128]{1,0:T(8,128)S(1)} %broadcast_select_fusion), channel_id=1, source_target_pairs={{0,9},{2,11},{4,6},{13,15},{3,10},{1,8},{12,14},{5,7},{16,25},{18,... | collective-permute-start | bytes 983048 | tf_op jit(solution)/shard_map/ppermute | solution.py:77
  33.1 16.8 %collective-permute-start.17 = (f32[256,128]{1,0:T(8,128)S(1)}, f32[256,128]{1,0:T(8,128)S(1)}, u32[]{:S(2)}, u32[]{:S(2)}) collective-permute-start(f32[256,128]{1,0:T(8,128)S(1)} %slice.26), channel_id=1, source_target_pairs={{0,64},{1,65},{2,66},{3,67},{4,68},{5,69},{6,70},{7,71},{8,72},{9,... | collective-permute-start | bytes 393224 | tf_op jit(solution)/shard_map/ppermute | solution.py:77
  38.9 5.8 %collective-permute-start.14 = (f32[128,128]{1,0:T(8,128)S(1)}, f32[128,128]{1,0:T(8,128)S(1)}, u32[]{:S(2)}, u32[]{:S(2)}) collective-permute-start(f32[128,128]{1,0:T(8,128)S(1)} %slice.31), channel_id=1, source_target_pairs={{0,64},{1,65},{2,66},{3,67},{4,68},{5,69},{6,70},{7,71},{8,72},{9,... | collective-permute-start | bytes 196616 | tf_op jit(solution)/shard_map/ppermute | solution.py:77
  44.8 8.1 %collective-permute-start.15 = (f32[128,128]{1,0:T(8,128)S(1)}, f32[128,128]{1,0:T(8,128)S(1)}, u32[]{:S(2)}, u32[]{:S(2)}) collective-permute-start(f32[128,128]{1,0:T(8,128)S(1)} %broadcast_select_fusion.3), channel_id=1, source_target_pairs={{0,2},{2,0},{9,11},{11,9},{4,13},{13,4},{6,15},{15,6},{3,1},{1,3},... | collective-permute-start | bytes 196616 | tf_op jit(solution)/shard_map/ppermute | solution.py:77
  50.0 8.0 %collective-permute-start.7 = (f32[512,128]{1,0:T(8,128)S(1)}, f32[512,128]{1,0:T(8,128)S(1)}, u32[]{:S(2)}, u32[]{:S(2)}) collective-permute-start(f32[512,128]{1,0:T(8,128)S(1)} %slice.30), channel_id=1, source_target_pairs={{0,2},{2,0},{9,11},{11,9},{4,13},{13,4},{6,15},{15,6},{3,1},{1,3},... | collective-permute-start | bytes 786440 | tf_op jit(solution)/shard_map/ppermute | solution.py:77
  52.9 7.8 %collective-permute-start.16 = (f32[2,128,128]{2,1,0:T(8,128)S(1)}, f32[2,128,128]{2,1,0:T(8,128)S(1)}, u32[]{:S(2)}, u32[]{:S(2)}) collective-permute-start(f32[2,128,128]{2,1,0:T(8,128)S(1)} %pad_maximum_fusion.5.d_mine), channel_id=1, source_target_pairs={{0,16},{1,17},{2,18},{3,19},{4,20},{5,21},{6,22},{7,23},{8,24},{9,... | collective-permute-start | bytes 393224 | tf_op jit(solution)/shard_map/ppermute | solution.py:77
  58.0 17.5 %collective-permute-start.18 = (f32[2,512,128]{2,1,0:T(8,128)S(1)}, f32[2,512,128]{2,1,0:T(8,128)S(1)}, u32[]{:S(2)}, u32[]{:S(2)}) collective-permute-start(f32[2,512,128]{2,1,0:T(8,128)S(1)} %pad_maximum_fusion.3.refs_0_), channel_id=1, source_target_pairs={{0,16},{1,17},{2,18},{3,19},{4,20},{5,21},{6,22},{7,23},{8,24},{9,... | collective-permute-start | bytes 1572872 | tf_op jit(solution)/shard_map/ppermute | solution.py:77
  58.1 14.3 %collective-permute-start.10 = (f32[2,512,128]{2,1,0:T(8,128)S(1)}, f32[2,512,128]{2,1,0:T(8,128)S(1)}, u32[]{:S(2)}, u32[]{:S(2)}) collective-permute-start(f32[2,512,128]{2,1,0:T(8,128)S(1)} %pad_maximum_fusion.3.refs_0_), channel_id=1, source_target_pairs={{0,12},{1,13},{2,14},{3,15},{4,0},{5,1},{6,2},{7,3},{8,4},{9,5},{1... | collective-permute-start | bytes 1572872 | tf_op jit(solution)/shard_map/ppermute | solution.py:77
  58.2 15.6 %collective-permute-start.12 = (f32[2,512,128]{2,1,0:T(8,128)S(1)}, f32[2,512,128]{2,1,0:T(8,128)S(1)}, u32[]{:S(2)}, u32[]{:S(2)}) collective-permute-start(f32[2,512,128]{2,1,0:T(8,128)S(1)} %pad_maximum_fusion.3.refs_0_), channel_id=1, source_target_pairs={{0,1},{1,2},{2,3},{3,0},{4,5},{5,6},{6,7},{7,4},{8,9},{9,10},{10,1... | collective-permute-start | bytes 1572872 | tf_op jit(solution)/shard_map/ppermute | solution.py:77
  58.7 16.8 %collective-permute-start.8 = (f32[2,512,128]{2,1,0:T(8,128)S(1)}, f32[2,512,128]{2,1,0:T(8,128)S(1)}, u32[]{:S(2)}, u32[]{:S(2)}) collective-permute-start(f32[2,512,128]{2,1,0:T(8,128)S(1)} %pad_maximum_fusion.3.refs_0_), channel_id=1, source_target_pairs={{0,4},{1,5},{2,6},{3,7},{4,8},{5,9},{6,10},{7,11},{8,12},{9,13},{1... | collective-permute-start | bytes 1572872 | tf_op jit(solution)/shard_map/ppermute | solution.py:77
  72.4 9.4 %collective-permute-start.11 = (f32[2,512,128]{2,1,0:T(8,128)S(1)}, f32[2,512,128]{2,1,0:T(8,128)S(1)}, u32[]{:S(2)}, u32[]{:S(2)}) collective-permute-start(f32[2,512,128]{2,1,0:T(8,128)S(1)} %collective-permute-done.10.refs_1_), channel_id=1, source_target_pairs={{0,16},{1,17},{2,18},{3,19},{4,20},{5,21},{6,22},{7,23},{8,24},{9,... | collective-permute-start | bytes 1572872 | tf_op jit(solution)/shard_map/ppermute | solution.py:77
  73.8 8.1 %collective-permute-start.13 = (f32[2,512,128]{2,1,0:T(8,128)S(1)}, f32[2,512,128]{2,1,0:T(8,128)S(1)}, u32[]{:S(2)}, u32[]{:S(2)}) collective-permute-start(f32[2,512,128]{2,1,0:T(8,128)S(1)} %collective-permute-done.12.refs_2_), channel_id=1, source_target_pairs={{0,16},{1,17},{2,18},{3,19},{4,20},{5,21},{6,22},{7,23},{8,24},{9,... | collective-permute-start | bytes 1572872 | tf_op jit(solution)/shard_map/ppermute | solution.py:77
  75.6 6.4 %collective-permute-start.9 = (f32[2,512,128]{2,1,0:T(8,128)S(1)}, f32[2,512,128]{2,1,0:T(8,128)S(1)}, u32[]{:S(2)}, u32[]{:S(2)}) collective-permute-start(f32[2,512,128]{2,1,0:T(8,128)S(1)} %collective-permute-done.8.refs_0_), channel_id=1, source_target_pairs={{0,16},{1,17},{2,18},{3,19},{4,20},{5,21},{6,22},{7,23},{8,24},{9,... | collective-permute-start | bytes 1572872 | tf_op jit(solution)/shard_map/ppermute | solution.py:77

commit v4 on v3

--- a/solution.py
+++ b/solution.py
@@ -48,9 +48,7 @@
     return (z + 2 * y) % 4
 
 
-UP = everywhere([((0, 0), (1, 0)), ((0, 1), (1, 1))], xs=(0,))
-DOWN = everywhere([((0, 0), (3, 0)), ((0, 1), (3, 1))], xs=(0,))
-SIDE = everywhere([((0, 0), (0, 3)), ((0, 1), (0, 2))], xs=(0,))
+SIDE = everywhere([((z, y), (z, 3 - y)) for z, y in ALL_ZY])
 ROW_SWAP = ROW_DOWN + [(b, a) for a, b in ROW_DOWN]
 
 
@@ -244,18 +242,15 @@
     def rows(array, at, size=SHARE):
         return lax.dynamic_slice(array, (at, 0), (size, WIDTH))
 
-    early = lax.optimization_barrier(front)
-    kept = jnp.concatenate([early[:DPART], rows(early, start(1))])
-    given = jnp.concatenate([early[DPART:P_SIZE], rows(early, start(1) + ROWS // 2)])
-    to_up = jnp.where(core == 0, kept, send(given, CORE_SWAP))
     beside = send(front, CORE_SWAP)
-    up = send(to_up, UP)
+    d_start = jnp.where(core == 0, front[:DPART], beside[DPART:P_SIZE])
 
     def share(delta):
         half = jnp.where(core == 0, rows(front, start(delta)), rows(beside, start(delta) + ROWS // 2))
-        return jnp.concatenate([to_up[:DPART], half])
-
-    down = send(share(3), DOWN)
+        return jnp.concatenate([d_start, half])
+
+    up = send(share(1), shift(1, 0))
+    down = send(share(3), shift(-1, 0))
     side = send(share(2), SIDE)
     near = y < 2
     held = jnp.where((z == 1) & near, up, jnp.where((z == 3) & near, down, jnp.where(near, share(0), side)))

time: 86.9 us -> 86.6 us (level)
  the two profiles are of different devices: /device:TPU:0 before, /device:TPU:9 now
where the time goes in v4:
time: 86.6 us; the launch traced here: 86.3 us
  starting transfers between devices  37.5 us (43%)
  waiting for transfers between devices  29.1 us (34%)
  Pallas kernels  14.8 us (17%)
  other arithmetic  3.55 us (4%)
  local copies, waits for them, and re-layouts  1.11 us (1%)
    ppermute x18, starting transfers between devices, send(): return lax.ppermute(value, AXES, pairs)  37.5 us
    ppermute x18, waiting for transfers between devices, send(): return lax.ppermute(value, AXES, pairs)  29.1 us
    pallas_call x3, Pallas kernels, apply_update(): pl.pallas_call(update_kernel, out_shape=jax.ShapeDtypeStruct((ROWS, WIDTH...  9.59 us
    pallas_call x1, Pallas kernels, factor(): pl.pallas_call(factor_kernel, out_shape=(pltpu.VMEM((P_SIZE, 2 * WIDTH),...  5.23 us
  transfers between devices with their start and end apart: 18, of which 8 were waited for; matrix products, arithmetic and copies ran while one was open for 3% of the time, Pallas kernels for 13%

profile of v4, /device:TPU:9, one launch (start us, length us, event | category | flops | bytes accessed | tf_op | source)
XLA Modules:
  0.0 86.3 jit_solution(10191560096472805676)
XLA Ops:
  0.0 0.7 collective-permute-start
  0.7 4.0 %collective-permute-done = f32[4096,128]{1,0:T(8,128)S(1)} collective-permute-done((f32[4096,128]{1,0:T(8,128)}, f32[4096,128]{1,0:T(8,128)S(1)}, u32[]{:S(2)}, u32[]{:S(2)}) %collective-permute-start) | collective-permute-done | bytes 2097184 | tf_op jit(solution)/shard_map/ppermute | solution.py:75
  4.7 0.8 slice_select_fusion
  5.5 1.3 %dynamic-slice_select_fusion.1 = (f32[512,128]{1,0:T(8,128)S(1)}, f32[512,128]{1,0:T(8,128)S(1)}, f32[512,128]{1,0:T(8,128)S(1)}, f32[512,128]{1,0:T(8,128)S(1)}) fusion(f32[4096,128]{1,0:T(8,128)S(1)} %collective-permute-done, s32[]{:T(128)S(6)} %select_n.192, f32[4096,128]{1,0:T(8,128)} %front.5, s32[]{:T(128)S(6)} %select_n.191, pred[]{:T(512)S(6)} %eq.66, ...), kind=kLoop, calls=%fused_computation.11 | loop fusion | flops 262144 | bytes 3145761 | tf_op jit(solution)/shard_map/jit(_where)/select_n | solution.py:249
  6.9 1.7 %collective-permute-start.1 = (f32[640,128]{1,0:T(8,128)S(1)}, f32[640,128]{1,0:T(8,128)S(1)}, u32[]{:S(2)}, u32[]{:S(2)}) collective-permute-start(f32[640,128]{1,0:T(8,128)S(1)} %get-tuple-element.19), channel_id=1, source_target_pairs={{0,4},{1,5},{2,6},{3,7},{4,8},{5,9},{6,10},{7,11},{8,12},{9,13},{1... | collective-permute-start | bytes 983048 | tf_op jit(solution)/shard_map/ppermute | solution.py:75
  8.6 2.2 %collective-permute-start.2 = (f32[640,128]{1,0:T(8,128)S(1)}, f32[640,128]{1,0:T(8,128)S(1)}, u32[]{:S(2)}, u32[]{:S(2)}) collective-permute-start(f32[640,128]{1,0:T(8,128)S(1)} %get-tuple-element.18), channel_id=1, source_target_pairs={{0,12},{1,13},{2,14},{3,15},{4,0},{5,1},{6,2},{7,3},{8,4},{9,5},{1... | collective-permute-start | bytes 983048 | tf_op jit(solution)/shard_map/ppermute | solution.py:75
  10.8 1.3 %collective-permute-start.3 = (f32[640,128]{1,0:T(8,128)S(1)}, f32[640,128]{1,0:T(8,128)S(1)}, u32[]{:S(2)}, u32[]{:S(2)}) collective-permute-start(f32[640,128]{1,0:T(8,128)S(1)} %get-tuple-element.17), channel_id=1, source_target_pairs={{0,3},{1,2},{2,1},{3,0},{4,7},{5,6},{6,5},{7,4},{8,11},{9,10},{10,... | collective-permute-start | bytes 983048 | tf_op jit(solution)/shard_map/ppermute | solution.py:75
  12.1 6.3 %collective-permute-done.1 = f32[640,128]{1,0:T(8,128)S(1)} collective-permute-done((f32[640,128]{1,0:T(8,128)S(1)}, f32[640,128]{1,0:T(8,128)S(1)}, u32[]{:S(2)}, u32[]{:S(2)}) %collective-permute-start.1) | collective-permute-done | bytes 327712 | tf_op jit(solution)/shard_map/ppermute | solution.py:75
  18.5 1.0 %collective-permute-done.3 = f32[640,128]{1,0:T(8,128)S(1)} collective-permute-done((f32[640,128]{1,0:T(8,128)S(1)}, f32[640,128]{1,0:T(8,128)S(1)}, u32[]{:S(2)}, u32[]{:S(2)}) %collective-permute-start.3) | collective-permute-done | bytes 327712 | tf_op jit(solution)/shard_map/ppermute | solution.py:75
  19.5 1.3 %collective-permute-start.4 = (f32[640,128]{1,0:T(8,128)S(1)}, f32[640,128]{1,0:T(8,128)S(1)}, u32[]{:S(2)}, u32[]{:S(2)}) collective-permute-start(f32[640,128]{1,0:T(8,128)S(1)} %fusion.2), channel_id=1, source_target_pairs={{0,32},{1,33},{2,34},{3,35},{4,36},{5,37},{6,38},{7,39},{8,40},{9,... | collective-permute-start | bytes 983048 | tf_op jit(solution)/shard_map/ppermute | solution.py:75
  20.8 6.5 %collective-permute-done.4 = f32[640,128]{1,0:T(8,128)S(1)} collective-permute-done((f32[640,128]{1,0:T(8,128)S(1)}, f32[640,128]{1,0:T(8,128)S(1)}, u32[]{:S(2)}, u32[]{:S(2)}) %collective-permute-start.4) | collective-permute-done | bytes 327712 | tf_op jit(solution)/shard_map/ppermute | solution.py:75
  27.4 3.9 %collective-permute-start.5 = (f32[640,128]{1,0:T(8,128)S(1)}, f32[640,128]{1,0:T(8,128)S(1)}, u32[]{:S(2)}, u32[]{:S(2)}) collective-permute-start(f32[640,128]{1,0:T(8,128)S(1)} %broadcast_select_fusion), channel_id=1, source_target_pairs={{0,9},{2,11},{4,6},{13,15},{3,10},{1,8},{12,14},{5,7},{16,25},{18,... | collective-permute-start | bytes 983048 | tf_op jit(solution)/shard_map/ppermute | solution.py:75
  31.2 0.9 %slice.20 = f32[256,128]{1,0:T(8,128)S(1)} slice(f32[4096,128]{1,0:T(8,128)} %front.5), slice={[0:256], [0:128]} | slice | bytes 262144 | tf_op jit(solution)/shard_map/slice | solution.py:262
  32.2 2.8 %collective-permute-start.16 = (f32[256,128]{1,0:T(8,128)S(1)}, f32[256,128]{1,0:T(8,128)S(1)}, u32[]{:S(2)}, u32[]{:S(2)}) collective-permute-start(f32[256,128]{1,0:T(8,128)S(1)} %slice.20), channel_id=1, source_target_pairs={{0,64},{1,65},{2,66},{3,67},{4,68},{5,69},{6,70},{7,71},{8,72},{9,... | collective-permute-start | bytes 393224 | tf_op jit(solution)/shard_map/ppermute | solution.py:75
  35.2 0.5 collective-permute-done.5
  35.7 2.8 %collective-permute-start.13 = (f32[128,128]{1,0:T(8,128)S(1)}, f32[128,128]{1,0:T(8,128)S(1)}, u32[]{:S(2)}, u32[]{:S(2)}) collective-permute-start(f32[128,128]{1,0:T(8,128)S(1)} %slice.23), channel_id=1, source_target_pairs={{0,64},{1,65},{2,66},{3,67},{4,68},{5,69},{6,70},{7,71},{8,72},{9,... | collective-permute-start | bytes 196616 | tf_op jit(solution)/shard_map/ppermute | solution.py:75
  38.6 2.8 %collective-permute-done.13 = f32[128,128]{1,0:T(8,128)S(1)} collective-permute-done((f32[128,128]{1,0:T(8,128)S(1)}, f32[128,128]{1,0:T(8,128)S(1)}, u32[]{:S(2)}, u32[]{:S(2)}) %collective-permute-start.13) | collective-permute-done | bytes 65568 | tf_op jit(solution)/shard_map/ppermute | solution.py:75
  41.5 1.4 %collective-permute-start.14 = (f32[128,128]{1,0:T(8,128)S(1)}, f32[128,128]{1,0:T(8,128)S(1)}, u32[]{:S(2)}, u32[]{:S(2)}) collective-permute-start(f32[128,128]{1,0:T(8,128)S(1)} %broadcast_select_fusion.3), channel_id=1, source_target_pairs={{0,2},{2,0},{9,11},{11,9},{4,13},{13,4},{6,15},{15,6},{3,1},{1,3},... | collective-permute-start | bytes 196616 | tf_op jit(solution)/shard_map/ppermute | solution.py:75
  42.9 0.9 %broadcast_select_fusion.2.top = f32[256,128]{1,0:T(8,128)S(1)} fusion(f32[256,128]{1,0:T(8,128)S(1)} %collective-permute-done.16, pred[]{:T(512)S(6)} %eq.75, f32[4096,128]{1,0:T(8,128)} %front.5), kind=kLoop, calls=%fused_computation.20 | loop fusion | flops 32768 | bytes 393217 | tf_op jit(solution)/shard_map/jit(_where)/select_n | solution.py:262
  43.8 1.7 %collective-permute-start.6 = (f32[512,128]{1,0:T(8,128)S(1)}, f32[512,128]{1,0:T(8,128)S(1)}, u32[]{:S(2)}, u32[]{:S(2)}) collective-permute-start(f32[512,128]{1,0:T(8,128)S(1)} %slice.22), channel_id=1, source_target_pairs={{0,2},{2,0},{9,11},{11,9},{4,13},{13,4},{6,15},{15,6},{3,1},{1,3},... | collective-permute-start | bytes 786440 | tf_op jit(solution)/shard_map/ppermute | solution.py:75
  45.5 0.6 collective-permute-done.14
  46.2 5.5 %collective-permute-start.15 = (f32[2,128,128]{2,1,0:T(8,128)S(1)}, f32[2,128,128]{2,1,0:T(8,128)S(1)}, u32[]{:S(2)}, u32[]{:S(2)}) collective-permute-start(f32[2,128,128]{2,1,0:T(8,128)S(1)} %pad_maximum_fusion.5.d_mine), channel_id=1, source_target_pairs={{0,16},{1,17},{2,18},{3,19},{4,20},{5,21},{6,22},{7,23},{8,24},{9,... | collective-permute-start | bytes 393224 | tf_op jit(solution)/shard_map/ppermute | solution.py:75
  51.8 3.9 %collective-permute-start.17 = (f32[2,512,128]{2,1,0:T(8,128)S(1)}, f32[2,512,128]{2,1,0:T(8,128)S(1)}, u32[]{:S(2)}, u32[]{:S(2)}) collective-permute-start(f32[2,512,128]{2,1,0:T(8,128)S(1)} %pad_maximum_fusion.4.refs_0_), channel_id=1, source_target_pairs={{0,16},{1,17},{2,18},{3,19},{4,20},{5,21},{6,22},{7,23},{8,24},{9,... | collective-permute-start | bytes 1572872 | tf_op jit(solution)/shard_map/ppermute | solution.py:75
  55.7 0.5 collective-permute-start.11
  56.2 5.6 %collective-permute-start.7 = (f32[2,512,128]{2,1,0:T(8,128)S(1)}, f32[2,512,128]{2,1,0:T(8,128)S(1)}, u32[]{:S(2)}, u32[]{:S(2)}) collective-permute-start(f32[2,512,128]{2,1,0:T(8,128)S(1)} %pad_maximum_fusion.4.refs_0_), channel_id=1, source_target_pairs={{0,4},{1,5},{2,6},{3,7},{4,8},{5,9},{6,10},{7,11},{8,12},{9,13},{1... | collective-permute-start | bytes 1572872 | tf_op jit(solution)/shard_map/ppermute | solution.py:75
  62.0 5.2 %factor.1 = (bf16[256,256]{1,0:T(8,128)(2,1)S(1)}, f32[256,128]{1,0:T(8,128)}) custom-call(s32[4]{0:T(128)S(1)} %pad_add_fusion.info, f32[2,128,128]{2,1,0:T(8,128)S(1)} %pad_maximum_fusion.5.d_mine, f32[2,128,128]{2,1,0:T(8,128)S(1)} %collective-permute-done.15.d_other, f32[256,128]{1,0:T(8,128)S(1)} %broadcast_select_fusion.2.top), custom_call_target="tpu_custom_call" | custom-call | flops 8999999488 | bytes 2000000 | tf_op jit(solution)/shard_map/factor/pallas_call | solution.py:161
  67.2 7.4 %collective-permute-done.9.refs_1_ = f32[2,512,128]{2,1,0:T(8,128)S(1)} collective-permute-done((f32[2,512,128]{2,1,0:T(8,128)S(1)}, f32[2,512,128]{2,1,0:T(8,128)S(1)}, u32[]{:S(2)}, u32[]{:S(2)}) %collective-permute-start.9) | collective-permute-done | bytes 524320 | tf_op jit(solution)/shard_map/ppermute | solution.py:75
  74.6 1.5 %collective-permute-start.10 = (f32[2,512,128]{2,1,0:T(8,128)S(1)}, f32[2,512,128]{2,1,0:T(8,128)S(1)}, u32[]{:S(2)}, u32[]{:S(2)}) collective-permute-start(f32[2,512,128]{2,1,0:T(8,128)S(1)} %collective-permute-done.9.refs_1_), channel_id=1, source_target_pairs={{0,16},{1,17},{2,18},{3,19},{4,20},{5,21},{6,22},{7,23},{8,24},{9,... | collective-permute-start | bytes 1572872 | tf_op jit(solution)/shard_map/ppermute | solution.py:75
  76.1 0.5 collective-permute-start.8
  76.6 2.9 %shard_map.17.refs_5_ = f32[4096,128]{1,0:T(8,128)} custom-call(s32[4]{0:T(128)S(1)} %pad_add_fusion.1.info, f32[4096,128]{1,0:T(8,128)} %front.5, f32[2,512,128]{2,1,0:T(8,128)S(1)} %pad_maximum_fusion.4.refs_0_, f32[2,512,128]{2,1,0:T(8,128)S(1)} %collective-permute-done.17.refs_1_, bf16[256,256]{1,0:T(8,128)(2,1)S(1)} %get-tuple-element.7.refs_2_.refs_3_, ...), custom_call_target="tpu_custom_call" | custom-call | flops 3000000000 | bytes 4000000 | tf_op jit(solution)/shard_map/pallas_call | solution.py:215
  79.5 3.4 %shard_map.18.refs_5_ = f32[4096,128]{1,0:T(8,128)} custom-call(s32[5]{0:T(128)S(1)} %stack.94.info, f32[4096,128]{1,0:T(8,128)} %front.5, f32[2,512,128]{2,1,0:T(8,128)S(1)} %collective-permute-done.7.refs_0_, f32[2,512,128]{2,1,0:T(8,128)S(1)} %collective-permute-done.9.refs_1_, ...), custom_call_target="tpu_custom_call", output_to_operand_aliasing={{}: (7, {})} | custom-call | flops 3000000000 | bytes 4000000 | tf_op jit(solution)/shard_map/pallas_call | solution.py:215
  82.9 3.4 %shard_map.19 = f32[4096,128]{1,0:T(8,128)} custom-call(s32[5]{0:T(128)S(1)} %stack.81.info, f32[4096,128]{1,0:T(8,128)} %front.5, f32[2,512,128]{2,1,0:T(8,128)S(1)} %collective-permute-done.8.refs_0_, f32[2,512,128]{2,1,0:T(8,128)S(1)} %collective-permute-done.10.refs_1_, ...), custom_call_target="tpu_custom_call", output_to_operand_aliasing={{}: (7, {})} | custom-call | flops 3000000000 | bytes 4000000 | tf_op jit(solution)/shard_map/pallas_call | solution.py:215
  (27 shorter events, 0.9 us)
Async XLA Ops:
  0.0 4.7 %collective-permute-start = (f32[4096,128]{1,0:T(8,128)}, f32[4096,128]{1,0:T(8,128)S(1)}, u32[]{:S(2)}, u32[]{:S(2)}) collective-permute-start(f32[4096,128]{1,0:T(8,128)} %front.5), channel_id=1, source_target_pairs={{0,16},{1,17},{2,18},{3,19},{4,20},{5,21},{6,22},{7,23},{8,24},{9,... | collective-permute-start | bytes 6291464 | tf_op jit(solution)/shard_map/ppermute | solution.py:75
  6.9 11.5 %collective-permute-start.1 = (f32[640,128]{1,0:T(8,128)S(1)}, f32[640,128]{1,0:T(8,128)S(1)}, u32[]{:S(2)}, u32[]{:S(2)}) collective-permute-start(f32[640,128]{1,0:T(8,128)S(1)} %get-tuple-element.19), channel_id=1, source_target_pairs={{0,4},{1,5},{2,6},{3,7},{4,8},{5,9},{6,10},{7,11},{8,12},{9,13},{1... | collective-permute-start | bytes 983048 | tf_op jit(solution)/shard_map/ppermute | solution.py:75
  8.6 9.8 %collective-permute-start.2 = (f32[640,128]{1,0:T(8,128)S(1)}, f32[640,128]{1,0:T(8,128)S(1)}, u32[]{:S(2)}, u32[]{:S(2)}) collective-permute-start(f32[640,128]{1,0:T(8,128)S(1)} %get-tuple-element.18), channel_id=1, source_target_pairs={{0,12},{1,13},{2,14},{3,15},{4,0},{5,1},{6,2},{7,3},{8,4},{9,5},{1... | collective-permute-start | bytes 983048 | tf_op jit(solution)/shard_map/ppermute | solution.py:75
  10.8 8.6 %collective-permute-start.3 = (f32[640,128]{1,0:T(8,128)S(1)}, f32[640,128]{1,0:T(8,128)S(1)}, u32[]{:S(2)}, u32[]{:S(2)}) collective-permute-start(f32[640,128]{1,0:T(8,128)S(1)} %get-tuple-element.17), channel_id=1, source_target_pairs={{0,3},{1,2},{2,1},{3,0},{4,7},{5,6},{6,5},{7,4},{8,11},{9,10},{10,... | collective-permute-start | bytes 983048 | tf_op jit(solution)/shard_map/ppermute | solution.py:75
  19.5 7.8 %collective-permute-start.4 = (f32[640,128]{1,0:T(8,128)S(1)}, f32[640,128]{1,0:T(8,128)S(1)}, u32[]{:S(2)}, u32[]{:S(2)}) collective-permute-start(f32[640,128]{1,0:T(8,128)S(1)} %fusion.2), channel_id=1, source_target_pairs={{0,32},{1,33},{2,34},{3,35},{4,36},{5,37},{6,38},{7,39},{8,40},{9,... | collective-permute-start | bytes 983048 | tf_op jit(solution)/shard_map/ppermute | solution.py:75
  27.4 8.3 %collective-permute-start.5 = (f32[640,128]{1,0:T(8,128)S(1)}, f32[640,128]{1,0:T(8,128)S(1)}, u32[]{:S(2)}, u32[]{:S(2)}) collective-permute-start(f32[640,128]{1,0:T(8,128)S(1)} %broadcast_select_fusion), channel_id=1, source_target_pairs={{0,9},{2,11},{4,6},{13,15},{3,10},{1,8},{12,14},{5,7},{16,25},{18,... | collective-permute-start | bytes 983048 | tf_op jit(solution)/shard_map/ppermute | solution.py:75
  32.2 10.7 %collective-permute-start.16 = (f32[256,128]{1,0:T(8,128)S(1)}, f32[256,128]{1,0:T(8,128)S(1)}, u32[]{:S(2)}, u32[]{:S(2)}) collective-permute-start(f32[256,128]{1,0:T(8,128)S(1)} %slice.20), channel_id=1, source_target_pairs={{0,64},{1,65},{2,66},{3,67},{4,68},{5,69},{6,70},{7,71},{8,72},{9,... | collective-permute-start | bytes 393224 | tf_op jit(solution)/shard_map/ppermute | solution.py:75
  35.7 5.7 %collective-permute-start.13 = (f32[128,128]{1,0:T(8,128)S(1)}, f32[128,128]{1,0:T(8,128)S(1)}, u32[]{:S(2)}, u32[]{:S(2)}) collective-permute-start(f32[128,128]{1,0:T(8,128)S(1)} %slice.23), channel_id=1, source_target_pairs={{0,64},{1,65},{2,66},{3,67},{4,68},{5,69},{6,70},{7,71},{8,72},{9,... | collective-permute-start | bytes 196616 | tf_op jit(solution)/shard_map/ppermute | solution.py:75
  41.5 4.7 %collective-permute-start.14 = (f32[128,128]{1,0:T(8,128)S(1)}, f32[128,128]{1,0:T(8,128)S(1)}, u32[]{:S(2)}, u32[]{:S(2)}) collective-permute-start(f32[128,128]{1,0:T(8,128)S(1)} %broadcast_select_fusion.3), channel_id=1, source_target_pairs={{0,2},{2,0},{9,11},{11,9},{4,13},{13,4},{6,15},{15,6},{3,1},{1,3},... | collective-permute-start | bytes 196616 | tf_op jit(solution)/shard_map/ppermute | solution.py:75
  43.8 7.9 %collective-permute-start.6 = (f32[512,128]{1,0:T(8,128)S(1)}, f32[512,128]{1,0:T(8,128)S(1)}, u32[]{:S(2)}, u32[]{:S(2)}) collective-permute-start(f32[512,128]{1,0:T(8,128)S(1)} %slice.22), channel_id=1, source_target_pairs={{0,2},{2,0},{9,11},{11,9},{4,13},{13,4},{6,15},{15,6},{3,1},{1,3},... | collective-permute-start | bytes 786440 | tf_op jit(solution)/shard_map/ppermute | solution.py:75
  46.2 15.8 %collective-permute-start.15 = (f32[2,128,128]{2,1,0:T(8,128)S(1)}, f32[2,128,128]{2,1,0:T(8,128)S(1)}, u32[]{:S(2)}, u32[]{:S(2)}) collective-permute-start(f32[2,128,128]{2,1,0:T(8,128)S(1)} %pad_maximum_fusion.5.d_mine), channel_id=1, source_target_pairs={{0,16},{1,17},{2,18},{3,19},{4,20},{5,21},{6,22},{7,23},{8,24},{9,... | collective-permute-start | bytes 393224 | tf_op jit(solution)/shard_map/ppermute | solution.py:75
  51.8 24.8 %collective-permute-start.17 = (f32[2,512,128]{2,1,0:T(8,128)S(1)}, f32[2,512,128]{2,1,0:T(8,128)S(1)}, u32[]{:S(2)}, u32[]{:S(2)}) collective-permute-start(f32[2,512,128]{2,1,0:T(8,128)S(1)} %pad_maximum_fusion.4.refs_0_), channel_id=1, source_target_pairs={{0,16},{1,17},{2,18},{3,19},{4,20},{5,21},{6,22},{7,23},{8,24},{9,... | collective-permute-start | bytes 1572872 | tf_op jit(solution)/shard_map/ppermute | solution.py:75
  55.7 20.4 %collective-permute-start.11 = (f32[2,512,128]{2,1,0:T(8,128)S(1)}, f32[2,512,128]{2,1,0:T(8,128)S(1)}, u32[]{:S(2)}, u32[]{:S(2)}) collective-permute-start(f32[2,512,128]{2,1,0:T(8,128)S(1)} %pad_maximum_fusion.4.refs_0_), channel_id=1, source_target_pairs={{0,1},{1,2},{2,3},{3,0},{4,5},{5,6},{6,7},{7,4},{8,9},{9,10},{10,1... | collective-permute-start | bytes 1572872 | tf_op jit(solution)/shard_map/ppermute | solution.py:75
  56.2 19.9 %collective-permute-start.7 = (f32[2,512,128]{2,1,0:T(8,128)S(1)}, f32[2,512,128]{2,1,0:T(8,128)S(1)}, u32[]{:S(2)}, u32[]{:S(2)}) collective-permute-start(f32[2,512,128]{2,1,0:T(8,128)S(1)} %pad_maximum_fusion.4.refs_0_), channel_id=1, source_target_pairs={{0,4},{1,5},{2,6},{3,7},{4,8},{5,9},{6,10},{7,11},{8,12},{9,13},{1... | collective-permute-start | bytes 1572872 | tf_op jit(solution)/shard_map/ppermute | solution.py:75
  61.8 12.8 %collective-permute-start.9 = (f32[2,512,128]{2,1,0:T(8,128)S(1)}, f32[2,512,128]{2,1,0:T(8,128)S(1)}, u32[]{:S(2)}, u32[]{:S(2)}) collective-permute-start(f32[2,512,128]{2,1,0:T(8,128)S(1)} %pad_maximum_fusion.4.refs_0_), channel_id=1, source_target_pairs={{0,12},{1,13},{2,14},{3,15},{4,0},{5,1},{6,2},{7,3},{8,4},{9,5},{1... | collective-permute-start | bytes 1572872 | tf_op jit(solution)/shard_map/ppermute | solution.py:75
  74.6 8.3 %collective-permute-start.10 = (f32[2,512,128]{2,1,0:T(8,128)S(1)}, f32[2,512,128]{2,1,0:T(8,128)S(1)}, u32[]{:S(2)}, u32[]{:S(2)}) collective-permute-start(f32[2,512,128]{2,1,0:T(8,128)S(1)} %collective-permute-done.9.refs_1_), channel_id=1, source_target_pairs={{0,16},{1,17},{2,18},{3,19},{4,20},{5,21},{6,22},{7,23},{8,24},{9,... | collective-permute-start | bytes 1572872 | tf_op jit(solution)/shard_map/ppermute | solution.py:75
  76.1 6.8 %collective-permute-start.12 = (f32[2,512,128]{2,1,0:T(8,128)S(1)}, f32[2,512,128]{2,1,0:T(8,128)S(1)}, u32[]{:S(2)}, u32[]{:S(2)}) collective-permute-start(f32[2,512,128]{2,1,0:T(8,128)S(1)} %collective-permute-done.11.refs_2_), channel_id=1, source_target_pairs={{0,16},{1,17},{2,18},{3,19},{4,20},{5,21},{6,22},{7,23},{8,24},{9,... | collective-permute-start | bytes 1572872 | tf_op jit(solution)/shard_map/ppermute | solution.py:75
  76.1 6.8 %collective-permute-start.8 = (f32[2,512,128]{2,1,0:T(8,128)S(1)}, f32[2,512,128]{2,1,0:T(8,128)S(1)}, u32[]{:S(2)}, u32[]{:S(2)}) collective-permute-start(f32[2,512,128]{2,1,0:T(8,128)S(1)} %collective-permute-done.7.refs_0_), channel_id=1, source_target_pairs={{0,16},{1,17},{2,18},{3,19},{4,20},{5,21},{6,22},{7,23},{8,24},{9,... | collective-permute-start | bytes 1572872 | tf_op jit(solution)/shard_map/ppermute | solution.py:75

commit v5 on v4

--- a/solution.py
+++ b/solution.py
@@ -15,6 +15,7 @@
 ROWS = 4096
 WIDTH = 128
 SHARE = 512
+DELTAS = (1, 3, 2, 0)
 DPART = 128
 
 
@@ -77,6 +78,42 @@
 
 def in_vmem(value):
     return pltpu.with_memory_space_constraint(value, pltpu.VMEM)
+
+
+def payload_kernel(info, front, beside, *refs):
+    outs, sems = refs[:-1], refs[-1]
+
+    def copies(source, half):
+        made = []
+        for at, (delta, out) in enumerate(zip(DELTAS, outs)):
+            begin = pl.multiple_of((info[1] + delta) % 4 * SHARE + half * (ROWS // 2), SHARE)
+            pivots, rows = source.at[half * DPART : (half + 1) * DPART, :], source.at[pl.ds(begin, SHARE), :]
+            made.append(pltpu.make_async_copy(pivots, out.at[0:DPART, :], sems.at[2 * at]))
+            made.append(pltpu.make_async_copy(rows, out.at[DPART:, :], sems.at[2 * at + 1]))
+        return made
+
+    for half, source in enumerate((front, beside)):
+        @pl.when(info[0] == half)
+        def _():
+            for copy in copies(source, half):
+                copy.start()
+
+    for copy in copies(front, 0):
+        copy.wait()
+
+
+def payloads(info, front, beside):
+    hbm = pl.BlockSpec(memory_space=pltpu.HBM)
+    front = pltpu.with_memory_space_constraint(front, pltpu.HBM)
+    return pl.pallas_call(
+        payload_kernel,
+        out_shape=tuple(pltpu.VMEM((DPART + SHARE, WIDTH), jnp.float32) for _ in DELTAS),
+        in_specs=[pl.BlockSpec(memory_space=pltpu.SMEM), hbm, pl.BlockSpec(memory_space=pltpu.VMEM)],
+        out_specs=tuple(pl.BlockSpec(memory_space=pltpu.VMEM) for _ in DELTAS),
+        scratch_shapes=[pltpu.SemaphoreType.DMA((2 * len(DELTAS),))],
+        compiler_params=pltpu.CompilerParams(vmem_limit_bytes=4 << 20),
+        name="payloads",
+    )(info, front, in_vmem(beside))
 
 
 def split3(value):
@@ -236,24 +273,13 @@
     panel = (x == 0) & (z == 0) & (y < 2) & (core == 0)
     info = jnp.stack([core, panel.astype(jnp.int32), y, row]).astype(jnp.int32)
 
-    def start(delta):
-        return (mine + delta) % 4 * SHARE
-
-    def rows(array, at, size=SHARE):
-        return lax.dynamic_slice(array, (at, 0), (size, WIDTH))
-
     beside = send(front, CORE_SWAP)
-    d_start = jnp.where(core == 0, front[:DPART], beside[DPART:P_SIZE])
-
-    def share(delta):
-        half = jnp.where(core == 0, rows(front, start(delta)), rows(beside, start(delta) + ROWS // 2))
-        return jnp.concatenate([d_start, half])
-
-    up = send(share(1), shift(1, 0))
-    down = send(share(3), shift(-1, 0))
-    side = send(share(2), SIDE)
+    to_up, to_down, to_side, to_self = payloads(jnp.stack([core, mine]).astype(jnp.int32), front, beside)
+    up = send(to_up, shift(1, 0))
+    down = send(to_down, shift(-1, 0))
+    side = send(to_side, SIDE)
     near = y < 2
-    held = jnp.where((z == 1) & near, up, jnp.where((z == 3) & near, down, jnp.where(near, share(0), side)))
+    held = jnp.where((z == 1) & near, up, jnp.where((z == 3) & near, down, jnp.where(near, to_self, side)))
     held = jnp.where(x == 0, held, send(held, X_SWAP))
 
     role = member(z, y)
@@ -278,19 +304,19 @@
     own_other = send(own, CORE_SWAP)
     update, top_done = factor(info, d_mine, d_other, top)
 
-    order = [(mine + 3) % 4, (mine + 1) % 4, (mine + 2) % 4]
-
     def at(*blocks):
         return jnp.stack([panel.astype(jnp.int32), row, *blocks]).astype(jnp.int32)
 
-    places = at(mine + 4 * core, mine + 4 * (1 - core))
-    out = apply_update(places, front, (own, own_other), update, top_done)
-    received = (before, after, far)
-    others = tuple(send(v, CORE_SWAP) for v in received)
-    places = at(*(p + 4 * core for p in order))
-    out = apply_update(places, front, received, update, top_done, out)
-    places = at(*(p + 4 * (1 - core) for p in order))
-    return apply_update(places, front, others, update, top_done, out)
+    here, there = core * 4, (1 - core) * 4
+    earlier, later, middle = (mine + 3) % 4, (mine + 1) % 4, (mine + 2) % 4
+    before_other = send(before, CORE_SWAP)
+    places = at(mine + here, mine + there, earlier + here)
+    out = apply_update(places, front, (own, own_other, before), update, top_done)
+    after_other, far_other = send(after, CORE_SWAP), send(far, CORE_SWAP)
+    places = at(later + here, middle + here, earlier + there)
+    out = apply_update(places, front, (after, far, before_other), update, top_done, out)
+    places = at(later + there, middle + there)
+    return apply_update(places, front, (after_other, far_other), update, top_done, out)
 
 
 def solution(mesh):

time: 86.6 us -> 83.2 us (0.961)
  the two profiles are of different devices: /device:TPU:9 before, /device:TPU:0 now
where the time goes in v5:
time: 83.2 us; the launch traced here: 82.1 us
  waiting for transfers between devices  31.4 us (38%)
  starting transfers between devices  31.3 us (38%)
  Pallas kernels  16.8 us (20%)
  other arithmetic  1.4 us (2%)
  local copies, waits for them, and re-layouts  1.11 us (1%)
    ppermute x18, waiting for transfers between devices, send(): return lax.ppermute(value, AXES, pairs)  31.4 us
    ppermute x18, starting transfers between devices, send(): return lax.ppermute(value, AXES, pairs)  31.3 us
    pallas_call x3, Pallas kernels, apply_update(): pl.pallas_call(update_kernel, out_shape=jax.ShapeDtypeStruct((ROWS, WIDTH...  9.66 us
    pallas_call x1, Pallas kernels, factor(): pl.pallas_call(factor_kernel, out_shape=(pltpu.VMEM((P_SIZE, 2 * WIDTH),...  5.23 us
    pallas_call x1, Pallas kernels, payloads(): pl.pallas_call(payload_kernel, out_shape=tuple((pltpu.VMEM((DPART + SHARE...  1.91 us
  transfers between devices with their start and end apart: 18, of which 9 were waited for; matrix products, arithmetic and copies ran while one was open for 3% of the time, Pallas kernels for 15%

profile of v5, /device:TPU:0, one launch (start us, length us, event | category | flops | bytes accessed | tf_op | source)
XLA Modules:
  0.0 82.1 jit_solution(16730986292835198592)
XLA Ops:
  0.1 4.3 %collective-permute-done.beside = f32[4096,128]{1,0:T(8,128)S(1)} collective-permute-done((f32[4096,128]{1,0:T(8,128)}, f32[4096,128]{1,0:T(8,128)S(1)}, u32[]{:S(2)}, u32[]{:S(2)}) %collective-permute-start) | collective-permute-done | bytes 2097184 | tf_op jit(solution)/shard_map/ppermute | solution.py:76
  4.4 1.9 %payloads.1 = (f32[640,128]{1,0:T(8,128)S(1)}, f32[640,128]{1,0:T(8,128)S(1)}, f32[640,128]{1,0:T(8,128)S(1)}, f32[640,128]{1,0:T(8,128)S(1)}) custom-call(s32[2]{0:T(128)S(1)} %pad_add_fusion.1.info, f32[4096,128]{1,0:T(8,128)} %front.7, f32[4096,128]{1,0:T(8,128)S(1)} %collective-permute-done.beside), custom_call_target="tpu_custom_call" | custom-call | tf_op jit(solution)/shard_map/payloads/pallas_call | solution.py:108
  6.3 2.1 %collective-permute-start.1 = (f32[640,128]{1,0:T(8,128)S(1)}, f32[640,128]{1,0:T(8,128)S(1)}, u32[]{:S(2)}, u32[]{:S(2)}) collective-permute-start(f32[640,128]{1,0:T(8,128)S(1)} %get-tuple-element.11), channel_id=1, source_target_pairs={{0,4},{1,5},{2,6},{3,7},{4,8},{5,9},{6,10},{7,11},{8,12},{9,13},{1... | collective-permute-start | bytes 983048 | tf_op jit(solution)/shard_map/ppermute | solution.py:76
  8.4 2.2 %collective-permute-start.2 = (f32[640,128]{1,0:T(8,128)S(1)}, f32[640,128]{1,0:T(8,128)S(1)}, u32[]{:S(2)}, u32[]{:S(2)}) collective-permute-start(f32[640,128]{1,0:T(8,128)S(1)} %get-tuple-element.12), channel_id=1, source_target_pairs={{0,12},{1,13},{2,14},{3,15},{4,0},{5,1},{6,2},{7,3},{8,4},{9,5},{1... | collective-permute-start | bytes 983048 | tf_op jit(solution)/shard_map/ppermute | solution.py:76
  10.6 3.0 %collective-permute-start.3 = (f32[640,128]{1,0:T(8,128)S(1)}, f32[640,128]{1,0:T(8,128)S(1)}, u32[]{:S(2)}, u32[]{:S(2)}) collective-permute-start(f32[640,128]{1,0:T(8,128)S(1)} %get-tuple-element.14), channel_id=1, source_target_pairs={{0,3},{1,2},{2,1},{3,0},{4,7},{5,6},{6,5},{7,4},{8,11},{9,10},{10,... | collective-permute-start | bytes 983048 | tf_op jit(solution)/shard_map/ppermute | solution.py:76
  13.6 4.1 %collective-permute-done.1 = f32[640,128]{1,0:T(8,128)S(1)} collective-permute-done((f32[640,128]{1,0:T(8,128)S(1)}, f32[640,128]{1,0:T(8,128)S(1)}, u32[]{:S(2)}, u32[]{:S(2)}) %collective-permute-start.1) | collective-permute-done | bytes 327712 | tf_op jit(solution)/shard_map/ppermute | solution.py:76
  17.7 2.8 %collective-permute-done.3 = f32[640,128]{1,0:T(8,128)S(1)} collective-permute-done((f32[640,128]{1,0:T(8,128)S(1)}, f32[640,128]{1,0:T(8,128)S(1)}, u32[]{:S(2)}, u32[]{:S(2)}) %collective-permute-start.3) | collective-permute-done | bytes 327712 | tf_op jit(solution)/shard_map/ppermute | solution.py:76
  20.6 1.6 %collective-permute-start.4 = (f32[640,128]{1,0:T(8,128)S(1)}, f32[640,128]{1,0:T(8,128)S(1)}, u32[]{:S(2)}, u32[]{:S(2)}) collective-permute-start(f32[640,128]{1,0:T(8,128)S(1)} %select_select_fusion), channel_id=1, source_target_pairs={{0,32},{1,33},{2,34},{3,35},{4,36},{5,37},{6,38},{7,39},{8,40},{9,... | collective-permute-start | bytes 983048 | tf_op jit(solution)/shard_map/ppermute | solution.py:76
  22.1 6.3 %collective-permute-done.4 = f32[640,128]{1,0:T(8,128)S(1)} collective-permute-done((f32[640,128]{1,0:T(8,128)S(1)}, f32[640,128]{1,0:T(8,128)S(1)}, u32[]{:S(2)}, u32[]{:S(2)}) %collective-permute-start.4) | collective-permute-done | bytes 327712 | tf_op jit(solution)/shard_map/ppermute | solution.py:76
  28.5 3.0 %collective-permute-start.5 = (f32[640,128]{1,0:T(8,128)S(1)}, f32[640,128]{1,0:T(8,128)S(1)}, u32[]{:S(2)}, u32[]{:S(2)}) collective-permute-start(f32[640,128]{1,0:T(8,128)S(1)} %broadcast_select_fusion), channel_id=1, source_target_pairs={{0,9},{2,11},{4,6},{13,15},{3,10},{1,8},{12,14},{5,7},{16,25},{18,... | collective-permute-start | bytes 983048 | tf_op jit(solution)/shard_map/ppermute | solution.py:76
  31.5 0.9 %slice.12 = f32[256,128]{1,0:T(8,128)S(1)} slice(f32[4096,128]{1,0:T(8,128)} %front.7), slice={[0:256], [0:128]} | slice | bytes 262144 | tf_op jit(solution)/shard_map/slice | solution.py:288
  32.4 3.1 %collective-permute-start.14 = (f32[256,128]{1,0:T(8,128)S(1)}, f32[256,128]{1,0:T(8,128)S(1)}, u32[]{:S(2)}, u32[]{:S(2)}) collective-permute-start(f32[256,128]{1,0:T(8,128)S(1)} %slice.12), channel_id=1, source_target_pairs={{0,64},{1,65},{2,66},{3,67},{4,68},{5,69},{6,70},{7,71},{8,72},{9,... | collective-permute-start | bytes 393224 | tf_op jit(solution)/shard_map/ppermute | solution.py:76
  35.6 0.5 collective-permute-done.5
  36.1 3.1 %collective-permute-start.11 = (f32[128,128]{1,0:T(8,128)S(1)}, f32[128,128]{1,0:T(8,128)S(1)}, u32[]{:S(2)}, u32[]{:S(2)}) collective-permute-start(f32[128,128]{1,0:T(8,128)S(1)} %slice.14), channel_id=1, source_target_pairs={{0,64},{1,65},{2,66},{3,67},{4,68},{5,69},{6,70},{7,71},{8,72},{9,... | collective-permute-start | bytes 196616 | tf_op jit(solution)/shard_map/ppermute | solution.py:76
  39.2 7.0 %collective-permute-start.6 = (f32[512,128]{1,0:T(8,128)S(1)}, f32[512,128]{1,0:T(8,128)S(1)}, u32[]{:S(2)}, u32[]{:S(2)}) collective-permute-start(f32[512,128]{1,0:T(8,128)S(1)} %slice.13), channel_id=1, source_target_pairs={{0,2},{2,0},{9,11},{11,9},{4,13},{13,4},{6,15},{15,6},{3,1},{1,3},... | collective-permute-start | bytes 786440 | tf_op jit(solution)/shard_map/ppermute | solution.py:76
  46.3 0.1 stack.106.info
  46.4 0.1 stack.102.info
  46.5 2.1 %collective-permute-start.12 = (f32[128,128]{1,0:T(8,128)S(1)}, f32[128,128]{1,0:T(8,128)S(1)}, u32[]{:S(2)}, u32[]{:S(2)}) collective-permute-start(f32[128,128]{1,0:T(8,128)S(1)} %broadcast_select_fusion.3), channel_id=1, source_target_pairs={{0,2},{2,0},{9,11},{11,9},{4,13},{13,4},{6,15},{15,6},{3,1},{1,3},... | collective-permute-start | bytes 196616 | tf_op jit(solution)/shard_map/ppermute | solution.py:76
  48.6 2.0 %collective-permute-done.6 = f32[512,128]{1,0:T(8,128)S(1)} collective-permute-done((f32[512,128]{1,0:T(8,128)S(1)}, f32[512,128]{1,0:T(8,128)S(1)}, u32[]{:S(2)}, u32[]{:S(2)}) %collective-permute-start.6) | collective-permute-done | bytes 262176 | tf_op jit(solution)/shard_map/ppermute | solution.py:76
  50.8 1.6 %collective-permute-done.12 = f32[128,128]{1,0:T(8,128)S(1)} collective-permute-done((f32[128,128]{1,0:T(8,128)S(1)}, f32[128,128]{1,0:T(8,128)S(1)}, u32[]{:S(2)}, u32[]{:S(2)}) %collective-permute-start.12) | collective-permute-done | bytes 65568 | tf_op jit(solution)/shard_map/ppermute | solution.py:76
  52.4 0.1 collective-permute-start.13
  52.5 0.9 %broadcast_select_fusion.2.top = f32[256,128]{1,0:T(8,128)S(1)} fusion(f32[256,128]{1,0:T(8,128)S(1)} %collective-permute-done.14, pred[]{:T(512)S(6)} %eq.62, f32[4096,128]{1,0:T(8,128)} %front.7), kind=kLoop, calls=%fused_computation.9 | loop fusion | flops 32768 | bytes 393217 | tf_op jit(solution)/shard_map/jit(_where)/select_n | solution.py:288
  53.4 0.6 collective-permute-start.17
  54.0 1.6 %collective-permute-start.7 = (f32[2,512,128]{2,1,0:T(8,128)S(1)}, f32[2,512,128]{2,1,0:T(8,128)S(1)}, u32[]{:S(2)}, u32[]{:S(2)}) collective-permute-start(f32[2,512,128]{2,1,0:T(8,128)S(1)} %pad_maximum_fusion.refs_0_), channel_id=1, source_target_pairs={{0,12},{1,13},{2,14},{3,15},{4,0},{5,1},{6,2},{7,3},{8,4},{9,5},{1... | collective-permute-start | bytes 1572872 | tf_op jit(solution)/shard_map/ppermute | solution.py:76
  55.6 1.2 %collective-permute-start.9 = (f32[2,512,128]{2,1,0:T(8,128)S(1)}, f32[2,512,128]{2,1,0:T(8,128)S(1)}, u32[]{:S(2)}, u32[]{:S(2)}) collective-permute-start(f32[2,512,128]{2,1,0:T(8,128)S(1)} %pad_maximum_fusion.refs_0_), channel_id=1, source_target_pairs={{0,1},{1,2},{2,3},{3,0},{4,5},{5,6},{6,7},{7,4},{8,9},{9,10},{10,1... | collective-permute-start | bytes 1572872 | tf_op jit(solution)/shard_map/ppermute | solution.py:76
  56.9 4.3 %collective-permute-done.15.refs_2_ = f32[2,512,128]{2,1,0:T(8,128)S(1)} collective-permute-done((f32[2,512,128]{2,1,0:T(8,128)S(1)}, f32[2,512,128]{2,1,0:T(8,128)S(1)}, u32[]{:S(2)}, u32[]{:S(2)}) %collective-permute-start.15) | collective-permute-done | bytes 524320 | tf_op jit(solution)/shard_map/ppermute | solution.py:76
  61.2 5.2 %factor.1 = (bf16[256,256]{1,0:T(8,128)(2,1)S(1)}, f32[256,128]{1,0:T(8,128)}) custom-call(s32[4]{0:T(128)S(1)} %pad_add_fusion.2.info, f32[2,128,128]{2,1,0:T(8,128)S(1)} %pad_maximum_fusion.1.d_mine, f32[2,128,128]{2,1,0:T(8,128)S(1)} %collective-permute-done.13.d_other, f32[256,128]{1,0:T(8,128)S(1)} %broadcast_select_fusion.2.top), custom_call_target="tpu_custom_call" | custom-call | flops 8999999488 | bytes 2000000 | tf_op jit(solution)/shard_map/factor/pallas_call | solution.py:198
  66.4 5.5 %collective-permute-done.9.refs_1_ = f32[2,512,128]{2,1,0:T(8,128)S(1)} collective-permute-done((f32[2,512,128]{2,1,0:T(8,128)S(1)}, f32[2,512,128]{2,1,0:T(8,128)S(1)}, u32[]{:S(2)}, u32[]{:S(2)}) %collective-permute-start.9) | collective-permute-done | bytes 524320 | tf_op jit(solution)/shard_map/ppermute | solution.py:76
  71.9 0.5 collective-permute-start.8
  72.4 3.4 %shard_map.17.refs_5_ = f32[4096,128]{1,0:T(8,128)} custom-call(s32[5]{0:T(128)S(1)} %stack.106.info, f32[4096,128]{1,0:T(8,128)} %front.7, f32[2,512,128]{2,1,0:T(8,128)S(1)} %pad_maximum_fusion.refs_0_, f32[2,512,128]{2,1,0:T(8,128)S(1)} %collective-permute-done.17.refs_1_, f32[2,512,128]{2,1,0:T(8,128)S(1)} %collective-permute-done.15.refs_2_, ...), custom_call_target="tpu_custom_call" | custom-call | flops 3000000000 | bytes 4000000 | tf_op jit(solution)/shard_map/pallas_call | solution.py:252
  75.9 3.4 %shard_map.18.refs_4_ = f32[4096,128]{1,0:T(8,128)} custom-call(s32[5]{0:T(128)S(1)} %stack.102.info, f32[4096,128]{1,0:T(8,128)} %front.7, f32[2,512,128]{2,1,0:T(8,128)S(1)} %collective-permute-done.7.refs_0_, f32[2,512,128]{2,1,0:T(8,128)S(1)} %collective-permute-done.9.refs_1_, ...), custom_call_target="tpu_custom_call", output_to_operand_aliasing={{}: (7, {})} | custom-call | flops 3000000000 | bytes 4000000 | tf_op jit(solution)/shard_map/pallas_call | solution.py:252
  79.3 2.9 %shard_map.19 = f32[4096,128]{1,0:T(8,128)} custom-call(s32[4]{0:T(128)S(1)} %pad_add_fusion.info, f32[4096,128]{1,0:T(8,128)} %front.7, f32[2,512,128]{2,1,0:T(8,128)S(1)} %collective-permute-done.8.refs_0_, f32[2,512,128]{2,1,0:T(8,128)S(1)} %collective-permute-done.10.refs_1_, ...), custom_call_target="tpu_custom_call", output_to_operand_aliasing={{}: (6, {})} | custom-call | flops 3000000000 | bytes 4000000 | tf_op jit(solution)/shard_map/pallas_call | solution.py:252
  (26 shorter events, 0.6 us)
Async XLA Ops:
  0.0 4.4 %collective-permute-start = (f32[4096,128]{1,0:T(8,128)}, f32[4096,128]{1,0:T(8,128)S(1)}, u32[]{:S(2)}, u32[]{:S(2)}) collective-permute-start(f32[4096,128]{1,0:T(8,128)} %front.7), channel_id=1, source_target_pairs={{0,16},{1,17},{2,18},{3,19},{4,20},{5,21},{6,22},{7,23},{8,24},{9,... | collective-permute-start | bytes 6291464 | tf_op jit(solution)/shard_map/ppermute | solution.py:76
  6.3 11.4 %collective-permute-start.1 = (f32[640,128]{1,0:T(8,128)S(1)}, f32[640,128]{1,0:T(8,128)S(1)}, u32[]{:S(2)}, u32[]{:S(2)}) collective-permute-start(f32[640,128]{1,0:T(8,128)S(1)} %get-tuple-element.11), channel_id=1, source_target_pairs={{0,4},{1,5},{2,6},{3,7},{4,8},{5,9},{6,10},{7,11},{8,12},{9,13},{1... | collective-permute-start | bytes 983048 | tf_op jit(solution)/shard_map/ppermute | solution.py:76
  8.4 9.3 %collective-permute-start.2 = (f32[640,128]{1,0:T(8,128)S(1)}, f32[640,128]{1,0:T(8,128)S(1)}, u32[]{:S(2)}, u32[]{:S(2)}) collective-permute-start(f32[640,128]{1,0:T(8,128)S(1)} %get-tuple-element.12), channel_id=1, source_target_pairs={{0,12},{1,13},{2,14},{3,15},{4,0},{5,1},{6,2},{7,3},{8,4},{9,5},{1... | collective-permute-start | bytes 983048 | tf_op jit(solution)/shard_map/ppermute | solution.py:76
  10.6 9.9 %collective-permute-start.3 = (f32[640,128]{1,0:T(8,128)S(1)}, f32[640,128]{1,0:T(8,128)S(1)}, u32[]{:S(2)}, u32[]{:S(2)}) collective-permute-start(f32[640,128]{1,0:T(8,128)S(1)} %get-tuple-element.14), channel_id=1, source_target_pairs={{0,3},{1,2},{2,1},{3,0},{4,7},{5,6},{6,5},{7,4},{8,11},{9,10},{10,... | collective-permute-start | bytes 983048 | tf_op jit(solution)/shard_map/ppermute | solution.py:76
  20.6 7.9 %collective-permute-start.4 = (f32[640,128]{1,0:T(8,128)S(1)}, f32[640,128]{1,0:T(8,128)S(1)}, u32[]{:S(2)}, u32[]{:S(2)}) collective-permute-start(f32[640,128]{1,0:T(8,128)S(1)} %select_select_fusion), channel_id=1, source_target_pairs={{0,32},{1,33},{2,34},{3,35},{4,36},{5,37},{6,38},{7,39},{8,40},{9,... | collective-permute-start | bytes 983048 | tf_op jit(solution)/shard_map/ppermute | solution.py:76
  28.5 7.5 %collective-permute-start.5 = (f32[640,128]{1,0:T(8,128)S(1)}, f32[640,128]{1,0:T(8,128)S(1)}, u32[]{:S(2)}, u32[]{:S(2)}) collective-permute-start(f32[640,128]{1,0:T(8,128)S(1)} %broadcast_select_fusion), channel_id=1, source_target_pairs={{0,9},{2,11},{4,6},{13,15},{3,10},{1,8},{12,14},{5,7},{16,25},{18,... | collective-permute-start | bytes 983048 | tf_op jit(solution)/shard_map/ppermute | solution.py:76
  32.4 20.1 %collective-permute-start.14 = (f32[256,128]{1,0:T(8,128)S(1)}, f32[256,128]{1,0:T(8,128)S(1)}, u32[]{:S(2)}, u32[]{:S(2)}) collective-permute-start(f32[256,128]{1,0:T(8,128)S(1)} %slice.12), channel_id=1, source_target_pairs={{0,64},{1,65},{2,66},{3,67},{4,68},{5,69},{6,70},{7,71},{8,72},{9,... | collective-permute-start | bytes 393224 | tf_op jit(solution)/shard_map/ppermute | solution.py:76
  36.1 10.4 %collective-permute-start.11 = (f32[128,128]{1,0:T(8,128)S(1)}, f32[128,128]{1,0:T(8,128)S(1)}, u32[]{:S(2)}, u32[]{:S(2)}) collective-permute-start(f32[128,128]{1,0:T(8,128)S(1)} %slice.14), channel_id=1, source_target_pairs={{0,64},{1,65},{2,66},{3,67},{4,68},{5,69},{6,70},{7,71},{8,72},{9,... | collective-permute-start | bytes 196616 | tf_op jit(solution)/shard_map/ppermute | solution.py:76
  39.2 11.4 %collective-permute-start.6 = (f32[512,128]{1,0:T(8,128)S(1)}, f32[512,128]{1,0:T(8,128)S(1)}, u32[]{:S(2)}, u32[]{:S(2)}) collective-permute-start(f32[512,128]{1,0:T(8,128)S(1)} %slice.13), channel_id=1, source_target_pairs={{0,2},{2,0},{9,11},{11,9},{4,13},{13,4},{6,15},{15,6},{3,1},{1,3},... | collective-permute-start | bytes 786440 | tf_op jit(solution)/shard_map/ppermute | solution.py:76
  46.5 5.8 %collective-permute-start.12 = (f32[128,128]{1,0:T(8,128)S(1)}, f32[128,128]{1,0:T(8,128)S(1)}, u32[]{:S(2)}, u32[]{:S(2)}) collective-permute-start(f32[128,128]{1,0:T(8,128)S(1)} %broadcast_select_fusion.3), channel_id=1, source_target_pairs={{0,2},{2,0},{9,11},{11,9},{4,13},{13,4},{6,15},{15,6},{3,1},{1,3},... | collective-permute-start | bytes 196616 | tf_op jit(solution)/shard_map/ppermute | solution.py:76
  50.7 10.5 %collective-permute-start.15 = (f32[2,512,128]{2,1,0:T(8,128)S(1)}, f32[2,512,128]{2,1,0:T(8,128)S(1)}, u32[]{:S(2)}, u32[]{:S(2)}) collective-permute-start(f32[2,512,128]{2,1,0:T(8,128)S(1)} %pad_maximum_fusion.refs_0_), channel_id=1, source_target_pairs={{0,4},{1,5},{2,6},{3,7},{4,8},{5,9},{6,10},{7,11},{8,12},{9,13},{1... | collective-permute-start | bytes 1572872 | tf_op jit(solution)/shard_map/ppermute | solution.py:76
  52.4 8.8 %collective-permute-start.13 = (f32[2,128,128]{2,1,0:T(8,128)S(1)}, f32[2,128,128]{2,1,0:T(8,128)S(1)}, u32[]{:S(2)}, u32[]{:S(2)}) collective-permute-start(f32[2,128,128]{2,1,0:T(8,128)S(1)} %pad_maximum_fusion.1.d_mine), channel_id=1, source_target_pairs={{0,16},{1,17},{2,18},{3,19},{4,20},{5,21},{6,22},{7,23},{8,24},{9,... | collective-permute-start | bytes 393224 | tf_op jit(solution)/shard_map/ppermute | solution.py:76
  53.4 19.0 %collective-permute-start.17 = (f32[2,512,128]{2,1,0:T(8,128)S(1)}, f32[2,512,128]{2,1,0:T(8,128)S(1)}, u32[]{:S(2)}, u32[]{:S(2)}) collective-permute-start(f32[2,512,128]{2,1,0:T(8,128)S(1)} %pad_maximum_fusion.refs_0_), channel_id=1, source_target_pairs={{0,16},{1,17},{2,18},{3,19},{4,20},{5,21},{6,22},{7,23},{8,24},{9,... | collective-permute-start | bytes 1572872 | tf_op jit(solution)/shard_map/ppermute | solution.py:76
  54.0 17.9 %collective-permute-start.7 = (f32[2,512,128]{2,1,0:T(8,128)S(1)}, f32[2,512,128]{2,1,0:T(8,128)S(1)}, u32[]{:S(2)}, u32[]{:S(2)}) collective-permute-start(f32[2,512,128]{2,1,0:T(8,128)S(1)} %pad_maximum_fusion.refs_0_), channel_id=1, source_target_pairs={{0,12},{1,13},{2,14},{3,15},{4,0},{5,1},{6,2},{7,3},{8,4},{9,5},{1... | collective-permute-start | bytes 1572872 | tf_op jit(solution)/shard_map/ppermute | solution.py:76
  55.6 16.3 %collective-permute-start.9 = (f32[2,512,128]{2,1,0:T(8,128)S(1)}, f32[2,512,128]{2,1,0:T(8,128)S(1)}, u32[]{:S(2)}, u32[]{:S(2)}) collective-permute-start(f32[2,512,128]{2,1,0:T(8,128)S(1)} %pad_maximum_fusion.refs_0_), channel_id=1, source_target_pairs={{0,1},{1,2},{2,3},{3,0},{4,5},{5,6},{6,7},{7,4},{8,9},{9,10},{10,1... | collective-permute-start | bytes 1572872 | tf_op jit(solution)/shard_map/ppermute | solution.py:76
  61.1 14.7 %collective-permute-start.16 = (f32[2,512,128]{2,1,0:T(8,128)S(1)}, f32[2,512,128]{2,1,0:T(8,128)S(1)}, u32[]{:S(2)}, u32[]{:S(2)}) collective-permute-start(f32[2,512,128]{2,1,0:T(8,128)S(1)} %collective-permute-done.15.refs_2_), channel_id=1, source_target_pairs={{0,16},{1,17},{2,18},{3,19},{4,20},{5,21},{6,22},{7,23},{8,24},{9,... | collective-permute-start | bytes 1572872 | tf_op jit(solution)/shard_map/ppermute | solution.py:76
  71.9 7.4 %collective-permute-start.10 = (f32[2,512,128]{2,1,0:T(8,128)S(1)}, f32[2,512,128]{2,1,0:T(8,128)S(1)}, u32[]{:S(2)}, u32[]{:S(2)}) collective-permute-start(f32[2,512,128]{2,1,0:T(8,128)S(1)} %collective-permute-done.9.refs_1_), channel_id=1, source_target_pairs={{0,16},{1,17},{2,18},{3,19},{4,20},{5,21},{6,22},{7,23},{8,24},{9,... | collective-permute-start | bytes 1572872 | tf_op jit(solution)/shard_map/ppermute | solution.py:76
  71.9 7.4 %collective-permute-start.8 = (f32[2,512,128]{2,1,0:T(8,128)S(1)}, f32[2,512,128]{2,1,0:T(8,128)S(1)}, u32[]{:S(2)}, u32[]{:S(2)}) collective-permute-start(f32[2,512,128]{2,1,0:T(8,128)S(1)} %collective-permute-done.7.refs_0_), channel_id=1, source_target_pairs={{0,16},{1,17},{2,18},{3,19},{4,20},{5,21},{6,22},{7,23},{8,24},{9,... | collective-permute-start | bytes 1572872 | tf_op jit(solution)/shard_map/ppermute | solution.py:76

commit v6 on v5

--- a/solution.py
+++ b/solution.py
@@ -80,40 +80,34 @@
     return pltpu.with_memory_space_constraint(value, pltpu.VMEM)
 
 
-def payload_kernel(info, front, beside, *refs):
+def payload_kernel(info, front, *refs):
     outs, sems = refs[:-1], refs[-1]
-
-    def copies(source, half):
-        made = []
-        for at, (delta, out) in enumerate(zip(DELTAS, outs)):
-            begin = pl.multiple_of((info[1] + delta) % 4 * SHARE + half * (ROWS // 2), SHARE)
-            pivots, rows = source.at[half * DPART : (half + 1) * DPART, :], source.at[pl.ds(begin, SHARE), :]
-            made.append(pltpu.make_async_copy(pivots, out.at[0:DPART, :], sems.at[2 * at]))
-            made.append(pltpu.make_async_copy(rows, out.at[DPART:, :], sems.at[2 * at + 1]))
-        return made
-
-    for half, source in enumerate((front, beside)):
-        @pl.when(info[0] == half)
-        def _():
-            for copy in copies(source, half):
-                copy.start()
-
-    for copy in copies(front, 0):
+    made = []
+    for at, out in enumerate(outs):
+        delta, half = DELTAS[at // 2], at % 2
+        begin = pl.multiple_of((info[0] + delta) % 4 * SHARE + half * (ROWS // 2), SHARE)
+        pivots, rows = front.at[half * DPART : (half + 1) * DPART, :], front.at[pl.ds(begin, SHARE), :]
+        made.append(pltpu.make_async_copy(pivots, out.at[0:DPART, :], sems.at[2 * at]))
+        made.append(pltpu.make_async_copy(rows, out.at[DPART:, :], sems.at[2 * at + 1]))
+    for copy in made:
+        copy.start()
+    for copy in made:
         copy.wait()
 
 
-def payloads(info, front, beside):
-    hbm = pl.BlockSpec(memory_space=pltpu.HBM)
+def payloads(info, front):
+    count = 2 * len(DELTAS)
     front = pltpu.with_memory_space_constraint(front, pltpu.HBM)
-    return pl.pallas_call(
+    out = pl.pallas_call(
         payload_kernel,
-        out_shape=tuple(pltpu.VMEM((DPART + SHARE, WIDTH), jnp.float32) for _ in DELTAS),
-        in_specs=[pl.BlockSpec(memory_space=pltpu.SMEM), hbm, pl.BlockSpec(memory_space=pltpu.VMEM)],
-        out_specs=tuple(pl.BlockSpec(memory_space=pltpu.VMEM) for _ in DELTAS),
-        scratch_shapes=[pltpu.SemaphoreType.DMA((2 * len(DELTAS),))],
+        out_shape=tuple(pltpu.VMEM((DPART + SHARE, WIDTH), jnp.float32) for _ in range(count)),
+        in_specs=[pl.BlockSpec(memory_space=pltpu.SMEM), pl.BlockSpec(memory_space=pltpu.HBM)],
+        out_specs=tuple(pl.BlockSpec(memory_space=pltpu.VMEM) for _ in range(count)),
+        scratch_shapes=[pltpu.SemaphoreType.DMA((2 * count,))],
         compiler_params=pltpu.CompilerParams(vmem_limit_bytes=4 << 20),
         name="payloads",
-    )(info, front, in_vmem(beside))
+    )(info, front)
+    return out[0::2], out[1::2]
 
 
 def split3(value):
@@ -273,11 +267,15 @@
     panel = (x == 0) & (z == 0) & (y < 2) & (core == 0)
     info = jnp.stack([core, panel.astype(jnp.int32), y, row]).astype(jnp.int32)
 
-    beside = send(front, CORE_SWAP)
-    to_up, to_down, to_side, to_self = payloads(jnp.stack([core, mine]).astype(jnp.int32), front, beside)
-    up = send(to_up, shift(1, 0))
-    down = send(to_down, shift(-1, 0))
-    side = send(to_side, SIDE)
+    kept, given = payloads(mine.reshape(1).astype(jnp.int32), front)
+
+    def payload(at):
+        return jnp.where(core == 0, kept[at], send(given[at], CORE_SWAP))
+
+    up = send(payload(0), shift(1, 0))
+    down = send(payload(1), shift(-1, 0))
+    side = send(payload(2), SIDE)
+    to_self = payload(3)
     near = y < 2
     held = jnp.where((z == 1) & near, up, jnp.where((z == 3) & near, down, jnp.where(near, to_self, side)))
     held = jnp.where(x == 0, held, send(held, X_SWAP))

time: 83.2 us -> 85.2 us (1.024)
  waiting for transfers between devices: 31.4 us -> 39.3 us
  starting transfers between devices: 31.3 us -> 24.8 us
    ppermute x18 -> x21, waiting for transfers between devices: 31.4 us -> 39.3 us  [send(): return lax.ppermute(value, AXES, pairs)]
    ppermute x18 -> x21, starting transfers between devices: 31.3 us -> 24.8 us  [send(): return lax.ppermute(value, AXES, pairs)]
  transfers between devices with their start and end apart: 18 -> 21, of which waited for: 9 -> 12; matrix products, arithmetic and copies ran while one was open for 3% -> 3% of each run, Pallas kernels for 15% -> 14%
where the time goes in v6:
time: 85.2 us; the launch traced here: 83.7 us
  waiting for transfers between devices  39.3 us (46%)
  starting transfers between devices  24.8 us (29%)
  Pallas kernels  16.7 us (20%)
  other arithmetic  1.45 us (2%)
  local copies, waits for them, and re-layouts  1.11 us (1%)
    ppermute x21, waiting for transfers between devices, send(): return lax.ppermute(value, AXES, pairs)  39.3 us
    ppermute x21, starting transfers between devices, send(): return lax.ppermute(value, AXES, pairs)  24.8 us
    pallas_call x3, Pallas kernels, apply_update(): pl.pallas_call(update_kernel, out_shape=jax.ShapeDtypeStruct((ROWS, WIDTH...  9.67 us
    pallas_call x1, Pallas kernels, factor(): pl.pallas_call(factor_kernel, out_shape=(pltpu.VMEM((P_SIZE, 2 * WIDTH),...  5.23 us
    pallas_call x1, Pallas kernels, payloads(): pl.pallas_call(payload_kernel, out_shape=tuple((pltpu.VMEM((DPART + SHARE...  1.83 us
  transfers between devices with their start and end apart: 21, of which 12 were waited for; matrix products, arithmetic and copies ran while one was open for 3% of the time, Pallas kernels for 14%

profile of v6, /device:TPU:0, one launch (start us, length us, event | category | flops | bytes accessed | tf_op | source)
XLA Modules:
  0.0 83.7 jit_solution(10992677032113229784)
XLA Ops:
  0.0 1.8 %payloads.1 = (f32[640,128]{1,0:T(8,128)S(1)}, f32[640,128]{1,0:T(8,128)S(1)}, f32[640,128]{1,0:T(8,128)S(1)}, f32[640,128]{1,0:T(8,128)S(1)}, f32[640,128]{1,0:...) custom-call(s32[1]{0:T(128)} %bitcast.4.info, f32[4096,128]{1,0:T(8,128)} %front.7), custom_call_target="tpu_custom_call" | custom-call | tf_op jit(solution)/shard_map/payloads/pallas_call | solution.py:101
  1.9 0.5 collective-permute-start.2
  2.5 0.4 collective-permute-start.4
  2.9 0.7 collective-permute-done.5
  3.7 3.2 %collective-permute-start.6 = (f32[640,128]{1,0:T(8,128)S(1)}, f32[640,128]{1,0:T(8,128)}, u32[]{:S(2)}, u32[]{:S(2)}) collective-permute-start(f32[640,128]{1,0:T(8,128)S(1)} %broadcast_select_fusion), channel_id=1, source_target_pairs={{0,3},{1,2},{2,1},{3,0},{4,7},{5,6},{6,5},{7,4},{8,11},{9,10},{10,... | collective-permute-start | bytes 983048 | tf_op jit(solution)/shard_map/ppermute | solution.py:76
  7.0 4.1 %collective-permute-start.3 = (f32[640,128]{1,0:T(8,128)S(1)}, f32[640,128]{1,0:T(8,128)S(1)}, u32[]{:S(2)}, u32[]{:S(2)}) collective-permute-start(f32[640,128]{1,0:T(8,128)S(1)} %broadcast_select_fusion.1), channel_id=1, source_target_pairs={{0,12},{1,13},{2,14},{3,15},{4,0},{5,1},{6,2},{7,3},{8,4},{9,5},{1... | collective-permute-start | bytes 983048 | tf_op jit(solution)/shard_map/ppermute | solution.py:76
  11.2 4.2 %collective-permute-done.6 = f32[640,128]{1,0:T(8,128)} collective-permute-done((f32[640,128]{1,0:T(8,128)S(1)}, f32[640,128]{1,0:T(8,128)}, u32[]{:S(2)}, u32[]{:S(2)}) %collective-permute-start.6) | collective-permute-done | bytes 327712 | tf_op jit(solution)/shard_map/ppermute | solution.py:76
  15.4 3.6 %collective-permute-done.3 = f32[640,128]{1,0:T(8,128)S(1)} collective-permute-done((f32[640,128]{1,0:T(8,128)S(1)}, f32[640,128]{1,0:T(8,128)S(1)}, u32[]{:S(2)}, u32[]{:S(2)}) %collective-permute-start.3) | collective-permute-done | bytes 327712 | tf_op jit(solution)/shard_map/ppermute | solution.py:76
  19.0 3.5 %collective-permute-done.1 = f32[640,128]{1,0:T(8,128)S(1)} collective-permute-done((f32[640,128]{1,0:T(8,128)S(1)}, f32[640,128]{1,0:T(8,128)S(1)}, u32[]{:S(2)}, u32[]{:S(2)}) %collective-permute-start.1) | collective-permute-done | bytes 327712 | tf_op jit(solution)/shard_map/ppermute | solution.py:76
  22.6 1.6 %collective-permute-start.7 = (f32[640,128]{1,0:T(8,128)S(1)}, f32[640,128]{1,0:T(8,128)S(1)}, u32[]{:S(2)}, u32[]{:S(2)}) collective-permute-start(f32[640,128]{1,0:T(8,128)S(1)} %select_select_fusion), channel_id=1, source_target_pairs={{0,32},{1,33},{2,34},{3,35},{4,36},{5,37},{6,38},{7,39},{8,40},{9,... | collective-permute-start | bytes 983048 | tf_op jit(solution)/shard_map/ppermute | solution.py:76
  24.2 8.8 %collective-permute-done.7 = f32[640,128]{1,0:T(8,128)S(1)} collective-permute-done((f32[640,128]{1,0:T(8,128)S(1)}, f32[640,128]{1,0:T(8,128)S(1)}, u32[]{:S(2)}, u32[]{:S(2)}) %collective-permute-start.7) | collective-permute-done | bytes 327712 | tf_op jit(solution)/shard_map/ppermute | solution.py:76
  33.0 1.3 %collective-permute-start.8 = (f32[640,128]{1,0:T(8,128)S(1)}, f32[640,128]{1,0:T(8,128)S(1)}, u32[]{:S(2)}, u32[]{:S(2)}) collective-permute-start(f32[640,128]{1,0:T(8,128)S(1)} %broadcast_select_fusion.3), channel_id=1, source_target_pairs={{0,9},{2,11},{4,6},{13,15},{3,10},{1,8},{12,14},{5,7},{16,25},{18,... | collective-permute-start | bytes 983048 | tf_op jit(solution)/shard_map/ppermute | solution.py:76
  34.4 0.9 %slice.12 = f32[256,128]{1,0:T(8,128)S(1)} slice(f32[4096,128]{1,0:T(8,128)} %front.7), slice={[0:256], [0:128]} | slice | bytes 262144 | tf_op jit(solution)/shard_map/slice | solution.py:286
  35.3 3.1 %collective-permute-start.17 = (f32[256,128]{1,0:T(8,128)S(1)}, f32[256,128]{1,0:T(8,128)S(1)}, u32[]{:S(2)}, u32[]{:S(2)}) collective-permute-start(f32[256,128]{1,0:T(8,128)S(1)} %slice.12), channel_id=1, source_target_pairs={{0,64},{1,65},{2,66},{3,67},{4,68},{5,69},{6,70},{7,71},{8,72},{9,... | collective-permute-start | bytes 393224 | tf_op jit(solution)/shard_map/ppermute | solution.py:76
  38.5 3.1 %collective-permute-done.8 = f32[640,128]{1,0:T(8,128)S(1)} collective-permute-done((f32[640,128]{1,0:T(8,128)S(1)}, f32[640,128]{1,0:T(8,128)S(1)}, u32[]{:S(2)}, u32[]{:S(2)}) %collective-permute-start.8) | collective-permute-done | bytes 327712 | tf_op jit(solution)/shard_map/ppermute | solution.py:76
  41.6 3.1 %collective-permute-start.14 = (f32[128,128]{1,0:T(8,128)S(1)}, f32[128,128]{1,0:T(8,128)S(1)}, u32[]{:S(2)}, u32[]{:S(2)}) collective-permute-start(f32[128,128]{1,0:T(8,128)S(1)} %slice.14), channel_id=1, source_target_pairs={{0,64},{1,65},{2,66},{3,67},{4,68},{5,69},{6,70},{7,71},{8,72},{9,... | collective-permute-start | bytes 196616 | tf_op jit(solution)/shard_map/ppermute | solution.py:76
  44.7 1.3 %collective-permute-start.9 = (f32[512,128]{1,0:T(8,128)S(1)}, f32[512,128]{1,0:T(8,128)S(1)}, u32[]{:S(2)}, u32[]{:S(2)}) collective-permute-start(f32[512,128]{1,0:T(8,128)S(1)} %slice.13), channel_id=1, source_target_pairs={{0,2},{2,0},{9,11},{11,9},{4,13},{13,4},{6,15},{15,6},{3,1},{1,3},... | collective-permute-start | bytes 786440 | tf_op jit(solution)/shard_map/ppermute | solution.py:76
  46.3 1.2 %collective-permute-done.14 = f32[128,128]{1,0:T(8,128)S(1)} collective-permute-done((f32[128,128]{1,0:T(8,128)S(1)}, f32[128,128]{1,0:T(8,128)S(1)}, u32[]{:S(2)}, u32[]{:S(2)}) %collective-permute-start.14) | collective-permute-done | bytes 65568 | tf_op jit(solution)/shard_map/ppermute | solution.py:76
  47.5 1.4 %collective-permute-start.15 = (f32[128,128]{1,0:T(8,128)S(1)}, f32[128,128]{1,0:T(8,128)S(1)}, u32[]{:S(2)}, u32[]{:S(2)}) collective-permute-start(f32[128,128]{1,0:T(8,128)S(1)} %broadcast_select_fusion.6), channel_id=1, source_target_pairs={{0,2},{2,0},{9,11},{11,9},{4,13},{13,4},{6,15},{15,6},{3,1},{1,3},... | collective-permute-start | bytes 196616 | tf_op jit(solution)/shard_map/ppermute | solution.py:76
  48.9 5.2 %collective-permute-done.9 = f32[512,128]{1,0:T(8,128)S(1)} collective-permute-done((f32[512,128]{1,0:T(8,128)S(1)}, f32[512,128]{1,0:T(8,128)S(1)}, u32[]{:S(2)}, u32[]{:S(2)}) %collective-permute-start.9) | collective-permute-done | bytes 262176 | tf_op jit(solution)/shard_map/ppermute | solution.py:76
  54.2 0.5 collective-permute-done.15
  54.9 0.9 %broadcast_select_fusion.5.top = f32[256,128]{1,0:T(8,128)S(1)} fusion(f32[256,128]{1,0:T(8,128)S(1)} %collective-permute-done.17, pred[]{:T(512)S(6)} %eq.66, f32[4096,128]{1,0:T(8,128)} %front.7), kind=kLoop, calls=%fused_computation.12 | loop fusion | flops 32768 | bytes 393217 | tf_op jit(solution)/shard_map/jit(_where)/select_n | solution.py:286
  55.8 0.6 collective-permute-start.20
  56.4 2.7 %collective-permute-start.10 = (f32[2,512,128]{2,1,0:T(8,128)S(1)}, f32[2,512,128]{2,1,0:T(8,128)S(1)}, u32[]{:S(2)}, u32[]{:S(2)}) collective-permute-start(f32[2,512,128]{2,1,0:T(8,128)S(1)} %pad_maximum_fusion.refs_0_), channel_id=1, source_target_pairs={{0,12},{1,13},{2,14},{3,15},{4,0},{5,1},{6,2},{7,3},{8,4},{9,5},{1... | collective-permute-start | bytes 1572872 | tf_op jit(solution)/shard_map/ppermute | solution.py:76
  59.1 1.1 %collective-permute-start.12 = (f32[2,512,128]{2,1,0:T(8,128)S(1)}, f32[2,512,128]{2,1,0:T(8,128)S(1)}, u32[]{:S(2)}, u32[]{:S(2)}) collective-permute-start(f32[2,512,128]{2,1,0:T(8,128)S(1)} %pad_maximum_fusion.refs_0_), channel_id=1, source_target_pairs={{0,1},{1,2},{2,3},{3,0},{4,5},{5,6},{6,7},{7,4},{8,9},{9,10},{10,1... | collective-permute-start | bytes 1572872 | tf_op jit(solution)/shard_map/ppermute | solution.py:76
  60.2 6.5 %collective-permute-done.18.refs_2_ = f32[2,512,128]{2,1,0:T(8,128)S(1)} collective-permute-done((f32[2,512,128]{2,1,0:T(8,128)S(1)}, f32[2,512,128]{2,1,0:T(8,128)S(1)}, u32[]{:S(2)}, u32[]{:S(2)}) %collective-permute-start.18) | collective-permute-done | bytes 524320 | tf_op jit(solution)/shard_map/ppermute | solution.py:76
  66.7 5.2 %factor.1 = (bf16[256,256]{1,0:T(8,128)(2,1)S(1)}, f32[256,128]{1,0:T(8,128)}) custom-call(s32[4]{0:T(128)S(1)} %pad_add_fusion.1.info, f32[2,128,128]{2,1,0:T(8,128)S(1)} %pad_maximum_fusion.1.d_mine, f32[2,128,128]{2,1,0:T(8,128)S(1)} %collective-permute-done.16.d_other, f32[256,128]{1,0:T(8,128)S(1)} %broadcast_select_fusion.5.top), custom_call_target="tpu_custom_call" | custom-call | flops 8999999488 | bytes 2000000 | tf_op jit(solution)/shard_map/factor/pallas_call | solution.py:192
  71.9 0.6 collective-permute-done.10.refs_0_
  72.5 1.4 %collective-permute-done.12.refs_1_ = f32[2,512,128]{2,1,0:T(8,128)S(1)} collective-permute-done((f32[2,512,128]{2,1,0:T(8,128)S(1)}, f32[2,512,128]{2,1,0:T(8,128)S(1)}, u32[]{:S(2)}, u32[]{:S(2)}) %collective-permute-start.12) | collective-permute-done | bytes 524320 | tf_op jit(solution)/shard_map/ppermute | solution.py:76
  73.9 3.5 %shard_map.17.refs_5_ = f32[4096,128]{1,0:T(8,128)} custom-call(s32[5]{0:T(128)S(1)} %stack.97.info, f32[4096,128]{1,0:T(8,128)} %front.7, f32[2,512,128]{2,1,0:T(8,128)S(1)} %pad_maximum_fusion.refs_0_, f32[2,512,128]{2,1,0:T(8,128)S(1)} %collective-permute-done.20.refs_1_, f32[2,512,128]{2,1,0:T(8,128)S(1)} %collective-permute-done.18.refs_2_, ...), custom_call_target="tpu_custom_call" | custom-call | flops 3000000000 | bytes 4000000 | tf_op jit(solution)/shard_map/pallas_call | solution.py:246
  77.4 3.4 %shard_map.18.refs_4_ = f32[4096,128]{1,0:T(8,128)} custom-call(s32[5]{0:T(128)S(1)} %stack.93.info, f32[4096,128]{1,0:T(8,128)} %front.7, f32[2,512,128]{2,1,0:T(8,128)S(1)} %collective-permute-done.10.refs_0_, f32[2,512,128]{2,1,0:T(8,128)S(1)} %collective-permute-done.12.refs_1_, ...), custom_call_target="tpu_custom_call", output_to_operand_aliasing={{}: (7, {})} | custom-call | flops 3000000000 | bytes 4000000 | tf_op jit(solution)/shard_map/pallas_call | solution.py:246
  80.8 2.9 %shard_map.19 = f32[4096,128]{1,0:T(8,128)} custom-call(s32[4]{0:T(128)S(1)} %pad_add_fusion.info, f32[4096,128]{1,0:T(8,128)} %front.7, f32[2,512,128]{2,1,0:T(8,128)S(1)} %collective-permute-done.11.refs_0_, f32[2,512,128]{2,1,0:T(8,128)S(1)} %collective-permute-done.13.refs_1_, ...), custom_call_target="tpu_custom_call", output_to_operand_aliasing={{}: (6, {})} | custom-call | flops 3000000000 | bytes 4000000 | tf_op jit(solution)/shard_map/pallas_call | solution.py:246
  (34 shorter events, 1.2 us)
Async XLA Ops:
  1.8 1.8 %collective-permute-start.5 = (f32[640,128]{1,0:T(8,128)S(1)}, f32[640,128]{1,0:T(8,128)}, u32[]{:S(2)}, u32[]{:S(2)}) collective-permute-start(f32[640,128]{1,0:T(8,128)S(1)} %get-tuple-element.22), channel_id=1, source_target_pairs={{0,16},{1,17},{2,18},{3,19},{4,20},{5,21},{6,22},{7,23},{8,24},{9,... | collective-permute-start | bytes 983048 | tf_op jit(solution)/shard_map/ppermute | solution.py:76
  1.9 5.0 %collective-permute-start.2 = (f32[640,128]{1,0:T(8,128)S(1)}, f32[640,128]{1,0:T(8,128)S(1)}, u32[]{:S(2)}, u32[]{:S(2)}) collective-permute-start(f32[640,128]{1,0:T(8,128)S(1)} %get-tuple-element.18), channel_id=1, source_target_pairs={{0,16},{1,17},{2,18},{3,19},{4,20},{5,21},{6,22},{7,23},{8,24},{9,... | collective-permute-start | bytes 983048 | tf_op jit(solution)/shard_map/ppermute | solution.py:76
  2.4 8.7 %collective-permute-start = (f32[640,128]{1,0:T(8,128)S(1)}, f32[640,128]{1,0:T(8,128)S(1)}, u32[]{:S(2)}, u32[]{:S(2)}) collective-permute-start(f32[640,128]{1,0:T(8,128)S(1)} %get-tuple-element.16), channel_id=1, source_target_pairs={{0,16},{1,17},{2,18},{3,19},{4,20},{5,21},{6,22},{7,23},{8,24},{9,... | collective-permute-start | bytes 983048 | tf_op jit(solution)/shard_map/ppermute | solution.py:76
  2.5 8.7 %collective-permute-start.4 = (f32[640,128]{1,0:T(8,128)S(1)}, f32[640,128]{1,0:T(8,128)}, u32[]{:S(2)}, u32[]{:S(2)}) collective-permute-start(f32[640,128]{1,0:T(8,128)S(1)} %get-tuple-element.20), channel_id=1, source_target_pairs={{0,16},{1,17},{2,18},{3,19},{4,20},{5,21},{6,22},{7,23},{8,24},{9,... | collective-permute-start | bytes 983048 | tf_op jit(solution)/shard_map/ppermute | solution.py:76
  3.7 11.7 %collective-permute-start.6 = (f32[640,128]{1,0:T(8,128)S(1)}, f32[640,128]{1,0:T(8,128)}, u32[]{:S(2)}, u32[]{:S(2)}) collective-permute-start(f32[640,128]{1,0:T(8,128)S(1)} %broadcast_select_fusion), channel_id=1, source_target_pairs={{0,3},{1,2},{2,1},{3,0},{4,7},{5,6},{6,5},{7,4},{8,11},{9,10},{10,... | collective-permute-start | bytes 983048 | tf_op jit(solution)/shard_map/ppermute | solution.py:76
  7.0 12.1 %collective-permute-start.3 = (f32[640,128]{1,0:T(8,128)S(1)}, f32[640,128]{1,0:T(8,128)S(1)}, u32[]{:S(2)}, u32[]{:S(2)}) collective-permute-start(f32[640,128]{1,0:T(8,128)S(1)} %broadcast_select_fusion.1), channel_id=1, source_target_pairs={{0,12},{1,13},{2,14},{3,15},{4,0},{5,1},{6,2},{7,3},{8,4},{9,5},{1... | collective-permute-start | bytes 983048 | tf_op jit(solution)/shard_map/ppermute | solution.py:76
  11.1 11.4 %collective-permute-start.1 = (f32[640,128]{1,0:T(8,128)S(1)}, f32[640,128]{1,0:T(8,128)S(1)}, u32[]{:S(2)}, u32[]{:S(2)}) collective-permute-start(f32[640,128]{1,0:T(8,128)S(1)} %broadcast_select_fusion.2), channel_id=1, source_target_pairs={{0,4},{1,5},{2,6},{3,7},{4,8},{5,9},{6,10},{7,11},{8,12},{9,13},{1... | collective-permute-start | bytes 983048 | tf_op jit(solution)/shard_map/ppermute | solution.py:76
  22.6 10.3 %collective-permute-start.7 = (f32[640,128]{1,0:T(8,128)S(1)}, f32[640,128]{1,0:T(8,128)S(1)}, u32[]{:S(2)}, u32[]{:S(2)}) collective-permute-start(f32[640,128]{1,0:T(8,128)S(1)} %select_select_fusion), channel_id=1, source_target_pairs={{0,32},{1,33},{2,34},{3,35},{4,36},{5,37},{6,38},{7,39},{8,40},{9,... | collective-permute-start | bytes 983048 | tf_op jit(solution)/shard_map/ppermute | solution.py:76
  33.0 8.5 %collective-permute-start.8 = (f32[640,128]{1,0:T(8,128)S(1)}, f32[640,128]{1,0:T(8,128)S(1)}, u32[]{:S(2)}, u32[]{:S(2)}) collective-permute-start(f32[640,128]{1,0:T(8,128)S(1)} %broadcast_select_fusion.3), channel_id=1, source_target_pairs={{0,9},{2,11},{4,6},{13,15},{3,10},{1,8},{12,14},{5,7},{16,25},{18,... | collective-permute-start | bytes 983048 | tf_op jit(solution)/shard_map/ppermute | solution.py:76
  35.3 19.6 %collective-permute-start.17 = (f32[256,128]{1,0:T(8,128)S(1)}, f32[256,128]{1,0:T(8,128)S(1)}, u32[]{:S(2)}, u32[]{:S(2)}) collective-permute-start(f32[256,128]{1,0:T(8,128)S(1)} %slice.12), channel_id=1, source_target_pairs={{0,64},{1,65},{2,66},{3,67},{4,68},{5,69},{6,70},{7,71},{8,72},{9,... | collective-permute-start | bytes 393224 | tf_op jit(solution)/shard_map/ppermute | solution.py:76
  41.6 5.8 %collective-permute-start.14 = (f32[128,128]{1,0:T(8,128)S(1)}, f32[128,128]{1,0:T(8,128)S(1)}, u32[]{:S(2)}, u32[]{:S(2)}) collective-permute-start(f32[128,128]{1,0:T(8,128)S(1)} %slice.14), channel_id=1, source_target_pairs={{0,64},{1,65},{2,66},{3,67},{4,68},{5,69},{6,70},{7,71},{8,72},{9,... | collective-permute-start | bytes 196616 | tf_op jit(solution)/shard_map/ppermute | solution.py:76
  44.7 9.4 %collective-permute-start.9 = (f32[512,128]{1,0:T(8,128)S(1)}, f32[512,128]{1,0:T(8,128)S(1)}, u32[]{:S(2)}, u32[]{:S(2)}) collective-permute-start(f32[512,128]{1,0:T(8,128)S(1)} %slice.13), channel_id=1, source_target_pairs={{0,2},{2,0},{9,11},{11,9},{4,13},{13,4},{6,15},{15,6},{3,1},{1,3},... | collective-permute-start | bytes 786440 | tf_op jit(solution)/shard_map/ppermute | solution.py:76
  47.5 7.3 %collective-permute-start.15 = (f32[128,128]{1,0:T(8,128)S(1)}, f32[128,128]{1,0:T(8,128)S(1)}, u32[]{:S(2)}, u32[]{:S(2)}) collective-permute-start(f32[128,128]{1,0:T(8,128)S(1)} %broadcast_select_fusion.6), channel_id=1, source_target_pairs={{0,2},{2,0},{9,11},{11,9},{4,13},{13,4},{6,15},{15,6},{3,1},{1,3},... | collective-permute-start | bytes 196616 | tf_op jit(solution)/shard_map/ppermute | solution.py:76
  54.2 12.5 %collective-permute-start.18 = (f32[2,512,128]{2,1,0:T(8,128)S(1)}, f32[2,512,128]{2,1,0:T(8,128)S(1)}, u32[]{:S(2)}, u32[]{:S(2)}) collective-permute-start(f32[2,512,128]{2,1,0:T(8,128)S(1)} %pad_maximum_fusion.refs_0_), channel_id=1, source_target_pairs={{0,4},{1,5},{2,6},{3,7},{4,8},{5,9},{6,10},{7,11},{8,12},{9,13},{1... | collective-permute-start | bytes 1572872 | tf_op jit(solution)/shard_map/ppermute | solution.py:76
  54.8 11.8 %collective-permute-start.16 = (f32[2,128,128]{2,1,0:T(8,128)S(1)}, f32[2,128,128]{2,1,0:T(8,128)S(1)}, u32[]{:S(2)}, u32[]{:S(2)}) collective-permute-start(f32[2,128,128]{2,1,0:T(8,128)S(1)} %pad_maximum_fusion.1.d_mine), channel_id=1, source_target_pairs={{0,16},{1,17},{2,18},{3,19},{4,20},{5,21},{6,22},{7,23},{8,24},{9,... | collective-permute-start | bytes 393224 | tf_op jit(solution)/shard_map/ppermute | solution.py:76
  55.8 18.1 %collective-permute-start.20 = (f32[2,512,128]{2,1,0:T(8,128)S(1)}, f32[2,512,128]{2,1,0:T(8,128)S(1)}, u32[]{:S(2)}, u32[]{:S(2)}) collective-permute-start(f32[2,512,128]{2,1,0:T(8,128)S(1)} %pad_maximum_fusion.refs_0_), channel_id=1, source_target_pairs={{0,16},{1,17},{2,18},{3,19},{4,20},{5,21},{6,22},{7,23},{8,24},{9,... | collective-permute-start | bytes 1572872 | tf_op jit(solution)/shard_map/ppermute | solution.py:76
  56.4 16.1 %collective-permute-start.10 = (f32[2,512,128]{2,1,0:T(8,128)S(1)}, f32[2,512,128]{2,1,0:T(8,128)S(1)}, u32[]{:S(2)}, u32[]{:S(2)}) collective-permute-start(f32[2,512,128]{2,1,0:T(8,128)S(1)} %pad_maximum_fusion.refs_0_), channel_id=1, source_target_pairs={{0,12},{1,13},{2,14},{3,15},{4,0},{5,1},{6,2},{7,3},{8,4},{9,5},{1... | collective-permute-start | bytes 1572872 | tf_op jit(solution)/shard_map/ppermute | solution.py:76
  59.1 14.8 %collective-permute-start.12 = (f32[2,512,128]{2,1,0:T(8,128)S(1)}, f32[2,512,128]{2,1,0:T(8,128)S(1)}, u32[]{:S(2)}, u32[]{:S(2)}) collective-permute-start(f32[2,512,128]{2,1,0:T(8,128)S(1)} %pad_maximum_fusion.refs_0_), channel_id=1, source_target_pairs={{0,1},{1,2},{2,3},{3,0},{4,5},{5,6},{6,7},{7,4},{8,9},{9,10},{10,1... | collective-permute-start | bytes 1572872 | tf_op jit(solution)/shard_map/ppermute | solution.py:76
  66.6 10.8 %collective-permute-start.19 = (f32[2,512,128]{2,1,0:T(8,128)S(1)}, f32[2,512,128]{2,1,0:T(8,128)S(1)}, u32[]{:S(2)}, u32[]{:S(2)}) collective-permute-start(f32[2,512,128]{2,1,0:T(8,128)S(1)} %collective-permute-done.18.refs_2_), channel_id=1, source_target_pairs={{0,16},{1,17},{2,18},{3,19},{4,20},{5,21},{6,22},{7,23},{8,24},{9,... | collective-permute-start | bytes 1572872 | tf_op jit(solution)/shard_map/ppermute | solution.py:76
  72.5 8.3 %collective-permute-start.11 = (f32[2,512,128]{2,1,0:T(8,128)S(1)}, f32[2,512,128]{2,1,0:T(8,128)S(1)}, u32[]{:S(2)}, u32[]{:S(2)}) collective-permute-start(f32[2,512,128]{2,1,0:T(8,128)S(1)} %collective-permute-done.10.refs_0_), channel_id=1, source_target_pairs={{0,16},{1,17},{2,18},{3,19},{4,20},{5,21},{6,22},{7,23},{8,24},{9,... | collective-permute-start | bytes 1572872 | tf_op jit(solution)/shard_map/ppermute | solution.py:76
  73.9 6.9 %collective-permute-start.13 = (f32[2,512,128]{2,1,0:T(8,128)S(1)}, f32[2,512,128]{2,1,0:T(8,128)S(1)}, u32[]{:S(2)}, u32[]{:S(2)}) collective-permute-start(f32[2,512,128]{2,1,0:T(8,128)S(1)} %collective-permute-done.12.refs_1_), channel_id=1, source_target_pairs={{0,16},{1,17},{2,18},{3,19},{4,20},{5,21},{6,22},{7,23},{8,24},{9,... | collective-permute-start | bytes 1572872 | tf_op jit(solution)/shard_map/ppermute | solution.py:76

commit v7 on v5

--- a/solution.py
+++ b/solution.py
@@ -64,7 +64,7 @@
     spread, trade = [], []
     for c in range(4):
         m = {int(member(z, y)): (z, y) for z, y in ALL_ZY if coset(z, y) == c}
-        spread += [(m[0], m[2]), (m[1], m[3])]
+        spread += [(m[0], m[2]), (m[1], m[3]), (m[2], m[0]), (m[3], m[1])]
         trade += [(m[0], m[1]), (m[1], m[0]), (m[2], m[3]), (m[3], m[2])]
     return everywhere(spread), everywhere(trade)
 
@@ -183,7 +183,8 @@
     def finish(update):
         high = update.astype(jnp.bfloat16)
         low = (update - high.astype(jnp.float32)).astype(jnp.bfloat16)
-        update_out[...] = jnp.concatenate([high, low], axis=1)
+        both = jnp.concatenate([high, low], axis=1)
+        update_out[...] = jnp.concatenate([both, both], axis=0)
 
     for case, side in enumerate(sides):
         @pl.when(kind == case)
@@ -197,7 +198,7 @@
     vmem = pl.BlockSpec(memory_space=pltpu.VMEM)
     return pl.pallas_call(
         factor_kernel,
-        out_shape=(pltpu.VMEM((P_SIZE, 2 * WIDTH), jnp.bfloat16), pltpu.HBM((P_SIZE, WIDTH), jnp.float32)),
+        out_shape=(pltpu.VMEM((2 * P_SIZE, 2 * WIDTH), jnp.bfloat16), pltpu.HBM((P_SIZE, WIDTH), jnp.float32)),
         in_specs=[pl.BlockSpec(memory_space=pltpu.SMEM), vmem, vmem, vmem],
         out_specs=(vmem, pl.BlockSpec(memory_space=pltpu.HBM)),
         scratch_shapes=[pltpu.VMEM((2 * P_SIZE, P_SIZE + WIDTH), jnp.float32), pltpu.SemaphoreType.DMA],
@@ -218,31 +219,35 @@
         rows = pl.ds(pl.multiple_of(info[2 + at] * SHARE, SHARE), SHARE)
         return pltpu.make_async_copy(front.at[rows, :], blocks.at[at], loads.at[at])
 
-    def store(at):
-        rows = pl.ds(pl.multiple_of(info[2 + at] * SHARE, SHARE), SHARE)
-        return pltpu.make_async_copy(blocks.at[at], out.at[rows, :], stores.at[at])
+    def store(at, half):
+        begin = pl.multiple_of(info[2 + at] * SHARE + half * P_SIZE, P_SIZE)
+        mine = blocks.at[at, half * P_SIZE : (half + 1) * P_SIZE, :]
+        return pltpu.make_async_copy(mine, out.at[pl.ds(begin, P_SIZE), :], stores.at[at, half])
 
     for at in range(count):
         load(at).start()
         pl.when(has_top[at])(top_load.start)
     for at in range(count):
-        panel = jnp.concatenate([parts[at][0], parts[at][1]], axis=1)
-        high = panel.astype(jnp.bfloat16)
-        low = (panel - high.astype(jnp.float32)).astype(jnp.bfloat16)
-        both = jnp.dot(high, update[...], preferred_element_type=jnp.float32)
-        both = both + jnp.dot(low, update[...], preferred_element_type=jnp.float32)
-        added = both[:, :WIDTH] + both[:, WIDTH:]
-        load(at).wait()
-        blocks[at] = jnp.where(info[0] == 0, blocks[at], 0.0) + added
-
-        @pl.when(has_top[at])
-        def _():
-            top_load.wait()
-            blocks[at, 0:P_SIZE, :] = top_rows[...]
-
-        store(at).start()
+        for half in range(2):
+            rows = slice(half * P_SIZE, (half + 1) * P_SIZE)
+            panel = jnp.concatenate([parts[at][0, rows, :], parts[at][1, rows, :]], axis=1)
+            high = panel.astype(jnp.bfloat16)
+            low = (panel - high.astype(jnp.float32)).astype(jnp.bfloat16)
+            both = jnp.dot(jnp.concatenate([high, low], axis=1), update[...], preferred_element_type=jnp.float32)
+            added = both[:, :WIDTH] + both[:, WIDTH:]
+            if half == 0:
+                load(at).wait()
+            blocks[at, rows, :] = jnp.where(info[0] == 0, blocks[at, rows, :], 0.0) + added
+            if half == 0:
+                @pl.when(has_top[at])
+                def _():
+                    top_load.wait()
+                    blocks[at, 0:P_SIZE, :] = top_rows[...]
+
+            store(at, half).start()
     for at in range(count):
-        store(at).wait()
+        for half in range(2):
+            store(at, half).wait()
 
 
 def apply_update(info, front, parts, update, top, done=None):
@@ -258,7 +263,7 @@
             pltpu.VMEM((count, SHARE, WIDTH), jnp.float32),
             pltpu.VMEM((P_SIZE, WIDTH), jnp.float32),
             pltpu.SemaphoreType.DMA((count,)),
-            pltpu.SemaphoreType.DMA((count,)),
+            pltpu.SemaphoreType.DMA((count, 2)),
             pltpu.SemaphoreType.DMA,
         ],
         input_output_aliases={} if done is None else {count + 4: 0},

time: 83.2 us -> 81.1 us (0.975)
  starting transfers between devices: 31.3 us -> 25.4 us
  waiting for transfers between devices: 31.4 us -> 35.5 us
    ppermute x18, starting transfers between devices: 31.3 us -> 25.4 us  [send(): return lax.ppermute(value, AXES, pairs)]
    ppermute x18, waiting for transfers between devices: 31.4 us -> 35.5 us  [send(): return lax.ppermute(value, AXES, pairs)]
  transfers between devices with their start and end apart: 18 -> 18, of which waited for: 9 -> 10; matrix products, arithmetic and copies ran while one was open for 3% -> 3% of each run, Pallas kernels for 15% -> 15%
where the time goes in v7:
time: 81.1 us; the launch traced here: 80 us
  waiting for transfers between devices  35.5 us (44%)
  starting transfers between devices  25.4 us (31%)
  Pallas kernels  16.4 us (20%)
  other arithmetic  1.4 us (2%)
  local copies, waits for them, and re-layouts  1.11 us (1%)
    ppermute x18, waiting for transfers between devices, send(): return lax.ppermute(value, AXES, pairs)  35.5 us
    ppermute x18, starting transfers between devices, send(): return lax.ppermute(value, AXES, pairs)  25.4 us
    pallas_call x3, Pallas kernels, apply_update(): pl.pallas_call(update_kernel, out_shape=jax.ShapeDtypeStruct((ROWS, WIDTH...  9.27 us
    pallas_call x1, Pallas kernels, factor(): pl.pallas_call(factor_kernel, out_shape=(pltpu.VMEM((2 * P_SIZE, 2 * WIDT...  5.23 us
    pallas_call x1, Pallas kernels, payloads(): pl.pallas_call(payload_kernel, out_shape=tuple((pltpu.VMEM((DPART + SHARE...  1.91 us
  transfers between devices with their start and end apart: 18, of which 10 were waited for; matrix products, arithmetic and copies ran while one was open for 3% of the time, Pallas kernels for 15%

profile of v7, /device:TPU:0, one launch (start us, length us, event | category | flops | bytes accessed | tf_op | source)
XLA Modules:
  0.0 80.0 jit_solution(1293423590416111904)
XLA Ops:
  0.1 4.3 %collective-permute-done.beside = f32[4096,128]{1,0:T(8,128)S(1)} collective-permute-done((f32[4096,128]{1,0:T(8,128)}, f32[4096,128]{1,0:T(8,128)S(1)}, u32[]{:S(2)}, u32[]{:S(2)}) %collective-permute-start) | collective-permute-done | bytes 2097184 | tf_op jit(solution)/shard_map/ppermute | solution.py:76
  4.4 1.9 %payloads.1 = (f32[640,128]{1,0:T(8,128)S(1)}, f32[640,128]{1,0:T(8,128)S(1)}, f32[640,128]{1,0:T(8,128)S(1)}, f32[640,128]{1,0:T(8,128)S(1)}) custom-call(s32[2]{0:T(128)S(1)} %pad_add_fusion.1.info, f32[4096,128]{1,0:T(8,128)} %front.7, f32[4096,128]{1,0:T(8,128)S(1)} %collective-permute-done.beside), custom_call_target="tpu_custom_call" | custom-call | tf_op jit(solution)/shard_map/payloads/pallas_call | solution.py:108
  6.3 2.1 %collective-permute-start.1 = (f32[640,128]{1,0:T(8,128)S(1)}, f32[640,128]{1,0:T(8,128)S(1)}, u32[]{:S(2)}, u32[]{:S(2)}) collective-permute-start(f32[640,128]{1,0:T(8,128)S(1)} %get-tuple-element.11), channel_id=1, source_target_pairs={{0,4},{1,5},{2,6},{3,7},{4,8},{5,9},{6,10},{7,11},{8,12},{9,13},{1... | collective-permute-start | bytes 983048 | tf_op jit(solution)/shard_map/ppermute | solution.py:76
  8.4 2.2 %collective-permute-start.2 = (f32[640,128]{1,0:T(8,128)S(1)}, f32[640,128]{1,0:T(8,128)S(1)}, u32[]{:S(2)}, u32[]{:S(2)}) collective-permute-start(f32[640,128]{1,0:T(8,128)S(1)} %get-tuple-element.12), channel_id=1, source_target_pairs={{0,12},{1,13},{2,14},{3,15},{4,0},{5,1},{6,2},{7,3},{8,4},{9,5},{1... | collective-permute-start | bytes 983048 | tf_op jit(solution)/shard_map/ppermute | solution.py:76
  10.6 3.0 %collective-permute-start.3 = (f32[640,128]{1,0:T(8,128)S(1)}, f32[640,128]{1,0:T(8,128)S(1)}, u32[]{:S(2)}, u32[]{:S(2)}) collective-permute-start(f32[640,128]{1,0:T(8,128)S(1)} %get-tuple-element.14), channel_id=1, source_target_pairs={{0,3},{1,2},{2,1},{3,0},{4,7},{5,6},{6,5},{7,4},{8,11},{9,10},{10,... | collective-permute-start | bytes 983048 | tf_op jit(solution)/shard_map/ppermute | solution.py:76
  13.6 4.1 %collective-permute-done.1 = f32[640,128]{1,0:T(8,128)S(1)} collective-permute-done((f32[640,128]{1,0:T(8,128)S(1)}, f32[640,128]{1,0:T(8,128)S(1)}, u32[]{:S(2)}, u32[]{:S(2)}) %collective-permute-start.1) | collective-permute-done | bytes 327712 | tf_op jit(solution)/shard_map/ppermute | solution.py:76
  17.7 2.8 %collective-permute-done.3 = f32[640,128]{1,0:T(8,128)S(1)} collective-permute-done((f32[640,128]{1,0:T(8,128)S(1)}, f32[640,128]{1,0:T(8,128)S(1)}, u32[]{:S(2)}, u32[]{:S(2)}) %collective-permute-start.3) | collective-permute-done | bytes 327712 | tf_op jit(solution)/shard_map/ppermute | solution.py:76
  20.6 1.6 %collective-permute-start.4 = (f32[640,128]{1,0:T(8,128)S(1)}, f32[640,128]{1,0:T(8,128)S(1)}, u32[]{:S(2)}, u32[]{:S(2)}) collective-permute-start(f32[640,128]{1,0:T(8,128)S(1)} %select_select_fusion), channel_id=1, source_target_pairs={{0,32},{1,33},{2,34},{3,35},{4,36},{5,37},{6,38},{7,39},{8,40},{9,... | collective-permute-start | bytes 983048 | tf_op jit(solution)/shard_map/ppermute | solution.py:76
  22.1 6.3 %collective-permute-done.4 = f32[640,128]{1,0:T(8,128)S(1)} collective-permute-done((f32[640,128]{1,0:T(8,128)S(1)}, f32[640,128]{1,0:T(8,128)S(1)}, u32[]{:S(2)}, u32[]{:S(2)}) %collective-permute-start.4) | collective-permute-done | bytes 327712 | tf_op jit(solution)/shard_map/ppermute | solution.py:76
  28.5 1.1 %collective-permute-start.5 = (f32[640,128]{1,0:T(8,128)S(1)}, f32[640,128]{1,0:T(8,128)S(1)}, u32[]{:S(2)}, u32[]{:S(2)}) collective-permute-start(f32[640,128]{1,0:T(8,128)S(1)} %broadcast_select_fusion), channel_id=1, source_target_pairs={{0,9},{2,11},{9,0},{11,2},{4,6},{13,15},{6,4},{15,13},{3,10},{1,8}... | collective-permute-start | bytes 983048 | tf_op jit(solution)/shard_map/ppermute | solution.py:76
  29.7 0.9 %slice.12 = f32[256,128]{1,0:T(8,128)S(1)} slice(f32[4096,128]{1,0:T(8,128)} %front.7), slice={[0:256], [0:128]} | slice | bytes 262144 | tf_op jit(solution)/shard_map/slice | solution.py:293
  30.6 3.1 %collective-permute-start.14 = (f32[256,128]{1,0:T(8,128)S(1)}, f32[256,128]{1,0:T(8,128)S(1)}, u32[]{:S(2)}, u32[]{:S(2)}) collective-permute-start(f32[256,128]{1,0:T(8,128)S(1)} %slice.12), channel_id=1, source_target_pairs={{0,64},{1,65},{2,66},{3,67},{4,68},{5,69},{6,70},{7,71},{8,72},{9,... | collective-permute-start | bytes 393224 | tf_op jit(solution)/shard_map/ppermute | solution.py:76
  33.8 4.3 %collective-permute-done.5 = f32[640,128]{1,0:T(8,128)S(1)} collective-permute-done((f32[640,128]{1,0:T(8,128)S(1)}, f32[640,128]{1,0:T(8,128)S(1)}, u32[]{:S(2)}, u32[]{:S(2)}) %collective-permute-start.5) | collective-permute-done | bytes 327712 | tf_op jit(solution)/shard_map/ppermute | solution.py:76
  38.2 3.1 %collective-permute-start.11 = (f32[128,128]{1,0:T(8,128)S(1)}, f32[128,128]{1,0:T(8,128)S(1)}, u32[]{:S(2)}, u32[]{:S(2)}) collective-permute-start(f32[128,128]{1,0:T(8,128)S(1)} %slice.14), channel_id=1, source_target_pairs={{0,64},{1,65},{2,66},{3,67},{4,68},{5,69},{6,70},{7,71},{8,72},{9,... | collective-permute-start | bytes 196616 | tf_op jit(solution)/shard_map/ppermute | solution.py:76
  41.3 1.9 %collective-permute-start.6 = (f32[512,128]{1,0:T(8,128)S(1)}, f32[512,128]{1,0:T(8,128)S(1)}, u32[]{:S(2)}, u32[]{:S(2)}) collective-permute-start(f32[512,128]{1,0:T(8,128)S(1)} %slice.13), channel_id=1, source_target_pairs={{0,2},{2,0},{9,11},{11,9},{4,13},{13,4},{6,15},{15,6},{3,1},{1,3},... | collective-permute-start | bytes 786440 | tf_op jit(solution)/shard_map/ppermute | solution.py:76
  43.2 0.1 stack.106.info
  43.4 0.6 collective-permute-done.11
  44.0 1.9 %collective-permute-start.12 = (f32[128,128]{1,0:T(8,128)S(1)}, f32[128,128]{1,0:T(8,128)S(1)}, u32[]{:S(2)}, u32[]{:S(2)}) collective-permute-start(f32[128,128]{1,0:T(8,128)S(1)} %broadcast_select_fusion.3), channel_id=1, source_target_pairs={{0,2},{2,0},{9,11},{11,9},{4,13},{13,4},{6,15},{15,6},{3,1},{1,3},... | collective-permute-start | bytes 196616 | tf_op jit(solution)/shard_map/ppermute | solution.py:76
  46.0 3.2 %collective-permute-done.6 = f32[512,128]{1,0:T(8,128)S(1)} collective-permute-done((f32[512,128]{1,0:T(8,128)S(1)}, f32[512,128]{1,0:T(8,128)S(1)}, u32[]{:S(2)}, u32[]{:S(2)}) %collective-permute-start.6) | collective-permute-done | bytes 262176 | tf_op jit(solution)/shard_map/ppermute | solution.py:76
  49.3 0.6 collective-permute-done.12
  49.9 0.1 collective-permute-start.13
  50.0 0.9 %broadcast_select_fusion.2.top = f32[256,128]{1,0:T(8,128)S(1)} fusion(f32[256,128]{1,0:T(8,128)S(1)} %collective-permute-done.14, pred[]{:T(512)S(6)} %eq.62, f32[4096,128]{1,0:T(8,128)} %front.7), kind=kLoop, calls=%fused_computation.9 | loop fusion | flops 32768 | bytes 393217 | tf_op jit(solution)/shard_map/jit(_where)/select_n | solution.py:293
  50.9 0.6 collective-permute-start.17
  51.5 2.7 %collective-permute-start.7 = (f32[2,512,128]{2,1,0:T(8,128)S(1)}, f32[2,512,128]{2,1,0:T(8,128)S(1)}, u32[]{:S(2)}, u32[]{:S(2)}) collective-permute-start(f32[2,512,128]{2,1,0:T(8,128)S(1)} %pad_maximum_fusion.refs_0_), channel_id=1, source_target_pairs={{0,12},{1,13},{2,14},{3,15},{4,0},{5,1},{6,2},{7,3},{8,4},{9,5},{1... | collective-permute-start | bytes 1572872 | tf_op jit(solution)/shard_map/ppermute | solution.py:76
  54.2 1.4 %collective-permute-start.9 = (f32[2,512,128]{2,1,0:T(8,128)S(1)}, f32[2,512,128]{2,1,0:T(8,128)S(1)}, u32[]{:S(2)}, u32[]{:S(2)}) collective-permute-start(f32[2,512,128]{2,1,0:T(8,128)S(1)} %pad_maximum_fusion.refs_0_), channel_id=1, source_target_pairs={{0,1},{1,2},{2,3},{3,0},{4,5},{5,6},{6,7},{7,4},{8,9},{9,10},{10,1... | collective-permute-start | bytes 1572872 | tf_op jit(solution)/shard_map/ppermute | solution.py:76
  55.6 4.1 %collective-permute-done.15.refs_2_ = f32[2,512,128]{2,1,0:T(8,128)S(1)} collective-permute-done((f32[2,512,128]{2,1,0:T(8,128)S(1)}, f32[2,512,128]{2,1,0:T(8,128)S(1)}, u32[]{:S(2)}, u32[]{:S(2)}) %collective-permute-start.15) | collective-permute-done | bytes 524320 | tf_op jit(solution)/shard_map/ppermute | solution.py:76
  59.7 5.2 %factor.1 = (bf16[512,256]{1,0:T(8,128)(2,1)S(1)}, f32[256,128]{1,0:T(8,128)}) custom-call(s32[4]{0:T(128)S(1)} %pad_add_fusion.2.info, f32[2,128,128]{2,1,0:T(8,128)S(1)} %pad_maximum_fusion.1.d_mine, f32[2,128,128]{2,1,0:T(8,128)S(1)} %collective-permute-done.13.d_other, f32[256,128]{1,0:T(8,128)S(1)} %broadcast_select_fusion.2.top), custom_call_target="tpu_custom_call" | custom-call | flops 8999999488 | bytes 2000000 | tf_op jit(solution)/shard_map/factor/pallas_call | solution.py:199
  64.9 5.2 %collective-permute-done.9.refs_1_ = f32[2,512,128]{2,1,0:T(8,128)S(1)} collective-permute-done((f32[2,512,128]{2,1,0:T(8,128)S(1)}, f32[2,512,128]{2,1,0:T(8,128)S(1)}, u32[]{:S(2)}, u32[]{:S(2)}) %collective-permute-start.9) | collective-permute-done | bytes 524320 | tf_op jit(solution)/shard_map/ppermute | solution.py:76
  70.2 0.5 collective-permute-start.8
  70.7 3.2 %shard_map.17.refs_5_ = f32[4096,128]{1,0:T(8,128)} custom-call(s32[5]{0:T(128)S(1)} %stack.106.info, f32[4096,128]{1,0:T(8,128)} %front.7, f32[2,512,128]{2,1,0:T(8,128)S(1)} %pad_maximum_fusion.refs_0_, f32[2,512,128]{2,1,0:T(8,128)S(1)} %collective-permute-done.17.refs_1_, f32[2,512,128]{2,1,0:T(8,128)S(1)} %collective-permute-done.15.refs_2_, ...), custom_call_target="tpu_custom_call" | custom-call | flops 3000000000 | bytes 4000000 | tf_op jit(solution)/shard_map/pallas_call | solution.py:257
  73.9 3.2 %shard_map.18.refs_4_ = f32[4096,128]{1,0:T(8,128)} custom-call(s32[5]{0:T(128)S(1)} %stack.102.info, f32[4096,128]{1,0:T(8,128)} %front.7, f32[2,512,128]{2,1,0:T(8,128)S(1)} %collective-permute-done.7.refs_0_, f32[2,512,128]{2,1,0:T(8,128)S(1)} %collective-permute-done.9.refs_1_, ...), custom_call_target="tpu_custom_call", output_to_operand_aliasing={{}: (7, {})} | custom-call | flops 3000000000 | bytes 4000000 | tf_op jit(solution)/shard_map/pallas_call | solution.py:257
  77.2 2.8 %shard_map.19 = f32[4096,128]{1,0:T(8,128)} custom-call(s32[4]{0:T(128)S(1)} %pad_add_fusion.info, f32[4096,128]{1,0:T(8,128)} %front.7, f32[2,512,128]{2,1,0:T(8,128)S(1)} %collective-permute-done.8.refs_0_, f32[2,512,128]{2,1,0:T(8,128)S(1)} %collective-permute-done.10.refs_1_, ...), custom_call_target="tpu_custom_call", output_to_operand_aliasing={{}: (6, {})} | custom-call | flops 3000000000 | bytes 4000000 | tf_op jit(solution)/shard_map/pallas_call | solution.py:257
  (26 shorter events, 0.7 us)
Async XLA Ops:
  0.0 4.4 %collective-permute-start = (f32[4096,128]{1,0:T(8,128)}, f32[4096,128]{1,0:T(8,128)S(1)}, u32[]{:S(2)}, u32[]{:S(2)}) collective-permute-start(f32[4096,128]{1,0:T(8,128)} %front.7), channel_id=1, source_target_pairs={{0,16},{1,17},{2,18},{3,19},{4,20},{5,21},{6,22},{7,23},{8,24},{9,... | collective-permute-start | bytes 6291464 | tf_op jit(solution)/shard_map/ppermute | solution.py:76
  6.3 11.4 %collective-permute-start.1 = (f32[640,128]{1,0:T(8,128)S(1)}, f32[640,128]{1,0:T(8,128)S(1)}, u32[]{:S(2)}, u32[]{:S(2)}) collective-permute-start(f32[640,128]{1,0:T(8,128)S(1)} %get-tuple-element.11), channel_id=1, source_target_pairs={{0,4},{1,5},{2,6},{3,7},{4,8},{5,9},{6,10},{7,11},{8,12},{9,13},{1... | collective-permute-start | bytes 983048 | tf_op jit(solution)/shard_map/ppermute | solution.py:76
  8.4 9.3 %collective-permute-start.2 = (f32[640,128]{1,0:T(8,128)S(1)}, f32[640,128]{1,0:T(8,128)S(1)}, u32[]{:S(2)}, u32[]{:S(2)}) collective-permute-start(f32[640,128]{1,0:T(8,128)S(1)} %get-tuple-element.12), channel_id=1, source_target_pairs={{0,12},{1,13},{2,14},{3,15},{4,0},{5,1},{6,2},{7,3},{8,4},{9,5},{1... | collective-permute-start | bytes 983048 | tf_op jit(solution)/shard_map/ppermute | solution.py:76
  10.6 9.9 %collective-permute-start.3 = (f32[640,128]{1,0:T(8,128)S(1)}, f32[640,128]{1,0:T(8,128)S(1)}, u32[]{:S(2)}, u32[]{:S(2)}) collective-permute-start(f32[640,128]{1,0:T(8,128)S(1)} %get-tuple-element.14), channel_id=1, source_target_pairs={{0,3},{1,2},{2,1},{3,0},{4,7},{5,6},{6,5},{7,4},{8,11},{9,10},{10,... | collective-permute-start | bytes 983048 | tf_op jit(solution)/shard_map/ppermute | solution.py:76
  20.6 7.9 %collective-permute-start.4 = (f32[640,128]{1,0:T(8,128)S(1)}, f32[640,128]{1,0:T(8,128)S(1)}, u32[]{:S(2)}, u32[]{:S(2)}) collective-permute-start(f32[640,128]{1,0:T(8,128)S(1)} %select_select_fusion), channel_id=1, source_target_pairs={{0,32},{1,33},{2,34},{3,35},{4,36},{5,37},{6,38},{7,39},{8,40},{9,... | collective-permute-start | bytes 983048 | tf_op jit(solution)/shard_map/ppermute | solution.py:76
  28.5 9.6 %collective-permute-start.5 = (f32[640,128]{1,0:T(8,128)S(1)}, f32[640,128]{1,0:T(8,128)S(1)}, u32[]{:S(2)}, u32[]{:S(2)}) collective-permute-start(f32[640,128]{1,0:T(8,128)S(1)} %broadcast_select_fusion), channel_id=1, source_target_pairs={{0,9},{2,11},{9,0},{11,2},{4,6},{13,15},{6,4},{15,13},{3,10},{1,8}... | collective-permute-start | bytes 983048 | tf_op jit(solution)/shard_map/ppermute | solution.py:76
  30.6 19.4 %collective-permute-start.14 = (f32[256,128]{1,0:T(8,128)S(1)}, f32[256,128]{1,0:T(8,128)S(1)}, u32[]{:S(2)}, u32[]{:S(2)}) collective-permute-start(f32[256,128]{1,0:T(8,128)S(1)} %slice.12), channel_id=1, source_target_pairs={{0,64},{1,65},{2,66},{3,67},{4,68},{5,69},{6,70},{7,71},{8,72},{9,... | collective-permute-start | bytes 393224 | tf_op jit(solution)/shard_map/ppermute | solution.py:76
  38.2 5.8 %collective-permute-start.11 = (f32[128,128]{1,0:T(8,128)S(1)}, f32[128,128]{1,0:T(8,128)S(1)}, u32[]{:S(2)}, u32[]{:S(2)}) collective-permute-start(f32[128,128]{1,0:T(8,128)S(1)} %slice.14), channel_id=1, source_target_pairs={{0,64},{1,65},{2,66},{3,67},{4,68},{5,69},{6,70},{7,71},{8,72},{9,... | collective-permute-start | bytes 196616 | tf_op jit(solution)/shard_map/ppermute | solution.py:76
  41.3 7.9 %collective-permute-start.6 = (f32[512,128]{1,0:T(8,128)S(1)}, f32[512,128]{1,0:T(8,128)S(1)}, u32[]{:S(2)}, u32[]{:S(2)}) collective-permute-start(f32[512,128]{1,0:T(8,128)S(1)} %slice.13), channel_id=1, source_target_pairs={{0,2},{2,0},{9,11},{11,9},{4,13},{13,4},{6,15},{15,6},{3,1},{1,3},... | collective-permute-start | bytes 786440 | tf_op jit(solution)/shard_map/ppermute | solution.py:76
  44.0 5.8 %collective-permute-start.12 = (f32[128,128]{1,0:T(8,128)S(1)}, f32[128,128]{1,0:T(8,128)S(1)}, u32[]{:S(2)}, u32[]{:S(2)}) collective-permute-start(f32[128,128]{1,0:T(8,128)S(1)} %broadcast_select_fusion.3), channel_id=1, source_target_pairs={{0,2},{2,0},{9,11},{11,9},{4,13},{13,4},{6,15},{15,6},{3,1},{1,3},... | collective-permute-start | bytes 196616 | tf_op jit(solution)/shard_map/ppermute | solution.py:76
  49.2 10.5 %collective-permute-start.15 = (f32[2,512,128]{2,1,0:T(8,128)S(1)}, f32[2,512,128]{2,1,0:T(8,128)S(1)}, u32[]{:S(2)}, u32[]{:S(2)}) collective-permute-start(f32[2,512,128]{2,1,0:T(8,128)S(1)} %pad_maximum_fusion.refs_0_), channel_id=1, source_target_pairs={{0,4},{1,5},{2,6},{3,7},{4,8},{5,9},{6,10},{7,11},{8,12},{9,13},{1... | collective-permute-start | bytes 1572872 | tf_op jit(solution)/shard_map/ppermute | solution.py:76
  49.9 9.8 %collective-permute-start.13 = (f32[2,128,128]{2,1,0:T(8,128)S(1)}, f32[2,128,128]{2,1,0:T(8,128)S(1)}, u32[]{:S(2)}, u32[]{:S(2)}) collective-permute-start(f32[2,128,128]{2,1,0:T(8,128)S(1)} %pad_maximum_fusion.1.d_mine), channel_id=1, source_target_pairs={{0,16},{1,17},{2,18},{3,19},{4,20},{5,21},{6,22},{7,23},{8,24},{9,... | collective-permute-start | bytes 393224 | tf_op jit(solution)/shard_map/ppermute | solution.py:76
  50.9 19.8 %collective-permute-start.17 = (f32[2,512,128]{2,1,0:T(8,128)S(1)}, f32[2,512,128]{2,1,0:T(8,128)S(1)}, u32[]{:S(2)}, u32[]{:S(2)}) collective-permute-start(f32[2,512,128]{2,1,0:T(8,128)S(1)} %pad_maximum_fusion.refs_0_), channel_id=1, source_target_pairs={{0,16},{1,17},{2,18},{3,19},{4,20},{5,21},{6,22},{7,23},{8,24},{9,... | collective-permute-start | bytes 1572872 | tf_op jit(solution)/shard_map/ppermute | solution.py:76
  51.5 18.7 %collective-permute-start.7 = (f32[2,512,128]{2,1,0:T(8,128)S(1)}, f32[2,512,128]{2,1,0:T(8,128)S(1)}, u32[]{:S(2)}, u32[]{:S(2)}) collective-permute-start(f32[2,512,128]{2,1,0:T(8,128)S(1)} %pad_maximum_fusion.refs_0_), channel_id=1, source_target_pairs={{0,12},{1,13},{2,14},{3,15},{4,0},{5,1},{6,2},{7,3},{8,4},{9,5},{1... | collective-permute-start | bytes 1572872 | tf_op jit(solution)/shard_map/ppermute | solution.py:76
  54.2 16.0 %collective-permute-start.9 = (f32[2,512,128]{2,1,0:T(8,128)S(1)}, f32[2,512,128]{2,1,0:T(8,128)S(1)}, u32[]{:S(2)}, u32[]{:S(2)}) collective-permute-start(f32[2,512,128]{2,1,0:T(8,128)S(1)} %pad_maximum_fusion.refs_0_), channel_id=1, source_target_pairs={{0,1},{1,2},{2,3},{3,0},{4,5},{5,6},{6,7},{7,4},{8,9},{9,10},{10,1... | collective-permute-start | bytes 1572872 | tf_op jit(solution)/shard_map/ppermute | solution.py:76
  59.7 14.2 %collective-permute-start.16 = (f32[2,512,128]{2,1,0:T(8,128)S(1)}, f32[2,512,128]{2,1,0:T(8,128)S(1)}, u32[]{:S(2)}, u32[]{:S(2)}) collective-permute-start(f32[2,512,128]{2,1,0:T(8,128)S(1)} %collective-permute-done.15.refs_2_), channel_id=1, source_target_pairs={{0,16},{1,17},{2,18},{3,19},{4,20},{5,21},{6,22},{7,23},{8,24},{9,... | collective-permute-start | bytes 1572872 | tf_op jit(solution)/shard_map/ppermute | solution.py:76
  70.2 7.0 %collective-permute-start.10 = (f32[2,512,128]{2,1,0:T(8,128)S(1)}, f32[2,512,128]{2,1,0:T(8,128)S(1)}, u32[]{:S(2)}, u32[]{:S(2)}) collective-permute-start(f32[2,512,128]{2,1,0:T(8,128)S(1)} %collective-permute-done.9.refs_1_), channel_id=1, source_target_pairs={{0,16},{1,17},{2,18},{3,19},{4,20},{5,21},{6,22},{7,23},{8,24},{9,... | collective-permute-start | bytes 1572872 | tf_op jit(solution)/shard_map/ppermute | solution.py:76
  70.2 7.0 %collective-permute-start.8 = (f32[2,512,128]{2,1,0:T(8,128)S(1)}, f32[2,512,128]{2,1,0:T(8,128)S(1)}, u32[]{:S(2)}, u32[]{:S(2)}) collective-permute-start(f32[2,512,128]{2,1,0:T(8,128)S(1)} %collective-permute-done.7.refs_0_), channel_id=1, source_target_pairs={{0,16},{1,17},{2,18},{3,19},{4,20},{5,21},{6,22},{7,23},{8,24},{9,... | collective-permute-start | bytes 1572872 | tf_op jit(solution)/shard_map/ppermute | solution.py:76

commit v8 on v7

--- a/solution.py
+++ b/solution.py
@@ -129,6 +129,19 @@
     rh, rm, rl = split3(right)
     lefts = jnp.concatenate([ll, lh, lm, lm, lh, lh], axis=1)
     rights = jnp.concatenate([rh, rl, rm, rh, rm, rh], axis=0)
+    return jnp.dot(lefts, rights, preferred_element_type=jnp.float32)
+
+
+def split2(value):
+    high = value.astype(jnp.bfloat16)
+    return high, (value - high.astype(jnp.float32)).astype(jnp.bfloat16)
+
+
+def short_dot(left, right):
+    lh, lm = split2(left)
+    rh, rm = split2(right)
+    lefts = jnp.concatenate([lm, lm, lh, lh], axis=1)
+    rights = jnp.concatenate([rm, rh, rm, rh], axis=0)
     return jnp.dot(lefts, rights, preferred_element_type=jnp.float32)
 
 
@@ -166,14 +179,18 @@
         inverse = jnp.where(on_diag, 2.0 * inv_row, 0.0) - inv_col * (pivot * inv_row)
         for _ in range(ITERS - 1):
             inverse = 2.0 * inverse - stacked_dot(inverse, stacked_dot(pivot, inverse))
-        lower = stacked_dot(f[hi:, base : base + WIDTH], inverse)
         left_col = hi // WIDTH * WIDTH
         col = lax.broadcasted_iota(jnp.int32, (WIDTH, total - left_col), 1) + left_col
         upper = jnp.where(col >= hi, f[base : base + WIDTH, left_col:], 0.0)
-        f[hi:, left_col:] = f[hi:, left_col:] - stacked_dot(lower, upper)
-        lane = lax.broadcasted_iota(jnp.int32, lower.shape, 1) + base
-        mine = (lane >= lo) & (lane < hi)
-        f[hi:, base : base + WIDTH] = jnp.where(mine, lower, f[hi:, base : base + WIDTH])
+        for first, last, product in ((hi, P_SIZE, stacked_dot), (P_SIZE, 2 * P_SIZE, short_dot)):
+            if first == last:
+                continue
+            window_rows = slice(first, last)
+            lower = product(f[window_rows, base : base + WIDTH], inverse)
+            f[window_rows, left_col:] = f[window_rows, left_col:] - product(lower, upper)
+            lane = lax.broadcasted_iota(jnp.int32, lower.shape, 1) + base
+            mine = (lane >= lo) & (lane < hi)
+            f[window_rows, base : base + WIDTH] = jnp.where(mine, lower, f[window_rows, base : base + WIDTH])
         if block == P_SIZE // B - 2:
             for case, side in enumerate(sides):
                 @pl.when(kind == case)
@@ -183,8 +200,7 @@
     def finish(update):
         high = update.astype(jnp.bfloat16)
         low = (update - high.astype(jnp.float32)).astype(jnp.bfloat16)
-        both = jnp.concatenate([high, low], axis=1)
-        update_out[...] = jnp.concatenate([both, both], axis=0)
+        update_out[...] = jnp.concatenate([high, low], axis=1)
 
     for case, side in enumerate(sides):
         @pl.when(kind == case)
@@ -198,7 +214,7 @@
     vmem = pl.BlockSpec(memory_space=pltpu.VMEM)
     return pl.pallas_call(
         factor_kernel,
-        out_shape=(pltpu.VMEM((2 * P_SIZE, 2 * WIDTH), jnp.bfloat16), pltpu.HBM((P_SIZE, WIDTH), jnp.float32)),
+        out_shape=(pltpu.VMEM((P_SIZE, 2 * WIDTH), jnp.bfloat16), pltpu.HBM((P_SIZE, WIDTH), jnp.float32)),
         in_specs=[pl.BlockSpec(memory_space=pltpu.SMEM), vmem, vmem, vmem],
         out_specs=(vmem, pl.BlockSpec(memory_space=pltpu.HBM)),
         scratch_shapes=[pltpu.VMEM((2 * P_SIZE, P_SIZE + WIDTH), jnp.float32), pltpu.SemaphoreType.DMA],
@@ -227,13 +243,14 @@
     for at in range(count):
         load(at).start()
         pl.when(has_top[at])(top_load.start)
+    twice = jnp.concatenate([update[...], update[...]], axis=0)
     for at in range(count):
         for half in range(2):
             rows = slice(half * P_SIZE, (half + 1) * P_SIZE)
             panel = jnp.concatenate([parts[at][0, rows, :], parts[at][1, rows, :]], axis=1)
             high = panel.astype(jnp.bfloat16)
             low = (panel - high.astype(jnp.float32)).astype(jnp.bfloat16)
-            both = jnp.dot(jnp.concatenate([high, low], axis=1), update[...], preferred_element_type=jnp.float32)
+            both = jnp.dot(jnp.concatenate([high, low], axis=1), twice, preferred_element_type=jnp.float32)
             added = both[:, :WIDTH] + both[:, WIDTH:]
             if half == 0:
                 load(at).wait()

time: 81.1 us -> 81.1 us (level)
  waiting for transfers between devices: 35.5 us -> 36.4 us
    ppermute x18, waiting for transfers between devices: 35.5 us -> 36.4 us  [send(): return lax.ppermute(value, AXES, pairs)]
    pallas_call x1, Pallas kernels: 5.23 us -> 4.35 us  [factor(): pl.pallas_call(factor_kernel, out_shape=(pltpu.VMEM((P_SIZE, 2 * WIDTH),...]
  transfers between devices with their start and end apart: 18 -> 18, of which waited for: 10 -> 10; matrix products, arithmetic and copies ran while one was open for 3% -> 3% of each run, Pallas kernels for 15% -> 14%
where the time goes in v8:
time: 81.1 us; the launch traced here: 80 us
  waiting for transfers between devices  36.4 us (45%)
  starting transfers between devices  25.4 us (31%)
  Pallas kernels  15.6 us (19%)
  other arithmetic  1.4 us (2%)
  local copies, waits for them, and re-layouts  1.11 us (1%)
    ppermute x18, waiting for transfers between devices, send(): return lax.ppermute(value, AXES, pairs)  36.4 us
    ppermute x18, starting transfers between devices, send(): return lax.ppermute(value, AXES, pairs)  25.4 us
    pallas_call x3, Pallas kernels, apply_update(): pl.pallas_call(update_kernel, out_shape=jax.ShapeDtypeStruct((ROWS, WIDTH...  9.3 us
    pallas_call x1, Pallas kernels, factor(): pl.pallas_call(factor_kernel, out_shape=(pltpu.VMEM((P_SIZE, 2 * WIDTH),...  4.35 us
    pallas_call x1, Pallas kernels, payloads(): pl.pallas_call(payload_kernel, out_shape=tuple((pltpu.VMEM((DPART + SHARE...  1.91 us
  transfers between devices with their start and end apart: 18, of which 10 were waited for; matrix products, arithmetic and copies ran while one was open for 3% of the time, Pallas kernels for 14%

profile of v8, /device:TPU:0, one launch (start us, length us, event | category | flops | bytes accessed | tf_op | source)
XLA Modules:
  0.0 80.0 jit_solution(14816478083172430811)
XLA Ops:
  0.1 4.3 %collective-permute-done.beside = f32[4096,128]{1,0:T(8,128)S(1)} collective-permute-done((f32[4096,128]{1,0:T(8,128)}, f32[4096,128]{1,0:T(8,128)S(1)}, u32[]{:S(2)}, u32[]{:S(2)}) %collective-permute-start) | collective-permute-done | bytes 2097184 | tf_op jit(solution)/shard_map/ppermute | solution.py:76
  4.4 1.9 %payloads.1 = (f32[640,128]{1,0:T(8,128)S(1)}, f32[640,128]{1,0:T(8,128)S(1)}, f32[640,128]{1,0:T(8,128)S(1)}, f32[640,128]{1,0:T(8,128)S(1)}) custom-call(s32[2]{0:T(128)S(1)} %pad_add_fusion.1.info, f32[4096,128]{1,0:T(8,128)} %front.7, f32[4096,128]{1,0:T(8,128)S(1)} %collective-permute-done.beside), custom_call_target="tpu_custom_call" | custom-call | tf_op jit(solution)/shard_map/payloads/pallas_call | solution.py:108
  6.3 2.1 %collective-permute-start.1 = (f32[640,128]{1,0:T(8,128)S(1)}, f32[640,128]{1,0:T(8,128)S(1)}, u32[]{:S(2)}, u32[]{:S(2)}) collective-permute-start(f32[640,128]{1,0:T(8,128)S(1)} %get-tuple-element.11), channel_id=1, source_target_pairs={{0,4},{1,5},{2,6},{3,7},{4,8},{5,9},{6,10},{7,11},{8,12},{9,13},{1... | collective-permute-start | bytes 983048 | tf_op jit(solution)/shard_map/ppermute | solution.py:76
  8.4 2.2 %collective-permute-start.2 = (f32[640,128]{1,0:T(8,128)S(1)}, f32[640,128]{1,0:T(8,128)S(1)}, u32[]{:S(2)}, u32[]{:S(2)}) collective-permute-start(f32[640,128]{1,0:T(8,128)S(1)} %get-tuple-element.12), channel_id=1, source_target_pairs={{0,12},{1,13},{2,14},{3,15},{4,0},{5,1},{6,2},{7,3},{8,4},{9,5},{1... | collective-permute-start | bytes 983048 | tf_op jit(solution)/shard_map/ppermute | solution.py:76
  10.6 3.0 %collective-permute-start.3 = (f32[640,128]{1,0:T(8,128)S(1)}, f32[640,128]{1,0:T(8,128)S(1)}, u32[]{:S(2)}, u32[]{:S(2)}) collective-permute-start(f32[640,128]{1,0:T(8,128)S(1)} %get-tuple-element.14), channel_id=1, source_target_pairs={{0,3},{1,2},{2,1},{3,0},{4,7},{5,6},{6,5},{7,4},{8,11},{9,10},{10,... | collective-permute-start | bytes 983048 | tf_op jit(solution)/shard_map/ppermute | solution.py:76
  13.6 4.1 %collective-permute-done.1 = f32[640,128]{1,0:T(8,128)S(1)} collective-permute-done((f32[640,128]{1,0:T(8,128)S(1)}, f32[640,128]{1,0:T(8,128)S(1)}, u32[]{:S(2)}, u32[]{:S(2)}) %collective-permute-start.1) | collective-permute-done | bytes 327712 | tf_op jit(solution)/shard_map/ppermute | solution.py:76
  17.7 2.8 %collective-permute-done.3 = f32[640,128]{1,0:T(8,128)S(1)} collective-permute-done((f32[640,128]{1,0:T(8,128)S(1)}, f32[640,128]{1,0:T(8,128)S(1)}, u32[]{:S(2)}, u32[]{:S(2)}) %collective-permute-start.3) | collective-permute-done | bytes 327712 | tf_op jit(solution)/shard_map/ppermute | solution.py:76
  20.6 1.6 %collective-permute-start.4 = (f32[640,128]{1,0:T(8,128)S(1)}, f32[640,128]{1,0:T(8,128)S(1)}, u32[]{:S(2)}, u32[]{:S(2)}) collective-permute-start(f32[640,128]{1,0:T(8,128)S(1)} %select_select_fusion), channel_id=1, source_target_pairs={{0,32},{1,33},{2,34},{3,35},{4,36},{5,37},{6,38},{7,39},{8,40},{9,... | collective-permute-start | bytes 983048 | tf_op jit(solution)/shard_map/ppermute | solution.py:76
  22.1 6.3 %collective-permute-done.4 = f32[640,128]{1,0:T(8,128)S(1)} collective-permute-done((f32[640,128]{1,0:T(8,128)S(1)}, f32[640,128]{1,0:T(8,128)S(1)}, u32[]{:S(2)}, u32[]{:S(2)}) %collective-permute-start.4) | collective-permute-done | bytes 327712 | tf_op jit(solution)/shard_map/ppermute | solution.py:76
  28.5 1.1 %collective-permute-start.5 = (f32[640,128]{1,0:T(8,128)S(1)}, f32[640,128]{1,0:T(8,128)S(1)}, u32[]{:S(2)}, u32[]{:S(2)}) collective-permute-start(f32[640,128]{1,0:T(8,128)S(1)} %broadcast_select_fusion), channel_id=1, source_target_pairs={{0,9},{2,11},{9,0},{11,2},{4,6},{13,15},{6,4},{15,13},{3,10},{1,8}... | collective-permute-start | bytes 983048 | tf_op jit(solution)/shard_map/ppermute | solution.py:76
  29.7 0.9 %slice.12 = f32[256,128]{1,0:T(8,128)S(1)} slice(f32[4096,128]{1,0:T(8,128)} %front.7), slice={[0:256], [0:128]} | slice | bytes 262144 | tf_op jit(solution)/shard_map/slice | solution.py:310
  30.6 3.1 %collective-permute-start.14 = (f32[256,128]{1,0:T(8,128)S(1)}, f32[256,128]{1,0:T(8,128)S(1)}, u32[]{:S(2)}, u32[]{:S(2)}) collective-permute-start(f32[256,128]{1,0:T(8,128)S(1)} %slice.12), channel_id=1, source_target_pairs={{0,64},{1,65},{2,66},{3,67},{4,68},{5,69},{6,70},{7,71},{8,72},{9,... | collective-permute-start | bytes 393224 | tf_op jit(solution)/shard_map/ppermute | solution.py:76
  33.8 4.3 %collective-permute-done.5 = f32[640,128]{1,0:T(8,128)S(1)} collective-permute-done((f32[640,128]{1,0:T(8,128)S(1)}, f32[640,128]{1,0:T(8,128)S(1)}, u32[]{:S(2)}, u32[]{:S(2)}) %collective-permute-start.5) | collective-permute-done | bytes 327712 | tf_op jit(solution)/shard_map/ppermute | solution.py:76
  38.2 3.1 %collective-permute-start.11 = (f32[128,128]{1,0:T(8,128)S(1)}, f32[128,128]{1,0:T(8,128)S(1)}, u32[]{:S(2)}, u32[]{:S(2)}) collective-permute-start(f32[128,128]{1,0:T(8,128)S(1)} %slice.14), channel_id=1, source_target_pairs={{0,64},{1,65},{2,66},{3,67},{4,68},{5,69},{6,70},{7,71},{8,72},{9,... | collective-permute-start | bytes 196616 | tf_op jit(solution)/shard_map/ppermute | solution.py:76
  41.3 1.9 %collective-permute-start.6 = (f32[512,128]{1,0:T(8,128)S(1)}, f32[512,128]{1,0:T(8,128)S(1)}, u32[]{:S(2)}, u32[]{:S(2)}) collective-permute-start(f32[512,128]{1,0:T(8,128)S(1)} %slice.13), channel_id=1, source_target_pairs={{0,2},{2,0},{9,11},{11,9},{4,13},{13,4},{6,15},{15,6},{3,1},{1,3},... | collective-permute-start | bytes 786440 | tf_op jit(solution)/shard_map/ppermute | solution.py:76
  43.2 0.1 stack.106.info
  43.4 0.6 collective-permute-done.11
  44.0 1.9 %collective-permute-start.12 = (f32[128,128]{1,0:T(8,128)S(1)}, f32[128,128]{1,0:T(8,128)S(1)}, u32[]{:S(2)}, u32[]{:S(2)}) collective-permute-start(f32[128,128]{1,0:T(8,128)S(1)} %broadcast_select_fusion.3), channel_id=1, source_target_pairs={{0,2},{2,0},{9,11},{11,9},{4,13},{13,4},{6,15},{15,6},{3,1},{1,3},... | collective-permute-start | bytes 196616 | tf_op jit(solution)/shard_map/ppermute | solution.py:76
  46.0 3.2 %collective-permute-done.6 = f32[512,128]{1,0:T(8,128)S(1)} collective-permute-done((f32[512,128]{1,0:T(8,128)S(1)}, f32[512,128]{1,0:T(8,128)S(1)}, u32[]{:S(2)}, u32[]{:S(2)}) %collective-permute-start.6) | collective-permute-done | bytes 262176 | tf_op jit(solution)/shard_map/ppermute | solution.py:76
  49.3 0.6 collective-permute-done.12
  49.9 0.1 collective-permute-start.13
  50.0 0.9 %broadcast_select_fusion.2.top = f32[256,128]{1,0:T(8,128)S(1)} fusion(f32[256,128]{1,0:T(8,128)S(1)} %collective-permute-done.14, pred[]{:T(512)S(6)} %eq.62, f32[4096,128]{1,0:T(8,128)} %front.7), kind=kLoop, calls=%fused_computation.9 | loop fusion | flops 32768 | bytes 393217 | tf_op jit(solution)/shard_map/jit(_where)/select_n | solution.py:310
  50.9 0.6 collective-permute-start.17
  51.5 2.7 %collective-permute-start.7 = (f32[2,512,128]{2,1,0:T(8,128)S(1)}, f32[2,512,128]{2,1,0:T(8,128)S(1)}, u32[]{:S(2)}, u32[]{:S(2)}) collective-permute-start(f32[2,512,128]{2,1,0:T(8,128)S(1)} %pad_maximum_fusion.refs_0_), channel_id=1, source_target_pairs={{0,12},{1,13},{2,14},{3,15},{4,0},{5,1},{6,2},{7,3},{8,4},{9,5},{1... | collective-permute-start | bytes 1572872 | tf_op jit(solution)/shard_map/ppermute | solution.py:76
  54.2 1.4 %collective-permute-start.9 = (f32[2,512,128]{2,1,0:T(8,128)S(1)}, f32[2,512,128]{2,1,0:T(8,128)S(1)}, u32[]{:S(2)}, u32[]{:S(2)}) collective-permute-start(f32[2,512,128]{2,1,0:T(8,128)S(1)} %pad_maximum_fusion.refs_0_), channel_id=1, source_target_pairs={{0,1},{1,2},{2,3},{3,0},{4,5},{5,6},{6,7},{7,4},{8,9},{9,10},{10,1... | collective-permute-start | bytes 1572872 | tf_op jit(solution)/shard_map/ppermute | solution.py:76
  55.6 4.1 %collective-permute-done.15.refs_2_ = f32[2,512,128]{2,1,0:T(8,128)S(1)} collective-permute-done((f32[2,512,128]{2,1,0:T(8,128)S(1)}, f32[2,512,128]{2,1,0:T(8,128)S(1)}, u32[]{:S(2)}, u32[]{:S(2)}) %collective-permute-start.15) | collective-permute-done | bytes 524320 | tf_op jit(solution)/shard_map/ppermute | solution.py:76
  59.7 4.4 %factor.1 = (bf16[256,256]{1,0:T(8,128)(2,1)S(1)}, f32[256,128]{1,0:T(8,128)}) custom-call(s32[4]{0:T(128)S(1)} %pad_add_fusion.2.info, f32[2,128,128]{2,1,0:T(8,128)S(1)} %pad_maximum_fusion.1.d_mine, f32[2,128,128]{2,1,0:T(8,128)S(1)} %collective-permute-done.13.d_other, f32[256,128]{1,0:T(8,128)S(1)} %broadcast_select_fusion.2.top), custom_call_target="tpu_custom_call" | custom-call | flops 8999999488 | bytes 2000000 | tf_op jit(solution)/shard_map/factor/pallas_call | solution.py:215
  64.0 6.1 %collective-permute-done.9.refs_1_ = f32[2,512,128]{2,1,0:T(8,128)S(1)} collective-permute-done((f32[2,512,128]{2,1,0:T(8,128)S(1)}, f32[2,512,128]{2,1,0:T(8,128)S(1)}, u32[]{:S(2)}, u32[]{:S(2)}) %collective-permute-start.9) | collective-permute-done | bytes 524320 | tf_op jit(solution)/shard_map/ppermute | solution.py:76
  70.2 0.5 collective-permute-start.8
  70.7 3.2 %shard_map.17.refs_5_ = f32[4096,128]{1,0:T(8,128)} custom-call(s32[5]{0:T(128)S(1)} %stack.106.info, f32[4096,128]{1,0:T(8,128)} %front.7, f32[2,512,128]{2,1,0:T(8,128)S(1)} %pad_maximum_fusion.refs_0_, f32[2,512,128]{2,1,0:T(8,128)S(1)} %collective-permute-done.17.refs_1_, f32[2,512,128]{2,1,0:T(8,128)S(1)} %collective-permute-done.15.refs_2_, ...), custom_call_target="tpu_custom_call" | custom-call | flops 3000000000 | bytes 4000000 | tf_op jit(solution)/shard_map/pallas_call | solution.py:274
  73.9 3.2 %shard_map.18.refs_4_ = f32[4096,128]{1,0:T(8,128)} custom-call(s32[5]{0:T(128)S(1)} %stack.102.info, f32[4096,128]{1,0:T(8,128)} %front.7, f32[2,512,128]{2,1,0:T(8,128)S(1)} %collective-permute-done.7.refs_0_, f32[2,512,128]{2,1,0:T(8,128)S(1)} %collective-permute-done.9.refs_1_, ...), custom_call_target="tpu_custom_call", output_to_operand_aliasing={{}: (7, {})} | custom-call | flops 3000000000 | bytes 4000000 | tf_op jit(solution)/shard_map/pallas_call | solution.py:274
  77.2 2.8 %shard_map.19 = f32[4096,128]{1,0:T(8,128)} custom-call(s32[4]{0:T(128)S(1)} %pad_add_fusion.info, f32[4096,128]{1,0:T(8,128)} %front.7, f32[2,512,128]{2,1,0:T(8,128)S(1)} %collective-permute-done.8.refs_0_, f32[2,512,128]{2,1,0:T(8,128)S(1)} %collective-permute-done.10.refs_1_, ...), custom_call_target="tpu_custom_call", output_to_operand_aliasing={{}: (6, {})} | custom-call | flops 3000000000 | bytes 4000000 | tf_op jit(solution)/shard_map/pallas_call | solution.py:274
  (26 shorter events, 0.7 us)
Async XLA Ops:
  0.0 4.4 %collective-permute-start = (f32[4096,128]{1,0:T(8,128)}, f32[4096,128]{1,0:T(8,128)S(1)}, u32[]{:S(2)}, u32[]{:S(2)}) collective-permute-start(f32[4096,128]{1,0:T(8,128)} %front.7), channel_id=1, source_target_pairs={{0,16},{1,17},{2,18},{3,19},{4,20},{5,21},{6,22},{7,23},{8,24},{9,... | collective-permute-start | bytes 6291464 | tf_op jit(solution)/shard_map/ppermute | solution.py:76
  6.3 11.4 %collective-permute-start.1 = (f32[640,128]{1,0:T(8,128)S(1)}, f32[640,128]{1,0:T(8,128)S(1)}, u32[]{:S(2)}, u32[]{:S(2)}) collective-permute-start(f32[640,128]{1,0:T(8,128)S(1)} %get-tuple-element.11), channel_id=1, source_target_pairs={{0,4},{1,5},{2,6},{3,7},{4,8},{5,9},{6,10},{7,11},{8,12},{9,13},{1... | collective-permute-start | bytes 983048 | tf_op jit(solution)/shard_map/ppermute | solution.py:76
  8.4 9.3 %collective-permute-start.2 = (f32[640,128]{1,0:T(8,128)S(1)}, f32[640,128]{1,0:T(8,128)S(1)}, u32[]{:S(2)}, u32[]{:S(2)}) collective-permute-start(f32[640,128]{1,0:T(8,128)S(1)} %get-tuple-element.12), channel_id=1, source_target_pairs={{0,12},{1,13},{2,14},{3,15},{4,0},{5,1},{6,2},{7,3},{8,4},{9,5},{1... | collective-permute-start | bytes 983048 | tf_op jit(solution)/shard_map/ppermute | solution.py:76
  10.6 9.9 %collective-permute-start.3 = (f32[640,128]{1,0:T(8,128)S(1)}, f32[640,128]{1,0:T(8,128)S(1)}, u32[]{:S(2)}, u32[]{:S(2)}) collective-permute-start(f32[640,128]{1,0:T(8,128)S(1)} %get-tuple-element.14), channel_id=1, source_target_pairs={{0,3},{1,2},{2,1},{3,0},{4,7},{5,6},{6,5},{7,4},{8,11},{9,10},{10,... | collective-permute-start | bytes 983048 | tf_op jit(solution)/shard_map/ppermute | solution.py:76
  20.6 7.9 %collective-permute-start.4 = (f32[640,128]{1,0:T(8,128)S(1)}, f32[640,128]{1,0:T(8,128)S(1)}, u32[]{:S(2)}, u32[]{:S(2)}) collective-permute-start(f32[640,128]{1,0:T(8,128)S(1)} %select_select_fusion), channel_id=1, source_target_pairs={{0,32},{1,33},{2,34},{3,35},{4,36},{5,37},{6,38},{7,39},{8,40},{9,... | collective-permute-start | bytes 983048 | tf_op jit(solution)/shard_map/ppermute | solution.py:76
  28.5 9.6 %collective-permute-start.5 = (f32[640,128]{1,0:T(8,128)S(1)}, f32[640,128]{1,0:T(8,128)S(1)}, u32[]{:S(2)}, u32[]{:S(2)}) collective-permute-start(f32[640,128]{1,0:T(8,128)S(1)} %broadcast_select_fusion), channel_id=1, source_target_pairs={{0,9},{2,11},{9,0},{11,2},{4,6},{13,15},{6,4},{15,13},{3,10},{1,8}... | collective-permute-start | bytes 983048 | tf_op jit(solution)/shard_map/ppermute | solution.py:76
  30.6 19.4 %collective-permute-start.14 = (f32[256,128]{1,0:T(8,128)S(1)}, f32[256,128]{1,0:T(8,128)S(1)}, u32[]{:S(2)}, u32[]{:S(2)}) collective-permute-start(f32[256,128]{1,0:T(8,128)S(1)} %slice.12), channel_id=1, source_target_pairs={{0,64},{1,65},{2,66},{3,67},{4,68},{5,69},{6,70},{7,71},{8,72},{9,... | collective-permute-start | bytes 393224 | tf_op jit(solution)/shard_map/ppermute | solution.py:76
  38.2 5.8 %collective-permute-start.11 = (f32[128,128]{1,0:T(8,128)S(1)}, f32[128,128]{1,0:T(8,128)S(1)}, u32[]{:S(2)}, u32[]{:S(2)}) collective-permute-start(f32[128,128]{1,0:T(8,128)S(1)} %slice.14), channel_id=1, source_target_pairs={{0,64},{1,65},{2,66},{3,67},{4,68},{5,69},{6,70},{7,71},{8,72},{9,... | collective-permute-start | bytes 196616 | tf_op jit(solution)/shard_map/ppermute | solution.py:76
  41.3 7.9 %collective-permute-start.6 = (f32[512,128]{1,0:T(8,128)S(1)}, f32[512,128]{1,0:T(8,128)S(1)}, u32[]{:S(2)}, u32[]{:S(2)}) collective-permute-start(f32[512,128]{1,0:T(8,128)S(1)} %slice.13), channel_id=1, source_target_pairs={{0,2},{2,0},{9,11},{11,9},{4,13},{13,4},{6,15},{15,6},{3,1},{1,3},... | collective-permute-start | bytes 786440 | tf_op jit(solution)/shard_map/ppermute | solution.py:76
  44.0 5.8 %collective-permute-start.12 = (f32[128,128]{1,0:T(8,128)S(1)}, f32[128,128]{1,0:T(8,128)S(1)}, u32[]{:S(2)}, u32[]{:S(2)}) collective-permute-start(f32[128,128]{1,0:T(8,128)S(1)} %broadcast_select_fusion.3), channel_id=1, source_target_pairs={{0,2},{2,0},{9,11},{11,9},{4,13},{13,4},{6,15},{15,6},{3,1},{1,3},... | collective-permute-start | bytes 196616 | tf_op jit(solution)/shard_map/ppermute | solution.py:76
  49.2 10.5 %collective-permute-start.15 = (f32[2,512,128]{2,1,0:T(8,128)S(1)}, f32[2,512,128]{2,1,0:T(8,128)S(1)}, u32[]{:S(2)}, u32[]{:S(2)}) collective-permute-start(f32[2,512,128]{2,1,0:T(8,128)S(1)} %pad_maximum_fusion.refs_0_), channel_id=1, source_target_pairs={{0,4},{1,5},{2,6},{3,7},{4,8},{5,9},{6,10},{7,11},{8,12},{9,13},{1... | collective-permute-start | bytes 1572872 | tf_op jit(solution)/shard_map/ppermute | solution.py:76
  49.9 9.8 %collective-permute-start.13 = (f32[2,128,128]{2,1,0:T(8,128)S(1)}, f32[2,128,128]{2,1,0:T(8,128)S(1)}, u32[]{:S(2)}, u32[]{:S(2)}) collective-permute-start(f32[2,128,128]{2,1,0:T(8,128)S(1)} %pad_maximum_fusion.1.d_mine), channel_id=1, source_target_pairs={{0,16},{1,17},{2,18},{3,19},{4,20},{5,21},{6,22},{7,23},{8,24},{9,... | collective-permute-start | bytes 393224 | tf_op jit(solution)/shard_map/ppermute | solution.py:76
  50.9 19.8 %collective-permute-start.17 = (f32[2,512,128]{2,1,0:T(8,128)S(1)}, f32[2,512,128]{2,1,0:T(8,128)S(1)}, u32[]{:S(2)}, u32[]{:S(2)}) collective-permute-start(f32[2,512,128]{2,1,0:T(8,128)S(1)} %pad_maximum_fusion.refs_0_), channel_id=1, source_target_pairs={{0,16},{1,17},{2,18},{3,19},{4,20},{5,21},{6,22},{7,23},{8,24},{9,... | collective-permute-start | bytes 1572872 | tf_op jit(solution)/shard_map/ppermute | solution.py:76
  51.5 18.7 %collective-permute-start.7 = (f32[2,512,128]{2,1,0:T(8,128)S(1)}, f32[2,512,128]{2,1,0:T(8,128)S(1)}, u32[]{:S(2)}, u32[]{:S(2)}) collective-permute-start(f32[2,512,128]{2,1,0:T(8,128)S(1)} %pad_maximum_fusion.refs_0_), channel_id=1, source_target_pairs={{0,12},{1,13},{2,14},{3,15},{4,0},{5,1},{6,2},{7,3},{8,4},{9,5},{1... | collective-permute-start | bytes 1572872 | tf_op jit(solution)/shard_map/ppermute | solution.py:76
  54.2 16.0 %collective-permute-start.9 = (f32[2,512,128]{2,1,0:T(8,128)S(1)}, f32[2,512,128]{2,1,0:T(8,128)S(1)}, u32[]{:S(2)}, u32[]{:S(2)}) collective-permute-start(f32[2,512,128]{2,1,0:T(8,128)S(1)} %pad_maximum_fusion.refs_0_), channel_id=1, source_target_pairs={{0,1},{1,2},{2,3},{3,0},{4,5},{5,6},{6,7},{7,4},{8,9},{9,10},{10,1... | collective-permute-start | bytes 1572872 | tf_op jit(solution)/shard_map/ppermute | solution.py:76
  59.7 14.3 %collective-permute-start.16 = (f32[2,512,128]{2,1,0:T(8,128)S(1)}, f32[2,512,128]{2,1,0:T(8,128)S(1)}, u32[]{:S(2)}, u32[]{:S(2)}) collective-permute-start(f32[2,512,128]{2,1,0:T(8,128)S(1)} %collective-permute-done.15.refs_2_), channel_id=1, source_target_pairs={{0,16},{1,17},{2,18},{3,19},{4,20},{5,21},{6,22},{7,23},{8,24},{9,... | collective-permute-start | bytes 1572872 | tf_op jit(solution)/shard_map/ppermute | solution.py:76
  70.2 7.0 %collective-permute-start.10 = (f32[2,512,128]{2,1,0:T(8,128)S(1)}, f32[2,512,128]{2,1,0:T(8,128)S(1)}, u32[]{:S(2)}, u32[]{:S(2)}) collective-permute-start(f32[2,512,128]{2,1,0:T(8,128)S(1)} %collective-permute-done.9.refs_1_), channel_id=1, source_target_pairs={{0,16},{1,17},{2,18},{3,19},{4,20},{5,21},{6,22},{7,23},{8,24},{9,... | collective-permute-start | bytes 1572872 | tf_op jit(solution)/shard_map/ppermute | solution.py:76
  70.2 7.0 %collective-permute-start.8 = (f32[2,512,128]{2,1,0:T(8,128)S(1)}, f32[2,512,128]{2,1,0:T(8,128)S(1)}, u32[]{:S(2)}, u32[]{:S(2)}) collective-permute-start(f32[2,512,128]{2,1,0:T(8,128)S(1)} %collective-permute-done.7.refs_0_), channel_id=1, source_target_pairs={{0,16},{1,17},{2,18},{3,19},{4,20},{5,21},{6,22},{7,23},{8,24},{9,... | collective-permute-start | bytes 1572872 | tf_op jit(solution)/shard_map/ppermute | solution.py:76

commit v9 on v8

--- a/solution.py
+++ b/solution.py
@@ -16,6 +16,7 @@
 WIDTH = 128
 SHARE = 512
 DELTAS = (1, 3, 2, 0)
+LAG = 2
 DPART = 128
 
 
@@ -80,40 +81,52 @@
     return pltpu.with_memory_space_constraint(value, pltpu.VMEM)
 
 
-def payload_kernel(info, front, beside, *refs):
-    outs, sems = refs[:-1], refs[-1]
-
-    def copies(source, half):
-        made = []
-        for at, (delta, out) in enumerate(zip(DELTAS, outs)):
-            begin = pl.multiple_of((info[1] + delta) % 4 * SHARE + half * (ROWS // 2), SHARE)
-            pivots, rows = source.at[half * DPART : (half + 1) * DPART, :], source.at[pl.ds(begin, SHARE), :]
-            made.append(pltpu.make_async_copy(pivots, out.at[0:DPART, :], sems.at[2 * at]))
-            made.append(pltpu.make_async_copy(rows, out.at[DPART:, :], sems.at[2 * at + 1]))
-        return made
-
-    for half, source in enumerate((front, beside)):
-        @pl.when(info[0] == half)
-        def _():
-            for copy in copies(source, half):
-                copy.start()
-
-    for copy in copies(front, 0):
+def payload_copies(info, source, half, outs, sems):
+    made = []
+    for at, (delta, out) in enumerate(zip(DELTAS, outs)):
+        begin = pl.multiple_of((info[1] + delta) % 4 * SHARE + half * (ROWS // 2), SHARE)
+        pivots, rows = source.at[half * DPART : (half + 1) * DPART, :], source.at[pl.ds(begin, SHARE), :]
+        made.append(pltpu.make_async_copy(pivots, out.at[0:DPART, :], sems.at[2 * at]))
+        made.append(pltpu.make_async_copy(rows, out.at[DPART:, :], sems.at[2 * at + 1]))
+    return made
+
+
+def kept_kernel(info, front, *refs):
+    made = payload_copies(info, front, 0, refs[:-1], refs[-1])
+    for copy in made:
+        copy.start()
+    for copy in made:
         copy.wait()
 
 
+def taken_kernel(info, beside, *refs):
+    made = payload_copies(info, beside, 1, refs[len(DELTAS) : -1], refs[-1])
+
+    @pl.when(info[0] == 1)
+    def _():
+        for copy in made:
+            copy.start()
+        for copy in made:
+            copy.wait()
+
+
 def payloads(info, front, beside):
-    hbm = pl.BlockSpec(memory_space=pltpu.HBM)
+    vmem = pl.BlockSpec(memory_space=pltpu.VMEM)
+    smem, hbm = pl.BlockSpec(memory_space=pltpu.SMEM), pl.BlockSpec(memory_space=pltpu.HBM)
+    count = len(DELTAS)
+    options = dict(
+        out_shape=tuple(pltpu.VMEM((DPART + SHARE, WIDTH), jnp.float32) for _ in DELTAS),
+        out_specs=(vmem,) * count,
+        scratch_shapes=[pltpu.SemaphoreType.DMA((2 * count,))],
+        compiler_params=pltpu.CompilerParams(vmem_limit_bytes=4 << 20),
+    )
     front = pltpu.with_memory_space_constraint(front, pltpu.HBM)
-    return pl.pallas_call(
-        payload_kernel,
-        out_shape=tuple(pltpu.VMEM((DPART + SHARE, WIDTH), jnp.float32) for _ in DELTAS),
-        in_specs=[pl.BlockSpec(memory_space=pltpu.SMEM), hbm, pl.BlockSpec(memory_space=pltpu.VMEM)],
-        out_specs=tuple(pl.BlockSpec(memory_space=pltpu.VMEM) for _ in DELTAS),
-        scratch_shapes=[pltpu.SemaphoreType.DMA((2 * len(DELTAS),))],
-        compiler_params=pltpu.CompilerParams(vmem_limit_bytes=4 << 20),
-        name="payloads",
-    )(info, front, in_vmem(beside))
+    kept = pl.pallas_call(kept_kernel, in_specs=[smem, hbm], name="kept", **options)(info, front)
+    aliases = {2 + at: at for at in range(count)}
+    taken = pl.pallas_call(
+        taken_kernel, in_specs=[smem] + [vmem] * (1 + count), input_output_aliases=aliases, name="taken", **options
+    )
+    return taken(info, in_vmem(beside), *map(in_vmem, kept))
 
 
 def split3(value):
@@ -225,7 +238,7 @@
 
 
 def update_kernel(info, front, *refs):
-    out, blocks, top_rows, loads, stores, top_sem = refs[-6:]
+    out, blocks, added, top_rows, loads, stores, top_sem = refs[-7:]
     count = blocks.shape[0]
     parts, update, top = refs[:count], refs[count], refs[count + 1]
     top_load = pltpu.make_async_copy(top, top_rows, top_sem)
@@ -244,27 +257,36 @@
         load(at).start()
         pl.when(has_top[at])(top_load.start)
     twice = jnp.concatenate([update[...], update[...]], axis=0)
-    for at in range(count):
-        for half in range(2):
-            rows = slice(half * P_SIZE, (half + 1) * P_SIZE)
-            panel = jnp.concatenate([parts[at][0, rows, :], parts[at][1, rows, :]], axis=1)
-            high = panel.astype(jnp.bfloat16)
-            low = (panel - high.astype(jnp.float32)).astype(jnp.bfloat16)
-            both = jnp.dot(jnp.concatenate([high, low], axis=1), twice, preferred_element_type=jnp.float32)
-            added = both[:, :WIDTH] + both[:, WIDTH:]
-            if half == 0:
-                load(at).wait()
-            blocks[at, rows, :] = jnp.where(info[0] == 0, blocks[at, rows, :], 0.0) + added
-            if half == 0:
-                @pl.when(has_top[at])
-                def _():
-                    top_load.wait()
-                    blocks[at, 0:P_SIZE, :] = top_rows[...]
-
-            store(at, half).start()
-    for at in range(count):
-        for half in range(2):
-            store(at, half).wait()
+    halves = [(at, half) for at in range(count) for half in range(2)]
+
+    def multiply(at, half):
+        rows = slice(half * P_SIZE, (half + 1) * P_SIZE)
+        panel = jnp.concatenate([parts[at][0, rows, :], parts[at][1, rows, :]], axis=1)
+        high = panel.astype(jnp.bfloat16)
+        low = (panel - high.astype(jnp.float32)).astype(jnp.bfloat16)
+        both = jnp.dot(jnp.concatenate([high, low], axis=1), twice, preferred_element_type=jnp.float32)
+        added[at, rows, :] = both[:, :WIDTH] + both[:, WIDTH:]
+
+    def finish(at, half):
+        rows = slice(half * P_SIZE, (half + 1) * P_SIZE)
+        if half == 0:
+            load(at).wait()
+        blocks[at, rows, :] = jnp.where(info[0] == 0, blocks[at, rows, :], 0.0) + added[at, rows, :]
+        if half == 0:
+            @pl.when(has_top[at])
+            def _():
+                top_load.wait()
+                blocks[at, 0:P_SIZE, :] = top_rows[...]
+
+        store(at, half).start()
+
+    for turn in range(len(halves) + LAG):
+        if turn < len(halves):
+            multiply(*halves[turn])
+        if turn >= LAG:
+            finish(*halves[turn - LAG])
+    for at, half in halves:
+        store(at, half).wait()
 
 
 def apply_update(info, front, parts, update, top, done=None):
@@ -278,6 +300,7 @@
         out_specs=hbm,
         scratch_shapes=[
             pltpu.VMEM((count, SHARE, WIDTH), jnp.float32),
+            pltpu.VMEM((count, SHARE, WIDTH), jnp.float32),
             pltpu.VMEM((P_SIZE, WIDTH), jnp.float32),
             pltpu.SemaphoreType.DMA((count,)),
             pltpu.SemaphoreType.DMA((count, 2)),

time: 81.1 us -> 81.8 us (level)
  waiting for transfers between devices: 36.4 us -> 37.8 us
    ppermute x18, waiting for transfers between devices: 36.4 us -> 37.8 us  [send(): return lax.ppermute(value, AXES, pairs)]
    pallas_call x1 -> x2, Pallas kernels: 1.91 us -> 2.53 us  [the longest x1 1.9 us: payloads(): pl.pallas_call(kept_kernel, in_specs=[smem, hbm], name='kept', **options)]
  transfers between devices with their start and end apart: 18 -> 18, of which waited for: 10 -> 10; matrix products, arithmetic and copies ran while one was open for 3% -> 3% of each run, Pallas kernels for 14% -> 15%
where the time goes in v9:
time: 81.8 us; the launch traced here: 80.8 us
  waiting for transfers between devices  37.8 us (46%)
  starting transfers between devices  24.7 us (30%)
  Pallas kernels  15.6 us (19%)
  other arithmetic  1.4 us (2%)
  local copies, waits for them, and re-layouts  1.11 us (1%)
    ppermute x18, waiting for transfers between devices, send(): return lax.ppermute(value, AXES, pairs)  37.8 us
    ppermute x18, starting transfers between devices, send(): return lax.ppermute(value, AXES, pairs)  24.7 us
    pallas_call x3, Pallas kernels, apply_update(): pl.pallas_call(update_kernel, out_shape=jax.ShapeDtypeStruct((ROWS, WIDTH...  8.75 us
    pallas_call x1, Pallas kernels, factor(): pl.pallas_call(factor_kernel, out_shape=(pltpu.VMEM((P_SIZE, 2 * WIDTH),...  4.35 us
    pallas_call x1, Pallas kernels, payloads(): pl.pallas_call(kept_kernel, in_specs=[smem, hbm], name='kept', **options)  1.9 us
  transfers between devices with their start and end apart: 18, of which 10 were waited for; matrix products, arithmetic and copies ran while one was open for 3% of the time, Pallas kernels for 15%

profile of v9, /device:TPU:0, one launch (start us, length us, event | category | flops | bytes accessed | tf_op | source)
XLA Modules:
  0.0 80.8 jit_solution(10640796188937847963)
XLA Ops:
  0.1 1.9 %kept.1 = (f32[640,128]{1,0:T(8,128)S(1)}, f32[640,128]{1,0:T(8,128)S(1)}, f32[640,128]{1,0:T(8,128)S(1)}, f32[640,128]{1,0:T(8,128)S(1)}) custom-call(s32[2]{0:T(128)S(1)} %pad_add_fusion.1.info, f32[4096,128]{1,0:T(8,128)} %front.7), custom_call_target="tpu_custom_call" | custom-call | tf_op jit(solution)/shard_map/kept/pallas_call | solution.py:124
  2.0 2.4 %collective-permute-done.beside = f32[4096,128]{1,0:T(8,128)S(1)} collective-permute-done((f32[4096,128]{1,0:T(8,128)}, f32[4096,128]{1,0:T(8,128)S(1)}, u32[]{:S(2)}, u32[]{:S(2)}) %collective-permute-start) | collective-permute-done | bytes 2097184 | tf_op jit(solution)/shard_map/ppermute | solution.py:77
  4.4 0.6 taken.1
  5.0 2.1 %collective-permute-start.1 = (f32[640,128]{1,0:T(8,128)S(1)}, f32[640,128]{1,0:T(8,128)S(1)}, u32[]{:S(2)}, u32[]{:S(2)}) collective-permute-start(f32[640,128]{1,0:T(8,128)S(1)} %get-tuple-element.19), channel_id=1, source_target_pairs={{0,4},{1,5},{2,6},{3,7},{4,8},{5,9},{6,10},{7,11},{8,12},{9,13},{1... | collective-permute-start | bytes 983048 | tf_op jit(solution)/shard_map/ppermute | solution.py:77
  7.1 2.2 %collective-permute-start.2 = (f32[640,128]{1,0:T(8,128)S(1)}, f32[640,128]{1,0:T(8,128)S(1)}, u32[]{:S(2)}, u32[]{:S(2)}) collective-permute-start(f32[640,128]{1,0:T(8,128)S(1)} %get-tuple-element.20), channel_id=1, source_target_pairs={{0,12},{1,13},{2,14},{3,15},{4,0},{5,1},{6,2},{7,3},{8,4},{9,5},{1... | collective-permute-start | bytes 983048 | tf_op jit(solution)/shard_map/ppermute | solution.py:77
  9.3 3.0 %collective-permute-start.3 = (f32[640,128]{1,0:T(8,128)S(1)}, f32[640,128]{1,0:T(8,128)S(1)}, u32[]{:S(2)}, u32[]{:S(2)}) collective-permute-start(f32[640,128]{1,0:T(8,128)S(1)} %get-tuple-element.22), channel_id=1, source_target_pairs={{0,3},{1,2},{2,1},{3,0},{4,7},{5,6},{6,5},{7,4},{8,11},{9,10},{10,... | collective-permute-start | bytes 983048 | tf_op jit(solution)/shard_map/ppermute | solution.py:77
  12.3 5.3 %collective-permute-done.1 = f32[640,128]{1,0:T(8,128)S(1)} collective-permute-done((f32[640,128]{1,0:T(8,128)S(1)}, f32[640,128]{1,0:T(8,128)S(1)}, u32[]{:S(2)}, u32[]{:S(2)}) %collective-permute-start.1) | collective-permute-done | bytes 327712 | tf_op jit(solution)/shard_map/ppermute | solution.py:77
  17.7 2.8 %collective-permute-done.3 = f32[640,128]{1,0:T(8,128)S(1)} collective-permute-done((f32[640,128]{1,0:T(8,128)S(1)}, f32[640,128]{1,0:T(8,128)S(1)}, u32[]{:S(2)}, u32[]{:S(2)}) %collective-permute-start.3) | collective-permute-done | bytes 327712 | tf_op jit(solution)/shard_map/ppermute | solution.py:77
  20.5 1.6 %collective-permute-start.4 = (f32[640,128]{1,0:T(8,128)S(1)}, f32[640,128]{1,0:T(8,128)S(1)}, u32[]{:S(2)}, u32[]{:S(2)}) collective-permute-start(f32[640,128]{1,0:T(8,128)S(1)} %select_select_fusion), channel_id=1, source_target_pairs={{0,32},{1,33},{2,34},{3,35},{4,36},{5,37},{6,38},{7,39},{8,40},{9,... | collective-permute-start | bytes 983048 | tf_op jit(solution)/shard_map/ppermute | solution.py:77
  22.1 7.6 %collective-permute-done.4 = f32[640,128]{1,0:T(8,128)S(1)} collective-permute-done((f32[640,128]{1,0:T(8,128)S(1)}, f32[640,128]{1,0:T(8,128)S(1)}, u32[]{:S(2)}, u32[]{:S(2)}) %collective-permute-start.4) | collective-permute-done | bytes 327712 | tf_op jit(solution)/shard_map/ppermute | solution.py:77
  29.8 1.1 %collective-permute-start.5 = (f32[640,128]{1,0:T(8,128)S(1)}, f32[640,128]{1,0:T(8,128)S(1)}, u32[]{:S(2)}, u32[]{:S(2)}) collective-permute-start(f32[640,128]{1,0:T(8,128)S(1)} %broadcast_select_fusion), channel_id=1, source_target_pairs={{0,9},{2,11},{9,0},{11,2},{4,6},{13,15},{6,4},{15,13},{3,10},{1,8}... | collective-permute-start | bytes 983048 | tf_op jit(solution)/shard_map/ppermute | solution.py:77
  30.9 0.9 %slice.12 = f32[256,128]{1,0:T(8,128)S(1)} slice(f32[4096,128]{1,0:T(8,128)} %front.7), slice={[0:256], [0:128]} | slice | bytes 262144 | tf_op jit(solution)/shard_map/slice | solution.py:333
  31.8 3.1 %collective-permute-start.14 = (f32[256,128]{1,0:T(8,128)S(1)}, f32[256,128]{1,0:T(8,128)S(1)}, u32[]{:S(2)}, u32[]{:S(2)}) collective-permute-start(f32[256,128]{1,0:T(8,128)S(1)} %slice.12), channel_id=1, source_target_pairs={{0,64},{1,65},{2,66},{3,67},{4,68},{5,69},{6,70},{7,71},{8,72},{9,... | collective-permute-start | bytes 393224 | tf_op jit(solution)/shard_map/ppermute | solution.py:77
  35.0 5.5 %collective-permute-done.5 = f32[640,128]{1,0:T(8,128)S(1)} collective-permute-done((f32[640,128]{1,0:T(8,128)S(1)}, f32[640,128]{1,0:T(8,128)S(1)}, u32[]{:S(2)}, u32[]{:S(2)}) %collective-permute-start.5) | collective-permute-done | bytes 327712 | tf_op jit(solution)/shard_map/ppermute | solution.py:77
  40.6 3.1 %collective-permute-start.11 = (f32[128,128]{1,0:T(8,128)S(1)}, f32[128,128]{1,0:T(8,128)S(1)}, u32[]{:S(2)}, u32[]{:S(2)}) collective-permute-start(f32[128,128]{1,0:T(8,128)S(1)} %slice.14), channel_id=1, source_target_pairs={{0,64},{1,65},{2,66},{3,67},{4,68},{5,69},{6,70},{7,71},{8,72},{9,... | collective-permute-start | bytes 196616 | tf_op jit(solution)/shard_map/ppermute | solution.py:77
  43.7 1.8 %collective-permute-start.6 = (f32[512,128]{1,0:T(8,128)S(1)}, f32[512,128]{1,0:T(8,128)S(1)}, u32[]{:S(2)}, u32[]{:S(2)}) collective-permute-start(f32[512,128]{1,0:T(8,128)S(1)} %slice.13), channel_id=1, source_target_pairs={{0,2},{2,0},{9,11},{11,9},{4,13},{13,4},{6,15},{15,6},{3,1},{1,3},... | collective-permute-start | bytes 786440 | tf_op jit(solution)/shard_map/ppermute | solution.py:77
  45.7 0.7 collective-permute-done.11
  46.4 1.9 %collective-permute-start.12 = (f32[128,128]{1,0:T(8,128)S(1)}, f32[128,128]{1,0:T(8,128)S(1)}, u32[]{:S(2)}, u32[]{:S(2)}) collective-permute-start(f32[128,128]{1,0:T(8,128)S(1)} %broadcast_select_fusion.3), channel_id=1, source_target_pairs={{0,2},{2,0},{9,11},{11,9},{4,13},{13,4},{6,15},{15,6},{3,1},{1,3},... | collective-permute-start | bytes 196616 | tf_op jit(solution)/shard_map/ppermute | solution.py:77
  48.3 3.3 %collective-permute-done.6 = f32[512,128]{1,0:T(8,128)S(1)} collective-permute-done((f32[512,128]{1,0:T(8,128)S(1)}, f32[512,128]{1,0:T(8,128)S(1)}, u32[]{:S(2)}, u32[]{:S(2)}) %collective-permute-start.6) | collective-permute-done | bytes 262176 | tf_op jit(solution)/shard_map/ppermute | solution.py:77
  51.8 0.5 collective-permute-done.12
  52.3 0.1 collective-permute-start.13
  52.4 0.9 %broadcast_select_fusion.2.top = f32[256,128]{1,0:T(8,128)S(1)} fusion(f32[256,128]{1,0:T(8,128)S(1)} %collective-permute-done.14, pred[]{:T(512)S(6)} %eq.62, f32[4096,128]{1,0:T(8,128)} %front.7), kind=kLoop, calls=%fused_computation.9 | loop fusion | flops 32768 | bytes 393217 | tf_op jit(solution)/shard_map/jit(_where)/select_n | solution.py:333
  53.4 0.6 collective-permute-start.17
  53.9 2.7 %collective-permute-start.7 = (f32[2,512,128]{2,1,0:T(8,128)S(1)}, f32[2,512,128]{2,1,0:T(8,128)S(1)}, u32[]{:S(2)}, u32[]{:S(2)}) collective-permute-start(f32[2,512,128]{2,1,0:T(8,128)S(1)} %pad_maximum_fusion.refs_0_), channel_id=1, source_target_pairs={{0,12},{1,13},{2,14},{3,15},{4,0},{5,1},{6,2},{7,3},{8,4},{9,5},{1... | collective-permute-start | bytes 1572872 | tf_op jit(solution)/shard_map/ppermute | solution.py:77
  56.6 0.9 %collective-permute-start.9 = (f32[2,512,128]{2,1,0:T(8,128)S(1)}, f32[2,512,128]{2,1,0:T(8,128)S(1)}, u32[]{:S(2)}, u32[]{:S(2)}) collective-permute-start(f32[2,512,128]{2,1,0:T(8,128)S(1)} %pad_maximum_fusion.refs_0_), channel_id=1, source_target_pairs={{0,1},{1,2},{2,3},{3,0},{4,5},{5,6},{6,7},{7,4},{8,9},{9,10},{10,1... | collective-permute-start | bytes 1572872 | tf_op jit(solution)/shard_map/ppermute | solution.py:77
  57.5 5.6 %collective-permute-done.15.refs_2_ = f32[2,512,128]{2,1,0:T(8,128)S(1)} collective-permute-done((f32[2,512,128]{2,1,0:T(8,128)S(1)}, f32[2,512,128]{2,1,0:T(8,128)S(1)}, u32[]{:S(2)}, u32[]{:S(2)}) %collective-permute-start.15) | collective-permute-done | bytes 524320 | tf_op jit(solution)/shard_map/ppermute | solution.py:77
  63.1 4.3 %factor.1 = (bf16[256,256]{1,0:T(8,128)(2,1)S(1)}, f32[256,128]{1,0:T(8,128)}) custom-call(s32[4]{0:T(128)S(1)} %pad_add_fusion.2.info, f32[2,128,128]{2,1,0:T(8,128)S(1)} %pad_maximum_fusion.1.d_mine, f32[2,128,128]{2,1,0:T(8,128)S(1)} %collective-permute-done.13.d_other, f32[256,128]{1,0:T(8,128)S(1)} %broadcast_select_fusion.2.top), custom_call_target="tpu_custom_call" | custom-call | flops 8999999488 | bytes 2000000 | tf_op jit(solution)/shard_map/factor/pallas_call | solution.py:228
  67.5 4.0 %collective-permute-done.9.refs_1_ = f32[2,512,128]{2,1,0:T(8,128)S(1)} collective-permute-done((f32[2,512,128]{2,1,0:T(8,128)S(1)}, f32[2,512,128]{2,1,0:T(8,128)S(1)}, u32[]{:S(2)}, u32[]{:S(2)}) %collective-permute-start.9) | collective-permute-done | bytes 524320 | tf_op jit(solution)/shard_map/ppermute | solution.py:77
  71.5 0.5 collective-permute-start.8
  72.0 3.0 %shard_map.17.refs_5_ = f32[4096,128]{1,0:T(8,128)} custom-call(s32[5]{0:T(128)S(1)} %stack.106.info, f32[4096,128]{1,0:T(8,128)} %front.7, f32[2,512,128]{2,1,0:T(8,128)S(1)} %pad_maximum_fusion.refs_0_, f32[2,512,128]{2,1,0:T(8,128)S(1)} %collective-permute-done.17.refs_1_, f32[2,512,128]{2,1,0:T(8,128)S(1)} %collective-permute-done.15.refs_2_, ...), custom_call_target="tpu_custom_call" | custom-call | flops 3000000000 | bytes 4000000 | tf_op jit(solution)/shard_map/pallas_call | solution.py:296
  75.0 3.0 %shard_map.18.refs_4_ = f32[4096,128]{1,0:T(8,128)} custom-call(s32[5]{0:T(128)S(1)} %stack.102.info, f32[4096,128]{1,0:T(8,128)} %front.7, f32[2,512,128]{2,1,0:T(8,128)S(1)} %collective-permute-done.7.refs_0_, f32[2,512,128]{2,1,0:T(8,128)S(1)} %collective-permute-done.9.refs_1_, ...), custom_call_target="tpu_custom_call", output_to_operand_aliasing={{}: (7, {})} | custom-call | flops 3000000000 | bytes 4000000 | tf_op jit(solution)/shard_map/pallas_call | solution.py:296
  78.0 2.8 %shard_map.19 = f32[4096,128]{1,0:T(8,128)} custom-call(s32[4]{0:T(128)S(1)} %pad_add_fusion.info, f32[4096,128]{1,0:T(8,128)} %front.7, f32[2,512,128]{2,1,0:T(8,128)S(1)} %collective-permute-done.8.refs_0_, f32[2,512,128]{2,1,0:T(8,128)S(1)} %collective-permute-done.10.refs_1_, ...), custom_call_target="tpu_custom_call", output_to_operand_aliasing={{}: (6, {})} | custom-call | flops 3000000000 | bytes 4000000 | tf_op jit(solution)/shard_map/pallas_call | solution.py:296
  (27 shorter events, 0.8 us)
Async XLA Ops:
  0.0 4.4 %collective-permute-start = (f32[4096,128]{1,0:T(8,128)}, f32[4096,128]{1,0:T(8,128)S(1)}, u32[]{:S(2)}, u32[]{:S(2)}) collective-permute-start(f32[4096,128]{1,0:T(8,128)} %front.7), channel_id=1, source_target_pairs={{0,16},{1,17},{2,18},{3,19},{4,20},{5,21},{6,22},{7,23},{8,24},{9,... | collective-permute-start | bytes 6291464 | tf_op jit(solution)/shard_map/ppermute | solution.py:77
  5.0 12.7 %collective-permute-start.1 = (f32[640,128]{1,0:T(8,128)S(1)}, f32[640,128]{1,0:T(8,128)S(1)}, u32[]{:S(2)}, u32[]{:S(2)}) collective-permute-start(f32[640,128]{1,0:T(8,128)S(1)} %get-tuple-element.19), channel_id=1, source_target_pairs={{0,4},{1,5},{2,6},{3,7},{4,8},{5,9},{6,10},{7,11},{8,12},{9,13},{1... | collective-permute-start | bytes 983048 | tf_op jit(solution)/shard_map/ppermute | solution.py:77
  7.1 10.6 %collective-permute-start.2 = (f32[640,128]{1,0:T(8,128)S(1)}, f32[640,128]{1,0:T(8,128)S(1)}, u32[]{:S(2)}, u32[]{:S(2)}) collective-permute-start(f32[640,128]{1,0:T(8,128)S(1)} %get-tuple-element.20), channel_id=1, source_target_pairs={{0,12},{1,13},{2,14},{3,15},{4,0},{5,1},{6,2},{7,3},{8,4},{9,5},{1... | collective-permute-start | bytes 983048 | tf_op jit(solution)/shard_map/ppermute | solution.py:77
  9.3 11.2 %collective-permute-start.3 = (f32[640,128]{1,0:T(8,128)S(1)}, f32[640,128]{1,0:T(8,128)S(1)}, u32[]{:S(2)}, u32[]{:S(2)}) collective-permute-start(f32[640,128]{1,0:T(8,128)S(1)} %get-tuple-element.22), channel_id=1, source_target_pairs={{0,3},{1,2},{2,1},{3,0},{4,7},{5,6},{6,5},{7,4},{8,11},{9,10},{10,... | collective-permute-start | bytes 983048 | tf_op jit(solution)/shard_map/ppermute | solution.py:77
  20.5 9.2 %collective-permute-start.4 = (f32[640,128]{1,0:T(8,128)S(1)}, f32[640,128]{1,0:T(8,128)S(1)}, u32[]{:S(2)}, u32[]{:S(2)}) collective-permute-start(f32[640,128]{1,0:T(8,128)S(1)} %select_select_fusion), channel_id=1, source_target_pairs={{0,32},{1,33},{2,34},{3,35},{4,36},{5,37},{6,38},{7,39},{8,40},{9,... | collective-permute-start | bytes 983048 | tf_op jit(solution)/shard_map/ppermute | solution.py:77
  29.8 10.7 %collective-permute-start.5 = (f32[640,128]{1,0:T(8,128)S(1)}, f32[640,128]{1,0:T(8,128)S(1)}, u32[]{:S(2)}, u32[]{:S(2)}) collective-permute-start(f32[640,128]{1,0:T(8,128)S(1)} %broadcast_select_fusion), channel_id=1, source_target_pairs={{0,9},{2,11},{9,0},{11,2},{4,6},{13,15},{6,4},{15,13},{3,10},{1,8}... | collective-permute-start | bytes 983048 | tf_op jit(solution)/shard_map/ppermute | solution.py:77
  31.8 20.6 %collective-permute-start.14 = (f32[256,128]{1,0:T(8,128)S(1)}, f32[256,128]{1,0:T(8,128)S(1)}, u32[]{:S(2)}, u32[]{:S(2)}) collective-permute-start(f32[256,128]{1,0:T(8,128)S(1)} %slice.12), channel_id=1, source_target_pairs={{0,64},{1,65},{2,66},{3,67},{4,68},{5,69},{6,70},{7,71},{8,72},{9,... | collective-permute-start | bytes 393224 | tf_op jit(solution)/shard_map/ppermute | solution.py:77
  40.6 5.8 %collective-permute-start.11 = (f32[128,128]{1,0:T(8,128)S(1)}, f32[128,128]{1,0:T(8,128)S(1)}, u32[]{:S(2)}, u32[]{:S(2)}) collective-permute-start(f32[128,128]{1,0:T(8,128)S(1)} %slice.14), channel_id=1, source_target_pairs={{0,64},{1,65},{2,66},{3,67},{4,68},{5,69},{6,70},{7,71},{8,72},{9,... | collective-permute-start | bytes 196616 | tf_op jit(solution)/shard_map/ppermute | solution.py:77
  43.7 7.9 %collective-permute-start.6 = (f32[512,128]{1,0:T(8,128)S(1)}, f32[512,128]{1,0:T(8,128)S(1)}, u32[]{:S(2)}, u32[]{:S(2)}) collective-permute-start(f32[512,128]{1,0:T(8,128)S(1)} %slice.13), channel_id=1, source_target_pairs={{0,2},{2,0},{9,11},{11,9},{4,13},{13,4},{6,15},{15,6},{3,1},{1,3},... | collective-permute-start | bytes 786440 | tf_op jit(solution)/shard_map/ppermute | solution.py:77
  46.4 5.9 %collective-permute-start.12 = (f32[128,128]{1,0:T(8,128)S(1)}, f32[128,128]{1,0:T(8,128)S(1)}, u32[]{:S(2)}, u32[]{:S(2)}) collective-permute-start(f32[128,128]{1,0:T(8,128)S(1)} %broadcast_select_fusion.3), channel_id=1, source_target_pairs={{0,2},{2,0},{9,11},{11,9},{4,13},{13,4},{6,15},{15,6},{3,1},{1,3},... | collective-permute-start | bytes 196616 | tf_op jit(solution)/shard_map/ppermute | solution.py:77
  51.7 11.4 %collective-permute-start.15 = (f32[2,512,128]{2,1,0:T(8,128)S(1)}, f32[2,512,128]{2,1,0:T(8,128)S(1)}, u32[]{:S(2)}, u32[]{:S(2)}) collective-permute-start(f32[2,512,128]{2,1,0:T(8,128)S(1)} %pad_maximum_fusion.refs_0_), channel_id=1, source_target_pairs={{0,4},{1,5},{2,6},{3,7},{4,8},{5,9},{6,10},{7,11},{8,12},{9,13},{1... | collective-permute-start | bytes 1572872 | tf_op jit(solution)/shard_map/ppermute | solution.py:77
  52.3 10.8 %collective-permute-start.13 = (f32[2,128,128]{2,1,0:T(8,128)S(1)}, f32[2,128,128]{2,1,0:T(8,128)S(1)}, u32[]{:S(2)}, u32[]{:S(2)}) collective-permute-start(f32[2,128,128]{2,1,0:T(8,128)S(1)} %pad_maximum_fusion.1.d_mine), channel_id=1, source_target_pairs={{0,16},{1,17},{2,18},{3,19},{4,20},{5,21},{6,22},{7,23},{8,24},{9,... | collective-permute-start | bytes 393224 | tf_op jit(solution)/shard_map/ppermute | solution.py:77
  53.4 18.6 %collective-permute-start.17 = (f32[2,512,128]{2,1,0:T(8,128)S(1)}, f32[2,512,128]{2,1,0:T(8,128)S(1)}, u32[]{:S(2)}, u32[]{:S(2)}) collective-permute-start(f32[2,512,128]{2,1,0:T(8,128)S(1)} %pad_maximum_fusion.refs_0_), channel_id=1, source_target_pairs={{0,16},{1,17},{2,18},{3,19},{4,20},{5,21},{6,22},{7,23},{8,24},{9,... | collective-permute-start | bytes 1572872 | tf_op jit(solution)/shard_map/ppermute | solution.py:77
  53.9 17.5 %collective-permute-start.7 = (f32[2,512,128]{2,1,0:T(8,128)S(1)}, f32[2,512,128]{2,1,0:T(8,128)S(1)}, u32[]{:S(2)}, u32[]{:S(2)}) collective-permute-start(f32[2,512,128]{2,1,0:T(8,128)S(1)} %pad_maximum_fusion.refs_0_), channel_id=1, source_target_pairs={{0,12},{1,13},{2,14},{3,15},{4,0},{5,1},{6,2},{7,3},{8,4},{9,5},{1... | collective-permute-start | bytes 1572872 | tf_op jit(solution)/shard_map/ppermute | solution.py:77
  56.6 14.8 %collective-permute-start.9 = (f32[2,512,128]{2,1,0:T(8,128)S(1)}, f32[2,512,128]{2,1,0:T(8,128)S(1)}, u32[]{:S(2)}, u32[]{:S(2)}) collective-permute-start(f32[2,512,128]{2,1,0:T(8,128)S(1)} %pad_maximum_fusion.refs_0_), channel_id=1, source_target_pairs={{0,1},{1,2},{2,3},{3,0},{4,5},{5,6},{6,7},{7,4},{8,9},{9,10},{10,1... | collective-permute-start | bytes 1572872 | tf_op jit(solution)/shard_map/ppermute | solution.py:77
  63.1 11.9 %collective-permute-start.16 = (f32[2,512,128]{2,1,0:T(8,128)S(1)}, f32[2,512,128]{2,1,0:T(8,128)S(1)}, u32[]{:S(2)}, u32[]{:S(2)}) collective-permute-start(f32[2,512,128]{2,1,0:T(8,128)S(1)} %collective-permute-done.15.refs_2_), channel_id=1, source_target_pairs={{0,16},{1,17},{2,18},{3,19},{4,20},{5,21},{6,22},{7,23},{8,24},{9,... | collective-permute-start | bytes 1572872 | tf_op jit(solution)/shard_map/ppermute | solution.py:77
  71.5 6.5 %collective-permute-start.10 = (f32[2,512,128]{2,1,0:T(8,128)S(1)}, f32[2,512,128]{2,1,0:T(8,128)S(1)}, u32[]{:S(2)}, u32[]{:S(2)}) collective-permute-start(f32[2,512,128]{2,1,0:T(8,128)S(1)} %collective-permute-done.9.refs_1_), channel_id=1, source_target_pairs={{0,16},{1,17},{2,18},{3,19},{4,20},{5,21},{6,22},{7,23},{8,24},{9,... | collective-permute-start | bytes 1572872 | tf_op jit(solution)/shard_map/ppermute | solution.py:77
  71.5 6.5 %collective-permute-start.8 = (f32[2,512,128]{2,1,0:T(8,128)S(1)}, f32[2,512,128]{2,1,0:T(8,128)S(1)}, u32[]{:S(2)}, u32[]{:S(2)}) collective-permute-start(f32[2,512,128]{2,1,0:T(8,128)S(1)} %collective-permute-done.7.refs_0_), channel_id=1, source_target_pairs={{0,16},{1,17},{2,18},{3,19},{4,20},{5,21},{6,22},{7,23},{8,24},{9,... | collective-permute-start | bytes 1572872 | tf_op jit(solution)/shard_map/ppermute | solution.py:77

commit v10 on v8

--- a/solution.py
+++ b/solution.py
@@ -16,6 +16,7 @@
 WIDTH = 128
 SHARE = 512
 DELTAS = (1, 3, 2, 0)
+LAG = 2
 DPART = 128
 
 
@@ -225,7 +226,7 @@
 
 
 def update_kernel(info, front, *refs):
-    out, blocks, top_rows, loads, stores, top_sem = refs[-6:]
+    out, blocks, added, top_rows, loads, stores, top_sem = refs[-7:]
     count = blocks.shape[0]
     parts, update, top = refs[:count], refs[count], refs[count + 1]
     top_load = pltpu.make_async_copy(top, top_rows, top_sem)
@@ -244,27 +245,36 @@
         load(at).start()
         pl.when(has_top[at])(top_load.start)
     twice = jnp.concatenate([update[...], update[...]], axis=0)
-    for at in range(count):
-        for half in range(2):
-            rows = slice(half * P_SIZE, (half + 1) * P_SIZE)
-            panel = jnp.concatenate([parts[at][0, rows, :], parts[at][1, rows, :]], axis=1)
-            high = panel.astype(jnp.bfloat16)
-            low = (panel - high.astype(jnp.float32)).astype(jnp.bfloat16)
-            both = jnp.dot(jnp.concatenate([high, low], axis=1), twice, preferred_element_type=jnp.float32)
-            added = both[:, :WIDTH] + both[:, WIDTH:]
-            if half == 0:
-                load(at).wait()
-            blocks[at, rows, :] = jnp.where(info[0] == 0, blocks[at, rows, :], 0.0) + added
-            if half == 0:
-                @pl.when(has_top[at])
-                def _():
-                    top_load.wait()
-                    blocks[at, 0:P_SIZE, :] = top_rows[...]
-
-            store(at, half).start()
-    for at in range(count):
-        for half in range(2):
-            store(at, half).wait()
+    halves = [(at, half) for at in range(count) for half in range(2)]
+
+    def multiply(at, half):
+        rows = slice(half * P_SIZE, (half + 1) * P_SIZE)
+        panel = jnp.concatenate([parts[at][0, rows, :], parts[at][1, rows, :]], axis=1)
+        high = panel.astype(jnp.bfloat16)
+        low = (panel - high.astype(jnp.float32)).astype(jnp.bfloat16)
+        both = jnp.dot(jnp.concatenate([high, low], axis=1), twice, preferred_element_type=jnp.float32)
+        added[at, rows, :] = both[:, :WIDTH] + both[:, WIDTH:]
+
+    def finish(at, half):
+        rows = slice(half * P_SIZE, (half + 1) * P_SIZE)
+        if half == 0:
+            load(at).wait()
+        blocks[at, rows, :] = jnp.where(info[0] == 0, blocks[at, rows, :], 0.0) + added[at, rows, :]
+        if half == 0:
+            @pl.when(has_top[at])
+            def _():
+                top_load.wait()
+                blocks[at, 0:P_SIZE, :] = top_rows[...]
+
+        store(at, half).start()
+
+    for turn in range(len(halves) + LAG):
+        if turn < len(halves):
+            multiply(*halves[turn])
+        if turn >= LAG:
+            finish(*halves[turn - LAG])
+    for at, half in halves:
+        store(at, half).wait()
 
 
 def apply_update(info, front, parts, update, top, done=None):
@@ -278,6 +288,7 @@
         out_specs=hbm,
         scratch_shapes=[
             pltpu.VMEM((count, SHARE, WIDTH), jnp.float32),
+            pltpu.VMEM((count, SHARE, WIDTH), jnp.float32),
             pltpu.VMEM((P_SIZE, WIDTH), jnp.float32),
             pltpu.SemaphoreType.DMA((count,)),
             pltpu.SemaphoreType.DMA((count, 2)),

time: 81.1 us -> 80.5 us (level)
  transfers between devices with their start and end apart: 18 -> 18, of which waited for: 10 -> 10; matrix products, arithmetic and copies ran while one was open for 3% -> 3% of each run, Pallas kernels for 14% -> 13%
where the time goes in v10:
time: 80.5 us; the launch traced here: 79.5 us
  waiting for transfers between devices  36.4 us (45%)
  starting transfers between devices  25.4 us (32%)
  Pallas kernels  15 us (19%)
  other arithmetic  1.4 us (2%)
  local copies, waits for them, and re-layouts  1.11 us (1%)
    ppermute x18, waiting for transfers between devices, send(): return lax.ppermute(value, AXES, pairs)  36.4 us
    ppermute x18, starting transfers between devices, send(): return lax.ppermute(value, AXES, pairs)  25.4 us
    pallas_call x3, Pallas kernels, apply_update(): pl.pallas_call(update_kernel, out_shape=jax.ShapeDtypeStruct((ROWS, WIDTH...  8.76 us
    pallas_call x1, Pallas kernels, factor(): pl.pallas_call(factor_kernel, out_shape=(pltpu.VMEM((P_SIZE, 2 * WIDTH),...  4.35 us
    pallas_call x1, Pallas kernels, payloads(): pl.pallas_call(payload_kernel, out_shape=tuple((pltpu.VMEM((DPART + SHARE...  1.91 us
  transfers between devices with their start and end apart: 18, of which 10 were waited for; matrix products, arithmetic and copies ran while one was open for 3% of the time, Pallas kernels for 13%

profile of v10, /device:TPU:0, one launch (start us, length us, event | category | flops | bytes accessed | tf_op | source)
XLA Modules:
  0.0 79.5 jit_solution(1876562457503919019)
XLA Ops:
  0.1 4.3 %collective-permute-done.beside = f32[4096,128]{1,0:T(8,128)S(1)} collective-permute-done((f32[4096,128]{1,0:T(8,128)}, f32[4096,128]{1,0:T(8,128)S(1)}, u32[]{:S(2)}, u32[]{:S(2)}) %collective-permute-start) | collective-permute-done | bytes 2097184 | tf_op jit(solution)/shard_map/ppermute | solution.py:77
  4.4 1.9 %payloads.1 = (f32[640,128]{1,0:T(8,128)S(1)}, f32[640,128]{1,0:T(8,128)S(1)}, f32[640,128]{1,0:T(8,128)S(1)}, f32[640,128]{1,0:T(8,128)S(1)}) custom-call(s32[2]{0:T(128)S(1)} %pad_add_fusion.1.info, f32[4096,128]{1,0:T(8,128)} %front.7, f32[4096,128]{1,0:T(8,128)S(1)} %collective-permute-done.beside), custom_call_target="tpu_custom_call" | custom-call | tf_op jit(solution)/shard_map/payloads/pallas_call | solution.py:109
  6.3 2.1 %collective-permute-start.1 = (f32[640,128]{1,0:T(8,128)S(1)}, f32[640,128]{1,0:T(8,128)S(1)}, u32[]{:S(2)}, u32[]{:S(2)}) collective-permute-start(f32[640,128]{1,0:T(8,128)S(1)} %get-tuple-element.11), channel_id=1, source_target_pairs={{0,4},{1,5},{2,6},{3,7},{4,8},{5,9},{6,10},{7,11},{8,12},{9,13},{1... | collective-permute-start | bytes 983048 | tf_op jit(solution)/shard_map/ppermute | solution.py:77
  8.4 2.2 %collective-permute-start.2 = (f32[640,128]{1,0:T(8,128)S(1)}, f32[640,128]{1,0:T(8,128)S(1)}, u32[]{:S(2)}, u32[]{:S(2)}) collective-permute-start(f32[640,128]{1,0:T(8,128)S(1)} %get-tuple-element.12), channel_id=1, source_target_pairs={{0,12},{1,13},{2,14},{3,15},{4,0},{5,1},{6,2},{7,3},{8,4},{9,5},{1... | collective-permute-start | bytes 983048 | tf_op jit(solution)/shard_map/ppermute | solution.py:77
  10.6 3.0 %collective-permute-start.3 = (f32[640,128]{1,0:T(8,128)S(1)}, f32[640,128]{1,0:T(8,128)S(1)}, u32[]{:S(2)}, u32[]{:S(2)}) collective-permute-start(f32[640,128]{1,0:T(8,128)S(1)} %get-tuple-element.14), channel_id=1, source_target_pairs={{0,3},{1,2},{2,1},{3,0},{4,7},{5,6},{6,5},{7,4},{8,11},{9,10},{10,... | collective-permute-start | bytes 983048 | tf_op jit(solution)/shard_map/ppermute | solution.py:77
  13.6 4.1 %collective-permute-done.1 = f32[640,128]{1,0:T(8,128)S(1)} collective-permute-done((f32[640,128]{1,0:T(8,128)S(1)}, f32[640,128]{1,0:T(8,128)S(1)}, u32[]{:S(2)}, u32[]{:S(2)}) %collective-permute-start.1) | collective-permute-done | bytes 327712 | tf_op jit(solution)/shard_map/ppermute | solution.py:77
  17.7 2.8 %collective-permute-done.3 = f32[640,128]{1,0:T(8,128)S(1)} collective-permute-done((f32[640,128]{1,0:T(8,128)S(1)}, f32[640,128]{1,0:T(8,128)S(1)}, u32[]{:S(2)}, u32[]{:S(2)}) %collective-permute-start.3) | collective-permute-done | bytes 327712 | tf_op jit(solution)/shard_map/ppermute | solution.py:77
  20.6 1.6 %collective-permute-start.4 = (f32[640,128]{1,0:T(8,128)S(1)}, f32[640,128]{1,0:T(8,128)S(1)}, u32[]{:S(2)}, u32[]{:S(2)}) collective-permute-start(f32[640,128]{1,0:T(8,128)S(1)} %select_select_fusion), channel_id=1, source_target_pairs={{0,32},{1,33},{2,34},{3,35},{4,36},{5,37},{6,38},{7,39},{8,40},{9,... | collective-permute-start | bytes 983048 | tf_op jit(solution)/shard_map/ppermute | solution.py:77
  22.1 6.3 %collective-permute-done.4 = f32[640,128]{1,0:T(8,128)S(1)} collective-permute-done((f32[640,128]{1,0:T(8,128)S(1)}, f32[640,128]{1,0:T(8,128)S(1)}, u32[]{:S(2)}, u32[]{:S(2)}) %collective-permute-start.4) | collective-permute-done | bytes 327712 | tf_op jit(solution)/shard_map/ppermute | solution.py:77
  28.5 1.1 %collective-permute-start.5 = (f32[640,128]{1,0:T(8,128)S(1)}, f32[640,128]{1,0:T(8,128)S(1)}, u32[]{:S(2)}, u32[]{:S(2)}) collective-permute-start(f32[640,128]{1,0:T(8,128)S(1)} %broadcast_select_fusion), channel_id=1, source_target_pairs={{0,9},{2,11},{9,0},{11,2},{4,6},{13,15},{6,4},{15,13},{3,10},{1,8}... | collective-permute-start | bytes 983048 | tf_op jit(solution)/shard_map/ppermute | solution.py:77
  29.7 0.9 %slice.12 = f32[256,128]{1,0:T(8,128)S(1)} slice(f32[4096,128]{1,0:T(8,128)} %front.7), slice={[0:256], [0:128]} | slice | bytes 262144 | tf_op jit(solution)/shard_map/slice | solution.py:321
  30.6 3.1 %collective-permute-start.14 = (f32[256,128]{1,0:T(8,128)S(1)}, f32[256,128]{1,0:T(8,128)S(1)}, u32[]{:S(2)}, u32[]{:S(2)}) collective-permute-start(f32[256,128]{1,0:T(8,128)S(1)} %slice.12), channel_id=1, source_target_pairs={{0,64},{1,65},{2,66},{3,67},{4,68},{5,69},{6,70},{7,71},{8,72},{9,... | collective-permute-start | bytes 393224 | tf_op jit(solution)/shard_map/ppermute | solution.py:77
  33.8 4.3 %collective-permute-done.5 = f32[640,128]{1,0:T(8,128)S(1)} collective-permute-done((f32[640,128]{1,0:T(8,128)S(1)}, f32[640,128]{1,0:T(8,128)S(1)}, u32[]{:S(2)}, u32[]{:S(2)}) %collective-permute-start.5) | collective-permute-done | bytes 327712 | tf_op jit(solution)/shard_map/ppermute | solution.py:77
  38.2 3.1 %collective-permute-start.11 = (f32[128,128]{1,0:T(8,128)S(1)}, f32[128,128]{1,0:T(8,128)S(1)}, u32[]{:S(2)}, u32[]{:S(2)}) collective-permute-start(f32[128,128]{1,0:T(8,128)S(1)} %slice.14), channel_id=1, source_target_pairs={{0,64},{1,65},{2,66},{3,67},{4,68},{5,69},{6,70},{7,71},{8,72},{9,... | collective-permute-start | bytes 196616 | tf_op jit(solution)/shard_map/ppermute | solution.py:77
  41.3 1.9 %collective-permute-start.6 = (f32[512,128]{1,0:T(8,128)S(1)}, f32[512,128]{1,0:T(8,128)S(1)}, u32[]{:S(2)}, u32[]{:S(2)}) collective-permute-start(f32[512,128]{1,0:T(8,128)S(1)} %slice.13), channel_id=1, source_target_pairs={{0,2},{2,0},{9,11},{11,9},{4,13},{13,4},{6,15},{15,6},{3,1},{1,3},... | collective-permute-start | bytes 786440 | tf_op jit(solution)/shard_map/ppermute | solution.py:77
  43.2 0.1 stack.106.info
  43.4 0.6 collective-permute-done.11
  44.0 1.9 %collective-permute-start.12 = (f32[128,128]{1,0:T(8,128)S(1)}, f32[128,128]{1,0:T(8,128)S(1)}, u32[]{:S(2)}, u32[]{:S(2)}) collective-permute-start(f32[128,128]{1,0:T(8,128)S(1)} %broadcast_select_fusion.3), channel_id=1, source_target_pairs={{0,2},{2,0},{9,11},{11,9},{4,13},{13,4},{6,15},{15,6},{3,1},{1,3},... | collective-permute-start | bytes 196616 | tf_op jit(solution)/shard_map/ppermute | solution.py:77
  46.0 3.2 %collective-permute-done.6 = f32[512,128]{1,0:T(8,128)S(1)} collective-permute-done((f32[512,128]{1,0:T(8,128)S(1)}, f32[512,128]{1,0:T(8,128)S(1)}, u32[]{:S(2)}, u32[]{:S(2)}) %collective-permute-start.6) | collective-permute-done | bytes 262176 | tf_op jit(solution)/shard_map/ppermute | solution.py:77
  49.3 0.6 collective-permute-done.12
  49.9 0.1 collective-permute-start.13
  50.0 0.9 %broadcast_select_fusion.2.top = f32[256,128]{1,0:T(8,128)S(1)} fusion(f32[256,128]{1,0:T(8,128)S(1)} %collective-permute-done.14, pred[]{:T(512)S(6)} %eq.62, f32[4096,128]{1,0:T(8,128)} %front.7), kind=kLoop, calls=%fused_computation.9 | loop fusion | flops 32768 | bytes 393217 | tf_op jit(solution)/shard_map/jit(_where)/select_n | solution.py:321
  50.9 0.6 collective-permute-start.17
  51.5 2.7 %collective-permute-start.7 = (f32[2,512,128]{2,1,0:T(8,128)S(1)}, f32[2,512,128]{2,1,0:T(8,128)S(1)}, u32[]{:S(2)}, u32[]{:S(2)}) collective-permute-start(f32[2,512,128]{2,1,0:T(8,128)S(1)} %pad_maximum_fusion.refs_0_), channel_id=1, source_target_pairs={{0,12},{1,13},{2,14},{3,15},{4,0},{5,1},{6,2},{7,3},{8,4},{9,5},{1... | collective-permute-start | bytes 1572872 | tf_op jit(solution)/shard_map/ppermute | solution.py:77
  54.2 1.4 %collective-permute-start.9 = (f32[2,512,128]{2,1,0:T(8,128)S(1)}, f32[2,512,128]{2,1,0:T(8,128)S(1)}, u32[]{:S(2)}, u32[]{:S(2)}) collective-permute-start(f32[2,512,128]{2,1,0:T(8,128)S(1)} %pad_maximum_fusion.refs_0_), channel_id=1, source_target_pairs={{0,1},{1,2},{2,3},{3,0},{4,5},{5,6},{6,7},{7,4},{8,9},{9,10},{10,1... | collective-permute-start | bytes 1572872 | tf_op jit(solution)/shard_map/ppermute | solution.py:77
  55.6 4.1 %collective-permute-done.15.refs_2_ = f32[2,512,128]{2,1,0:T(8,128)S(1)} collective-permute-done((f32[2,512,128]{2,1,0:T(8,128)S(1)}, f32[2,512,128]{2,1,0:T(8,128)S(1)}, u32[]{:S(2)}, u32[]{:S(2)}) %collective-permute-start.15) | collective-permute-done | bytes 524320 | tf_op jit(solution)/shard_map/ppermute | solution.py:77
  59.7 4.4 %factor.1 = (bf16[256,256]{1,0:T(8,128)(2,1)S(1)}, f32[256,128]{1,0:T(8,128)}) custom-call(s32[4]{0:T(128)S(1)} %pad_add_fusion.2.info, f32[2,128,128]{2,1,0:T(8,128)S(1)} %pad_maximum_fusion.1.d_mine, f32[2,128,128]{2,1,0:T(8,128)S(1)} %collective-permute-done.13.d_other, f32[256,128]{1,0:T(8,128)S(1)} %broadcast_select_fusion.2.top), custom_call_target="tpu_custom_call" | custom-call | flops 8999999488 | bytes 2000000 | tf_op jit(solution)/shard_map/factor/pallas_call | solution.py:216
  64.0 6.1 %collective-permute-done.9.refs_1_ = f32[2,512,128]{2,1,0:T(8,128)S(1)} collective-permute-done((f32[2,512,128]{2,1,0:T(8,128)S(1)}, f32[2,512,128]{2,1,0:T(8,128)S(1)}, u32[]{:S(2)}, u32[]{:S(2)}) %collective-permute-start.9) | collective-permute-done | bytes 524320 | tf_op jit(solution)/shard_map/ppermute | solution.py:77
  70.2 0.5 collective-permute-start.8
  70.7 3.0 %shard_map.17.refs_5_ = f32[4096,128]{1,0:T(8,128)} custom-call(s32[5]{0:T(128)S(1)} %stack.106.info, f32[4096,128]{1,0:T(8,128)} %front.7, f32[2,512,128]{2,1,0:T(8,128)S(1)} %pad_maximum_fusion.refs_0_, f32[2,512,128]{2,1,0:T(8,128)S(1)} %collective-permute-done.17.refs_1_, f32[2,512,128]{2,1,0:T(8,128)S(1)} %collective-permute-done.15.refs_2_, ...), custom_call_target="tpu_custom_call" | custom-call | flops 3000000000 | bytes 4000000 | tf_op jit(solution)/shard_map/pallas_call | solution.py:284
  73.7 3.0 %shard_map.18.refs_4_ = f32[4096,128]{1,0:T(8,128)} custom-call(s32[5]{0:T(128)S(1)} %stack.102.info, f32[4096,128]{1,0:T(8,128)} %front.7, f32[2,512,128]{2,1,0:T(8,128)S(1)} %collective-permute-done.7.refs_0_, f32[2,512,128]{2,1,0:T(8,128)S(1)} %collective-permute-done.9.refs_1_, ...), custom_call_target="tpu_custom_call", output_to_operand_aliasing={{}: (7, {})} | custom-call | flops 3000000000 | bytes 4000000 | tf_op jit(solution)/shard_map/pallas_call | solution.py:284
  76.7 2.8 %shard_map.19 = f32[4096,128]{1,0:T(8,128)} custom-call(s32[4]{0:T(128)S(1)} %pad_add_fusion.info, f32[4096,128]{1,0:T(8,128)} %front.7, f32[2,512,128]{2,1,0:T(8,128)S(1)} %collective-permute-done.8.refs_0_, f32[2,512,128]{2,1,0:T(8,128)S(1)} %collective-permute-done.10.refs_1_, ...), custom_call_target="tpu_custom_call", output_to_operand_aliasing={{}: (6, {})} | custom-call | flops 3000000000 | bytes 4000000 | tf_op jit(solution)/shard_map/pallas_call | solution.py:284
  (26 shorter events, 0.7 us)
Async XLA Ops:
  0.0 4.4 %collective-permute-start = (f32[4096,128]{1,0:T(8,128)}, f32[4096,128]{1,0:T(8,128)S(1)}, u32[]{:S(2)}, u32[]{:S(2)}) collective-permute-start(f32[4096,128]{1,0:T(8,128)} %front.7), channel_id=1, source_target_pairs={{0,16},{1,17},{2,18},{3,19},{4,20},{5,21},{6,22},{7,23},{8,24},{9,... | collective-permute-start | bytes 6291464 | tf_op jit(solution)/shard_map/ppermute | solution.py:77
  6.3 11.4 %collective-permute-start.1 = (f32[640,128]{1,0:T(8,128)S(1)}, f32[640,128]{1,0:T(8,128)S(1)}, u32[]{:S(2)}, u32[]{:S(2)}) collective-permute-start(f32[640,128]{1,0:T(8,128)S(1)} %get-tuple-element.11), channel_id=1, source_target_pairs={{0,4},{1,5},{2,6},{3,7},{4,8},{5,9},{6,10},{7,11},{8,12},{9,13},{1... | collective-permute-start | bytes 983048 | tf_op jit(solution)/shard_map/ppermute | solution.py:77
  8.4 9.3 %collective-permute-start.2 = (f32[640,128]{1,0:T(8,128)S(1)}, f32[640,128]{1,0:T(8,128)S(1)}, u32[]{:S(2)}, u32[]{:S(2)}) collective-permute-start(f32[640,128]{1,0:T(8,128)S(1)} %get-tuple-element.12), channel_id=1, source_target_pairs={{0,12},{1,13},{2,14},{3,15},{4,0},{5,1},{6,2},{7,3},{8,4},{9,5},{1... | collective-permute-start | bytes 983048 | tf_op jit(solution)/shard_map/ppermute | solution.py:77
  10.6 9.9 %collective-permute-start.3 = (f32[640,128]{1,0:T(8,128)S(1)}, f32[640,128]{1,0:T(8,128)S(1)}, u32[]{:S(2)}, u32[]{:S(2)}) collective-permute-start(f32[640,128]{1,0:T(8,128)S(1)} %get-tuple-element.14), channel_id=1, source_target_pairs={{0,3},{1,2},{2,1},{3,0},{4,7},{5,6},{6,5},{7,4},{8,11},{9,10},{10,... | collective-permute-start | bytes 983048 | tf_op jit(solution)/shard_map/ppermute | solution.py:77
  20.6 7.9 %collective-permute-start.4 = (f32[640,128]{1,0:T(8,128)S(1)}, f32[640,128]{1,0:T(8,128)S(1)}, u32[]{:S(2)}, u32[]{:S(2)}) collective-permute-start(f32[640,128]{1,0:T(8,128)S(1)} %select_select_fusion), channel_id=1, source_target_pairs={{0,32},{1,33},{2,34},{3,35},{4,36},{5,37},{6,38},{7,39},{8,40},{9,... | collective-permute-start | bytes 983048 | tf_op jit(solution)/shard_map/ppermute | solution.py:77
  28.5 9.6 %collective-permute-start.5 = (f32[640,128]{1,0:T(8,128)S(1)}, f32[640,128]{1,0:T(8,128)S(1)}, u32[]{:S(2)}, u32[]{:S(2)}) collective-permute-start(f32[640,128]{1,0:T(8,128)S(1)} %broadcast_select_fusion), channel_id=1, source_target_pairs={{0,9},{2,11},{9,0},{11,2},{4,6},{13,15},{6,4},{15,13},{3,10},{1,8}... | collective-permute-start | bytes 983048 | tf_op jit(solution)/shard_map/ppermute | solution.py:77
  30.6 19.4 %collective-permute-start.14 = (f32[256,128]{1,0:T(8,128)S(1)}, f32[256,128]{1,0:T(8,128)S(1)}, u32[]{:S(2)}, u32[]{:S(2)}) collective-permute-start(f32[256,128]{1,0:T(8,128)S(1)} %slice.12), channel_id=1, source_target_pairs={{0,64},{1,65},{2,66},{3,67},{4,68},{5,69},{6,70},{7,71},{8,72},{9,... | collective-permute-start | bytes 393224 | tf_op jit(solution)/shard_map/ppermute | solution.py:77
  38.2 5.8 %collective-permute-start.11 = (f32[128,128]{1,0:T(8,128)S(1)}, f32[128,128]{1,0:T(8,128)S(1)}, u32[]{:S(2)}, u32[]{:S(2)}) collective-permute-start(f32[128,128]{1,0:T(8,128)S(1)} %slice.14), channel_id=1, source_target_pairs={{0,64},{1,65},{2,66},{3,67},{4,68},{5,69},{6,70},{7,71},{8,72},{9,... | collective-permute-start | bytes 196616 | tf_op jit(solution)/shard_map/ppermute | solution.py:77
  41.3 7.9 %collective-permute-start.6 = (f32[512,128]{1,0:T(8,128)S(1)}, f32[512,128]{1,0:T(8,128)S(1)}, u32[]{:S(2)}, u32[]{:S(2)}) collective-permute-start(f32[512,128]{1,0:T(8,128)S(1)} %slice.13), channel_id=1, source_target_pairs={{0,2},{2,0},{9,11},{11,9},{4,13},{13,4},{6,15},{15,6},{3,1},{1,3},... | collective-permute-start | bytes 786440 | tf_op jit(solution)/shard_map/ppermute | solution.py:77
  44.0 5.8 %collective-permute-start.12 = (f32[128,128]{1,0:T(8,128)S(1)}, f32[128,128]{1,0:T(8,128)S(1)}, u32[]{:S(2)}, u32[]{:S(2)}) collective-permute-start(f32[128,128]{1,0:T(8,128)S(1)} %broadcast_select_fusion.3), channel_id=1, source_target_pairs={{0,2},{2,0},{9,11},{11,9},{4,13},{13,4},{6,15},{15,6},{3,1},{1,3},... | collective-permute-start | bytes 196616 | tf_op jit(solution)/shard_map/ppermute | solution.py:77
  49.2 10.5 %collective-permute-start.15 = (f32[2,512,128]{2,1,0:T(8,128)S(1)}, f32[2,512,128]{2,1,0:T(8,128)S(1)}, u32[]{:S(2)}, u32[]{:S(2)}) collective-permute-start(f32[2,512,128]{2,1,0:T(8,128)S(1)} %pad_maximum_fusion.refs_0_), channel_id=1, source_target_pairs={{0,4},{1,5},{2,6},{3,7},{4,8},{5,9},{6,10},{7,11},{8,12},{9,13},{1... | collective-permute-start | bytes 1572872 | tf_op jit(solution)/shard_map/ppermute | solution.py:77
  49.9 9.8 %collective-permute-start.13 = (f32[2,128,128]{2,1,0:T(8,128)S(1)}, f32[2,128,128]{2,1,0:T(8,128)S(1)}, u32[]{:S(2)}, u32[]{:S(2)}) collective-permute-start(f32[2,128,128]{2,1,0:T(8,128)S(1)} %pad_maximum_fusion.1.d_mine), channel_id=1, source_target_pairs={{0,16},{1,17},{2,18},{3,19},{4,20},{5,21},{6,22},{7,23},{8,24},{9,... | collective-permute-start | bytes 393224 | tf_op jit(solution)/shard_map/ppermute | solution.py:77
  50.9 19.8 %collective-permute-start.17 = (f32[2,512,128]{2,1,0:T(8,128)S(1)}, f32[2,512,128]{2,1,0:T(8,128)S(1)}, u32[]{:S(2)}, u32[]{:S(2)}) collective-permute-start(f32[2,512,128]{2,1,0:T(8,128)S(1)} %pad_maximum_fusion.refs_0_), channel_id=1, source_target_pairs={{0,16},{1,17},{2,18},{3,19},{4,20},{5,21},{6,22},{7,23},{8,24},{9,... | collective-permute-start | bytes 1572872 | tf_op jit(solution)/shard_map/ppermute | solution.py:77
  51.5 18.7 %collective-permute-start.7 = (f32[2,512,128]{2,1,0:T(8,128)S(1)}, f32[2,512,128]{2,1,0:T(8,128)S(1)}, u32[]{:S(2)}, u32[]{:S(2)}) collective-permute-start(f32[2,512,128]{2,1,0:T(8,128)S(1)} %pad_maximum_fusion.refs_0_), channel_id=1, source_target_pairs={{0,12},{1,13},{2,14},{3,15},{4,0},{5,1},{6,2},{7,3},{8,4},{9,5},{1... | collective-permute-start | bytes 1572872 | tf_op jit(solution)/shard_map/ppermute | solution.py:77
  54.2 16.0 %collective-permute-start.9 = (f32[2,512,128]{2,1,0:T(8,128)S(1)}, f32[2,512,128]{2,1,0:T(8,128)S(1)}, u32[]{:S(2)}, u32[]{:S(2)}) collective-permute-start(f32[2,512,128]{2,1,0:T(8,128)S(1)} %pad_maximum_fusion.refs_0_), channel_id=1, source_target_pairs={{0,1},{1,2},{2,3},{3,0},{4,5},{5,6},{6,7},{7,4},{8,9},{9,10},{10,1... | collective-permute-start | bytes 1572872 | tf_op jit(solution)/shard_map/ppermute | solution.py:77
  59.7 14.0 %collective-permute-start.16 = (f32[2,512,128]{2,1,0:T(8,128)S(1)}, f32[2,512,128]{2,1,0:T(8,128)S(1)}, u32[]{:S(2)}, u32[]{:S(2)}) collective-permute-start(f32[2,512,128]{2,1,0:T(8,128)S(1)} %collective-permute-done.15.refs_2_), channel_id=1, source_target_pairs={{0,16},{1,17},{2,18},{3,19},{4,20},{5,21},{6,22},{7,23},{8,24},{9,... | collective-permute-start | bytes 1572872 | tf_op jit(solution)/shard_map/ppermute | solution.py:77
  70.2 6.5 %collective-permute-start.10 = (f32[2,512,128]{2,1,0:T(8,128)S(1)}, f32[2,512,128]{2,1,0:T(8,128)S(1)}, u32[]{:S(2)}, u32[]{:S(2)}) collective-permute-start(f32[2,512,128]{2,1,0:T(8,128)S(1)} %collective-permute-done.9.refs_1_), channel_id=1, source_target_pairs={{0,16},{1,17},{2,18},{3,19},{4,20},{5,21},{6,22},{7,23},{8,24},{9,... | collective-permute-start | bytes 1572872 | tf_op jit(solution)/shard_map/ppermute | solution.py:77
  70.2 6.5 %collective-permute-start.8 = (f32[2,512,128]{2,1,0:T(8,128)S(1)}, f32[2,512,128]{2,1,0:T(8,128)S(1)}, u32[]{:S(2)}, u32[]{:S(2)}) collective-permute-start(f32[2,512,128]{2,1,0:T(8,128)S(1)} %collective-permute-done.7.refs_0_), channel_id=1, source_target_pairs={{0,16},{1,17},{2,18},{3,19},{4,20},{5,21},{6,22},{7,23},{8,24},{9,... | collective-permute-start | bytes 1572872 | tf_op jit(solution)/shard_map/ppermute | solution.py:77
